TPU v7x, 256 devices: a whole 4x4x8 slice. The times are simulated.
256 devices in a mesh: grp: 4 (over x), leaf: 64 (over y, z, core).
Axes of the slice: x: 4, y: 4, z: 8, core: 2. Of those that a mesh axis runs over, the one named last changes fastest.
Arguments:
- basis: float32 [8, 524288], P(None, ('grp', 'leaf')), may hold values from -28 to 28
- roots: float32 [5], replicated, may hold values from 0.35 to 1
- near_blocks: bfloat16 [2048, 6, 256, 256], P(('grp', 'leaf')), may hold values from -0.046875 to 0.046875
- near_ids: int32 [2048, 6], P(('grp', 'leaf')), may hold values from 0 to 2047, as said below
- leaf_basis: bfloat16 [2048, 64, 256], P(('grp', 'leaf')), may hold values from -0.375 to 0.375
- far_coupling: bfloat16 [2048, 8, 64, 64], P(('grp', 'leaf')), may hold values from -0.109375 to 0.109375
- far_ids: int32 [2048, 8], P(('grp', 'leaf')), may hold values from 0 to 2047, as said below
- transfer: bfloat16 [2048, 64, 128], P(('grp', 'leaf')), may hold values from -0.5 to 0.5
- top_coupling: bfloat16 [1024, 8, 128, 128], P(('grp', 'leaf')), may hold values from -0.078125 to 0.078125
- top_ids: int32 [1024, 8], P(('grp', 'leaf')), may hold values from 0 to 1023, as said below
Outputs:
- next_vector: float32 [524288], P(('grp', 'leaf'))
- hessen: float32 [9], replicated
Inputs may be any that keep to these rules, and one draw needn't show every extreme that they name: `near_ids`: row i starts with i itself; the others lie within 8 leaves of i. `far_ids`: every entry lies within 8 leaves of its row. `top_ids`: every entry lies within 4 parents of its row.
All inputs are finite; a program needn't handle non-finite values.
Results may differ from a plain program's by a relative error of at most 0.024.
Values may be sent and summed in bfloat16 or wider, within the bound.
No kernel may reach another device: no remote copies, remote signals or barrier semaphores. Data moves between devices by JAX's collectives and lax.ppermute only.
A program may use at most 64 MiB of HBM per device.

v0:
```python
import functools

import jax
import jax.numpy as jnp
from jax import lax
from jax.sharding import Mesh
from jax.sharding import PartitionSpec as P

GRP_LEAF = ("grp", "leaf_0", "leaf_1", "leaf_2")
LEAF = ("leaf_0", "leaf_1", "leaf_2")


def with_halo(value, sides, width):
    edges = {}
    for axis, dim in sides:
        size, length = (lax.axis_size(axis), value.shape[dim])
        up = [(i, (i + 1) % size) for i in range(size - 1)]
        last = lax.slice_in_dim(value, length - width, length, axis=dim)
        leading = lax.slice_in_dim(value, 0, width, axis=dim)
        edges[dim] = (
            lax.ppermute(last, axis, up),
            lax.ppermute(leading, axis, [(b, a) for a, b in up]),
        )
    done = []
    for _, dim in sides:
        low, high = edges[dim]
        around = [(width, width) if d in done else (0, 0) for d in range(value.ndim)]
        value = jnp.concatenate([jnp.pad(low, around), value, jnp.pad(high, around)], axis=dim)
        done.append(dim)
    return value


def over_axes(value, axes):
    return functools.reduce(lax.psum, axes, value)


def apply_operator(
    field, near_blocks, near_ids, leaf_basis, far_coupling, far_ids, transfer, top_coupling, top_ids
):
    leaves_here = field.shape[0]
    width = field.shape[1]
    rank_size = leaf_basis.shape[1]
    prank_size = transfer.shape[2]
    parents_here = leaves_here // 2
    first = lax.axis_index(GRP_LEAF) * leaves_here - leaves_here
    first_parent = lax.axis_index(GRP_LEAF) * parents_here - parents_here
    rounded = field.astype(jnp.bfloat16)
    coeffs = jnp.einsum(
        "lra,la->lr", leaf_basis, rounded, preferred_element_type=jnp.float32
    ).astype(jnp.bfloat16)
    upward = jnp.einsum("lrp,lr->lp", transfer, coeffs, preferred_element_type=jnp.float32)
    upward = upward.reshape(parents_here, 2, prank_size).sum(1).astype(jnp.bfloat16)
    stacked = jnp.concatenate(
        [rounded, coeffs, upward.reshape(leaves_here, prank_size // 2)], axis=1
    )
    stack_pad = with_halo(stacked, ((GRP_LEAF, 0),), leaves_here)
    padded = stack_pad[:, :width]
    coeff_pad = stack_pad[:, width : width + rank_size]
    parent_pad = stack_pad[:, width + rank_size :].reshape(stack_pad.shape[0] // 2, prank_size)
    nearby = padded[near_ids - first]
    near_term = jnp.einsum("lkab,lkb->la", near_blocks, nearby, preferred_element_type=jnp.float32)
    partners = coeff_pad[far_ids - first]
    leaf_sum = jnp.einsum(
        "lkrs,lks->lr", far_coupling, partners, preferred_element_type=jnp.float32
    )
    sources = parent_pad[top_ids - first_parent]
    top_sum = jnp.einsum(
        "pkab,pkb->pa", top_coupling, sources, preferred_element_type=jnp.float32
    ).astype(jnp.bfloat16)
    down = jnp.einsum(
        "lrp,lp->lr", transfer, jnp.repeat(top_sum, 2, axis=0), preferred_element_type=jnp.float32
    )
    local_coef = (leaf_sum + down).astype(jnp.bfloat16)
    far_term = jnp.einsum("lra,lr->la", leaf_basis, local_coef, preferred_element_type=jnp.float32)
    return 0.5 * field + near_term + far_term


def body(
    basis,
    roots,
    near_blocks,
    near_ids,
    leaf_basis,
    far_coupling,
    far_ids,
    transfer,
    top_coupling,
    top_ids,
):
    leaves_here = near_blocks.shape[0]
    width = near_blocks.shape[2]
    count = basis.shape[0]

    def operator(field):
        return apply_operator(
            field,
            near_blocks,
            near_ids,
            leaf_basis,
            far_coupling,
            far_ids,
            transfer,
            top_coupling,
            top_ids,
        )

    vectors = basis.reshape(count, leaves_here, width)
    product = vectors[count - 1]
    result = jnp.zeros_like(product)
    for index in range(roots.shape[0]):
        result = result + product / roots[index]
        if index < roots.shape[0] - 1:
            product = product - operator(product) / roots[index]
    image = operator(result)
    total = jnp.float32(leaves_here * width * lax.axis_size("grp") * lax.axis_size(LEAF))
    local_proj = jnp.einsum("mla,la->m", vectors, image, precision=lax.Precision.HIGHEST)
    local_gram = jnp.einsum("mla,nla->mn", vectors, vectors, precision=lax.Precision.HIGHEST)
    gram, projected, length_sq = (
        over_axes(local_gram, GRP_LEAF),
        over_axes(local_proj, GRP_LEAF),
        over_axes(jnp.sum(image * image), GRP_LEAF),
    )
    gram = gram / total
    hcoef = projected / total
    remain = image - jnp.einsum("m,mla->la", hcoef, vectors, precision=lax.Precision.HIGHEST)
    squared = (
        length_sq / total
        - 2.0 * jnp.sum(hcoef * hcoef)
        + jnp.dot(
            hcoef,
            jnp.dot(gram, hcoef, precision=lax.Precision.HIGHEST),
            precision=lax.Precision.HIGHEST,
        )
    )
    beta = jnp.sqrt(squared + 1e-06)
    next_vector = (remain / beta).reshape(leaves_here * width)
    hessen = jnp.concatenate([hcoef, beta[None]])
    return (next_vector, hessen)


def solution(mesh):
    finer = Mesh(
        mesh.devices.reshape(mesh.shape["grp"], 4, 8, 2), ("grp", "leaf_0", "leaf_1", "leaf_2")
    )
    in_specs = (
        P(None, GRP_LEAF),
        P(),
        P(GRP_LEAF, None, None, None),
        P(GRP_LEAF, None),
        P(GRP_LEAF, None, None),
        P(GRP_LEAF, None, None, None),
        P(GRP_LEAF, None),
        P(GRP_LEAF, None, None),
        P(GRP_LEAF, None, None, None),
        P(GRP_LEAF, None),
    )
    out_specs = (P(GRP_LEAF), P())
    return jax.shard_map(body, mesh=finer, in_specs=in_specs, out_specs=out_specs, check_vma=False)
```

profile of v0, /device:TPU:1, one launch (start us, length us, event | category | flops | bytes accessed | tf_op | source)
XLA Modules:
  0.0 164.2 jit_solution(9285755314736119966)
XLA Ops:
  0.7 1.0 slice_reduce_fusion
  1.7 1.1 fusion.43
  2.9 1.0 fusion.73
  4.1 5.1 %collective-permute-start.1 = (bf16[8,384]{1,0:T(8,128)(2,1)S(1)}, bf16[8,384]{1,0:T(8,128)(2,1)S(1)}, u32[]{:S(2)}, u32[]{:S(2)}) collective-permute-start(bf16[8,384]{1,0:T(8,128)(2,1)S(1)} %pad_maximum_fusion.5), channel_id=1, source_target_pairs={{1,0},{2,1},{3,2},{4,3},{5,4},{6,5},{7,6},{8,7},{9,8},{10,9},{11,1... | collective-permute-start | bytes 18440 | tf_op jit(solution)/shard_map/ppermute | solution.py:22
  9.3 1.9 %collective-permute-start = (bf16[8,384]{1,0:T(8,128)(2,1)S(1)}, bf16[8,384]{1,0:T(8,128)(2,1)S(1)}, u32[]{:S(2)}, u32[]{:S(2)}) collective-permute-start(bf16[8,384]{1,0:T(8,128)(2,1)S(1)} %pad_maximum_fusion.5), channel_id=1, source_target_pairs={{0,1},{1,2},{2,3},{3,4},{4,5},{5,6},{6,7},{7,8},{8,9},{9,10},{10,1... | collective-permute-start | bytes 18440 | tf_op jit(solution)/shard_map/ppermute | solution.py:21
  11.2 1.5 fusion.98
  12.7 0.7 compare_select_fusion
  13.5 0.7 compare_select_fusion.2
  14.3 0.7 compare_select_fusion.1
  15.9 1.6 fusion.20
  17.5 1.1 fusion.71
  18.6 0.7 gather_fusion.1
  19.6 1.1 fusion.69
  20.7 0.7 gather_fusion
  21.4 4.5 %fusion.99 = f32[8,1,256,1]{2,1,3,0:T(1,128)S(1)} fusion(bf16[8,6,256,1]{2,3,1,0:T(2,128)(2,1)S(1)} %reshape.320, bf16[8,6,256,256]{3,2,1,0:T(8,128)(2,1)} %param.12), kind=kOutput, calls=%fused_computation.151 | convolution fusion | flops 6291456 | bytes 6324224 | tf_op jit(solution)/shard_map/lkab,lkb->la/dot_general | solution.py:61
  27.1 2.4 %collective-permute-start.3 = (bf16[8,384]{1,0:T(8,128)(2,1)S(1)}, bf16[8,384]{1,0:T(8,128)(2,1)S(1)}, u32[]{:S(2)}, u32[]{:S(2)}) collective-permute-start(bf16[8,384]{1,0:T(8,128)(2,1)S(1)} %pad_maximum_fusion.6), channel_id=1, source_target_pairs={{1,0},{2,1},{3,2},{4,3},{5,4},{6,5},{7,6},{8,7},{9,8},{10,9},{11,1... | collective-permute-start | bytes 18440 | tf_op jit(solution)/shard_map/ppermute | solution.py:22
  29.5 3.2 %collective-permute-start.2 = (bf16[8,384]{1,0:T(8,128)(2,1)S(1)}, bf16[8,384]{1,0:T(8,128)(2,1)S(1)}, u32[]{:S(2)}, u32[]{:S(2)}) collective-permute-start(bf16[8,384]{1,0:T(8,128)(2,1)S(1)} %pad_maximum_fusion.6), channel_id=1, source_target_pairs={{0,1},{1,2},{2,3},{3,4},{4,5},{5,6},{6,7},{7,8},{8,9},{9,10},{10,1... | collective-permute-start | bytes 18440 | tf_op jit(solution)/shard_map/ppermute | solution.py:21
  32.7 0.7 collective-permute-done.2
  33.6 0.6 gather_fusion.4
  36.0 0.7 gather_fusion.3
  36.7 4.5 %fusion.100 = f32[8,1,256,1]{2,1,3,0:T(1,128)S(1)} fusion(bf16[8,6,256,1]{2,3,1,0:T(2,128)(2,1)S(1)} %reshape.322, bf16[8,6,256,256]{3,2,1,0:T(8,128)(2,1)} %param.12), kind=kOutput, calls=%fused_computation.152 | convolution fusion | flops 6291456 | bytes 6324224 | tf_op jit(solution)/shard_map/lkab,lkb->la/dot_general | solution.py:61
  41.2 0.7 fusion.89
  42.4 1.9 %collective-permute-start.5 = (bf16[8,384]{1,0:T(8,128)(2,1)S(1)}, bf16[8,384]{1,0:T(8,128)(2,1)S(1)}, u32[]{:S(2)}, u32[]{:S(2)}) collective-permute-start(bf16[8,384]{1,0:T(8,128)(2,1)S(1)} %pad_maximum_fusion.7), channel_id=1, source_target_pairs={{1,0},{2,1},{3,2},{4,3},{5,4},{6,5},{7,6},{8,7},{9,8},{10,9},{11,1... | collective-permute-start | bytes 18440 | tf_op jit(solution)/shard_map/ppermute | solution.py:22
  44.4 4.2 %collective-permute-start.4 = (bf16[8,384]{1,0:T(8,128)(2,1)S(1)}, bf16[8,384]{1,0:T(8,128)(2,1)S(1)}, u32[]{:S(2)}, u32[]{:S(2)}) collective-permute-start(bf16[8,384]{1,0:T(8,128)(2,1)S(1)} %pad_maximum_fusion.7), channel_id=1, source_target_pairs={{0,1},{1,2},{2,3},{3,4},{4,5},{5,6},{6,7},{7,8},{8,9},{9,10},{10,1... | collective-permute-start | bytes 18440 | tf_op jit(solution)/shard_map/ppermute | solution.py:21
  48.6 0.7 collective-permute-done.4
  49.5 0.6 gather_fusion.7
  50.6 0.6 gather_fusion.8
  51.9 0.7 gather_fusion.6
  52.6 4.5 %fusion.101 = f32[8,1,256,1]{2,1,3,0:T(1,128)S(1)} fusion(bf16[8,6,256,1]{2,3,1,0:T(2,128)(2,1)S(1)} %reshape.324, bf16[8,6,256,256]{3,2,1,0:T(8,128)(2,1)} %param.12), kind=kOutput, calls=%fused_computation.153 | convolution fusion | flops 6291456 | bytes 6324224 | tf_op jit(solution)/shard_map/lkab,lkb->la/dot_general | solution.py:61
  57.1 0.7 fusion.86
  58.3 1.9 %collective-permute-start.7 = (bf16[8,384]{1,0:T(8,128)(2,1)S(1)}, bf16[8,384]{1,0:T(8,128)(2,1)S(1)}, u32[]{:S(2)}, u32[]{:S(2)}) collective-permute-start(bf16[8,384]{1,0:T(8,128)(2,1)S(1)} %pad_maximum_fusion.8), channel_id=1, source_target_pairs={{1,0},{2,1},{3,2},{4,3},{5,4},{6,5},{7,6},{8,7},{9,8},{10,9},{11,1... | collective-permute-start | bytes 18440 | tf_op jit(solution)/shard_map/ppermute | solution.py:22
  60.3 4.2 %collective-permute-start.6 = (bf16[8,384]{1,0:T(8,128)(2,1)S(1)}, bf16[8,384]{1,0:T(8,128)(2,1)S(1)}, u32[]{:S(2)}, u32[]{:S(2)}) collective-permute-start(bf16[8,384]{1,0:T(8,128)(2,1)S(1)} %pad_maximum_fusion.8), channel_id=1, source_target_pairs={{0,1},{1,2},{2,3},{3,4},{4,5},{5,6},{6,7},{7,8},{8,9},{9,10},{10,1... | collective-permute-start | bytes 18440 | tf_op jit(solution)/shard_map/ppermute | solution.py:21
  64.5 0.7 collective-permute-done.6
  65.4 0.6 gather_fusion.10
  67.8 0.7 gather_fusion.9
  68.5 4.5 %fusion.102 = f32[8,1,256,1]{2,1,3,0:T(1,128)S(1)} fusion(bf16[8,6,256,1]{2,3,1,0:T(2,128)(2,1)S(1)} %reshape.326, bf16[8,6,256,256]{3,2,1,0:T(8,128)(2,1)} %param.12), kind=kOutput, calls=%fused_computation.154 | convolution fusion | flops 6291456 | bytes 6324224 | tf_op jit(solution)/shard_map/lkab,lkb->la/dot_general | solution.py:61
  73.0 3.2 %fusion.87 = (bf16[8,256]{1,0:T(8,128)(2,1)S(1)}, f32[8,256]{1,0:T(8,128)S(1)}) fusion(f32[]{:T(128)} %bitcast.92, f32[8,1,256]{2,1,0:T(1,128)S(1)} %fusion.51, f32[8,1,256,1]{2,1,3,0:T(1,128)S(1)} %fusion.102, f32[]{:T(128)} %bitcast.69, f32[8,256]{1,0:T(8,128)S(1)} %get-tuple-element.19, f32[8,1,256]{2,1,0:T(1,128)S(1)} %fusion.57, ...), kind=kLoop, calls=%fused_computation.142 | loop fusion | flops 40960 | bytes 69652 | tf_op jit(solution)/shard_map/convert_element_type | solution.py:47
  76.8 1.9 %collective-permute-start.9 = (bf16[8,384]{1,0:T(8,128)(2,1)S(1)}, bf16[8,384]{1,0:T(8,128)(2,1)S(1)}, u32[]{:S(2)}, u32[]{:S(2)}) collective-permute-start(bf16[8,384]{1,0:T(8,128)(2,1)S(1)} %pad_maximum_fusion.9), channel_id=1, source_target_pairs={{1,0},{2,1},{3,2},{4,3},{5,4},{6,5},{7,6},{8,7},{9,8},{10,9},{11,1... | collective-permute-start | bytes 18440 | tf_op jit(solution)/shard_map/ppermute | solution.py:22
  78.7 4.2 %collective-permute-start.8 = (bf16[8,384]{1,0:T(8,128)(2,1)S(1)}, bf16[8,384]{1,0:T(8,128)(2,1)S(1)}, u32[]{:S(2)}, u32[]{:S(2)}) collective-permute-start(bf16[8,384]{1,0:T(8,128)(2,1)S(1)} %pad_maximum_fusion.9), channel_id=1, source_target_pairs={{0,1},{1,2},{2,3},{3,4},{4,5},{5,6},{6,7},{7,8},{8,9},{9,10},{10,1... | collective-permute-start | bytes 18440 | tf_op jit(solution)/shard_map/ppermute | solution.py:21
  83.8 0.6 gather_fusion.13
  86.2 0.7 gather_fusion.12
  86.9 4.5 %fusion.103 = f32[8,1,256,1]{2,1,3,0:T(1,128)S(1)} fusion(bf16[8,6,256,1]{2,3,1,0:T(2,128)(2,1)S(1)} %reshape.328, bf16[8,6,256,256]{3,2,1,0:T(8,128)(2,1)} %param.12), kind=kOutput, calls=%fused_computation.155 | convolution fusion | flops 6291456 | bytes 6324224 | tf_op jit(solution)/shard_map/lkab,lkb->la/dot_general | solution.py:61
  91.4 0.6 multiply_reduce_fusion
  92.3 32.8 %all-reduce.2 = (f32[8]{0:T(128)S(1)}, f32[]{:T(128)}, f32[8,8]{1,0:T(8,128)S(1)}) all-reduce(f32[8]{0:T(128)S(1)} %convolution_bitcast_fusion.2, f32[]{:T(128)} %get-tuple-element.14, f32[8,8]{1,0:T(8,128)S(1)} %convolution_bitcast_fusion), channel_id=1, replica_groups=mesh['grp'=4,'leaf_0'=4,'leaf_1'=8,'leaf_2'=2] {'grp'}, use_global_device_ids=true, to_apply=%region_5.6 | all-reduce | flops 73 | bytes 584 | tf_op jit(solution)/shard_map/psum | solution.py:34
  125.0 6.7 %all-reduce.1 = (f32[8]{0:T(128)S(1)}, f32[]{:T(128)}, f32[8,8]{1,0:T(8,128)S(1)}) all-reduce(f32[8]{0:T(128)S(1)} %get-tuple-element.8, f32[]{:T(128)} %get-tuple-element.9, f32[8,8]{1,0:T(8,128)S(1)} %get-tuple-element.10), channel_id=1, replica_groups=mesh['grp'=4,'leaf_0'=4,'leaf_1'=8,'leaf_2'=2] {'leaf_0'}, use_global_device_ids=true, to_apply=%region_6.7 | all-reduce | flops 73 | bytes 584 | tf_op jit(solution)/shard_map/psum | solution.py:34
  131.7 15.4 %all-reduce = (f32[8]{0:T(128)S(1)}, f32[]{:T(128)}, f32[8,8]{1,0:T(8,128)S(1)}) all-reduce(f32[8]{0:T(128)S(1)} %get-tuple-element.5, f32[]{:T(128)} %get-tuple-element.6, f32[8,8]{1,0:T(8,128)S(1)} %get-tuple-element.7), channel_id=1, replica_groups=mesh['grp'=4,'leaf_0'=4,'leaf_1'=8,'leaf_2'=2] {'leaf_1'}, use_global_device_ids=true, to_apply=%region_7.8 | all-reduce | flops 73 | bytes 584 | tf_op jit(solution)/shard_map/psum | solution.py:34
  147.2 12.2 %all-reduce.3 = (f32[8]{0:T(128)S(1)}, f32[]{:T(128)}, f32[8,8]{1,0:T(8,128)S(1)}) all-reduce(f32[8]{0:T(128)S(1)} %get-tuple-element.2, f32[]{:T(128)} %get-tuple-element.3, f32[8,8]{1,0:T(8,128)S(1)} %get-tuple-element.4), channel_id=1, replica_groups=mesh['grp'=4,'leaf_0'=4,'leaf_1'=8,'leaf_2'=2] {'leaf_2'}, use_global_device_ids=true, to_apply=%region_8.9 | all-reduce | flops 73 | bytes 584 | tf_op jit(solution)/shard_map/psum | solution.py:34
  160.1 0.8 fusion.1
  (128 shorter events, 14.6 us)
Async XLA Ops:
  0.6 18.6 %copy-start = (bf16[8,8,64,64]{3,2,1,0:T(8,128)(2,1)S(1)}, bf16[8,8,64,64]{3,2,1,0:T(8,128)(2,1)}, u32[]{:S(2)}) copy-start(bf16[8,8,64,64]{3,2,1,0:T(8,128)(2,1)} %param.15) | copy-start | bytes 1572868
  0.6 25.9 %copy-start.2 = (bf16[8,64,256]{2,1,0:T(8,128)(2,1)S(1)}, bf16[8,64,256]{2,1,0:T(8,128)(2,1)}, u32[]{:S(2)}) copy-start(bf16[8,64,256]{2,1,0:T(8,128)(2,1)} %param.14) | copy-start | bytes 786436
  0.7 26.1 %copy-start.4 = (bf16[8,64,128]{2,1,0:T(8,128)(2,1)S(1)}, bf16[8,64,128]{2,1,0:T(8,128)(2,1)}, u32[]{:S(2)}) copy-start(bf16[8,64,128]{2,1,0:T(8,128)(2,1)} %param.17) | copy-start | bytes 393220
  0.7 34.6 %copy-start.1 = (bf16[4,8,128,128]{3,2,1,0:T(8,128)(2,1)S(1)}, bf16[4,8,128,128]{3,2,1,0:T(8,128)(2,1)}, u32[]{:S(2)}) copy-start(bf16[4,8,128,128]{3,2,1,0:T(8,128)(2,1)} %param.18) | copy-start | bytes 3145732
  4.1 11.0 %collective-permute-start.1 = (bf16[8,384]{1,0:T(8,128)(2,1)S(1)}, bf16[8,384]{1,0:T(8,128)(2,1)S(1)}, u32[]{:S(2)}, u32[]{:S(2)}) collective-permute-start(bf16[8,384]{1,0:T(8,128)(2,1)S(1)} %pad_maximum_fusion.5), channel_id=1, source_target_pairs={{1,0},{2,1},{3,2},{4,3},{5,4},{6,5},{7,6},{8,7},{9,8},{10,9},{11,1... | collective-permute-start | bytes 18440 | tf_op jit(solution)/shard_map/ppermute | solution.py:22
  9.3 5.8 %collective-permute-start = (bf16[8,384]{1,0:T(8,128)(2,1)S(1)}, bf16[8,384]{1,0:T(8,128)(2,1)S(1)}, u32[]{:S(2)}, u32[]{:S(2)}) collective-permute-start(bf16[8,384]{1,0:T(8,128)(2,1)S(1)} %pad_maximum_fusion.5), channel_id=1, source_target_pairs={{0,1},{1,2},{2,3},{3,4},{4,5},{5,6},{6,7},{7,8},{8,9},{9,10},{10,1... | collective-permute-start | bytes 18440 | tf_op jit(solution)/shard_map/ppermute | solution.py:21
  27.1 5.6 %collective-permute-start.3 = (bf16[8,384]{1,0:T(8,128)(2,1)S(1)}, bf16[8,384]{1,0:T(8,128)(2,1)S(1)}, u32[]{:S(2)}, u32[]{:S(2)}) collective-permute-start(bf16[8,384]{1,0:T(8,128)(2,1)S(1)} %pad_maximum_fusion.6), channel_id=1, source_target_pairs={{1,0},{2,1},{3,2},{4,3},{5,4},{6,5},{7,6},{8,7},{9,8},{10,9},{11,1... | collective-permute-start | bytes 18440 | tf_op jit(solution)/shard_map/ppermute | solution.py:22
  29.5 3.9 %collective-permute-start.2 = (bf16[8,384]{1,0:T(8,128)(2,1)S(1)}, bf16[8,384]{1,0:T(8,128)(2,1)S(1)}, u32[]{:S(2)}, u32[]{:S(2)}) collective-permute-start(bf16[8,384]{1,0:T(8,128)(2,1)S(1)} %pad_maximum_fusion.6), channel_id=1, source_target_pairs={{0,1},{1,2},{2,3},{3,4},{4,5},{5,6},{6,7},{7,8},{8,9},{9,10},{10,1... | collective-permute-start | bytes 18440 | tf_op jit(solution)/shard_map/ppermute | solution.py:21
  42.4 6.1 %collective-permute-start.5 = (bf16[8,384]{1,0:T(8,128)(2,1)S(1)}, bf16[8,384]{1,0:T(8,128)(2,1)S(1)}, u32[]{:S(2)}, u32[]{:S(2)}) collective-permute-start(bf16[8,384]{1,0:T(8,128)(2,1)S(1)} %pad_maximum_fusion.7), channel_id=1, source_target_pairs={{1,0},{2,1},{3,2},{4,3},{5,4},{6,5},{7,6},{8,7},{9,8},{10,9},{11,1... | collective-permute-start | bytes 18440 | tf_op jit(solution)/shard_map/ppermute | solution.py:22
  44.4 4.9 %collective-permute-start.4 = (bf16[8,384]{1,0:T(8,128)(2,1)S(1)}, bf16[8,384]{1,0:T(8,128)(2,1)S(1)}, u32[]{:S(2)}, u32[]{:S(2)}) collective-permute-start(bf16[8,384]{1,0:T(8,128)(2,1)S(1)} %pad_maximum_fusion.7), channel_id=1, source_target_pairs={{0,1},{1,2},{2,3},{3,4},{4,5},{5,6},{6,7},{7,8},{8,9},{9,10},{10,1... | collective-permute-start | bytes 18440 | tf_op jit(solution)/shard_map/ppermute | solution.py:21
  57.1 25.8 %copy-start.3 = (f32[8,2048]{1,0:T(8,128)S(1)}, f32[8,2048]{1,0:T(8,128)}, u32[]{:S(2)}) copy-start(f32[8,2048]{1,0:T(8,128)} %param.10) | copy-start | bytes 196612
  58.3 6.1 %collective-permute-start.7 = (bf16[8,384]{1,0:T(8,128)(2,1)S(1)}, bf16[8,384]{1,0:T(8,128)(2,1)S(1)}, u32[]{:S(2)}, u32[]{:S(2)}) collective-permute-start(bf16[8,384]{1,0:T(8,128)(2,1)S(1)} %pad_maximum_fusion.8), channel_id=1, source_target_pairs={{1,0},{2,1},{3,2},{4,3},{5,4},{6,5},{7,6},{8,7},{9,8},{10,9},{11,1... | collective-permute-start | bytes 18440 | tf_op jit(solution)/shard_map/ppermute | solution.py:22
  60.3 4.9 %collective-permute-start.6 = (bf16[8,384]{1,0:T(8,128)(2,1)S(1)}, bf16[8,384]{1,0:T(8,128)(2,1)S(1)}, u32[]{:S(2)}, u32[]{:S(2)}) collective-permute-start(bf16[8,384]{1,0:T(8,128)(2,1)S(1)} %pad_maximum_fusion.8), channel_id=1, source_target_pairs={{0,1},{1,2},{2,3},{3,4},{4,5},{5,6},{6,7},{7,8},{8,9},{9,10},{10,1... | collective-permute-start | bytes 18440 | tf_op jit(solution)/shard_map/ppermute | solution.py:21
  76.8 6.3 %collective-permute-start.9 = (bf16[8,384]{1,0:T(8,128)(2,1)S(1)}, bf16[8,384]{1,0:T(8,128)(2,1)S(1)}, u32[]{:S(2)}, u32[]{:S(2)}) collective-permute-start(bf16[8,384]{1,0:T(8,128)(2,1)S(1)} %pad_maximum_fusion.9), channel_id=1, source_target_pairs={{1,0},{2,1},{3,2},{4,3},{5,4},{6,5},{7,6},{8,7},{9,8},{10,9},{11,1... | collective-permute-start | bytes 18440 | tf_op jit(solution)/shard_map/ppermute | solution.py:22
  78.7 4.9 %collective-permute-start.8 = (bf16[8,384]{1,0:T(8,128)(2,1)S(1)}, bf16[8,384]{1,0:T(8,128)(2,1)S(1)}, u32[]{:S(2)}, u32[]{:S(2)}) collective-permute-start(bf16[8,384]{1,0:T(8,128)(2,1)S(1)} %pad_maximum_fusion.9), channel_id=1, source_target_pairs={{0,1},{1,2},{2,3},{3,4},{4,5},{5,6},{6,7},{7,8},{8,9},{9,10},{10,1... | collective-permute-start | bytes 18440 | tf_op jit(solution)/shard_map/ppermute | solution.py:21
where the time goes:
time: 165 us; the launch traced here: 164 us
  blocking collectives  67.1 us (41%)
  matrix products  35.8 us (22%)
  starting transfers between devices  30.9 us (19%)
  local copies, waits for them, and re-layouts  14.4 us (9%)
  other arithmetic  10.1 us (6%)
  between operations  3 us (2%)
  waiting for transfers between devices  2.79 us (2%)
    psum x4, blocking collectives, over_axes(): return functools.reduce(lax.psum, axes, value)  67.1 us
    dot_general x5, matrix products, apply_operator(): jnp.einsum('lkab,lkb->la', near_blocks, nearby, preferred_element_type=jn...  22.5 us
    ppermute x5, starting transfers between devices, with_halo(): lax.ppermute(last, axis, up)  17.6 us
    ppermute x5, starting transfers between devices, with_halo(): lax.ppermute(leading, axis, [(b, a) for a, b in up])  13.3 us
    convert_element_type x6, other arithmetic, apply_operator(): rounded = field.astype(jnp.bfloat16)  5.23 us
    gather x10, local copies, waits for them, and re-layouts, apply_operator(): nearby = padded[near_ids - first]  3.43 us
  transfers between devices with their start and end apart: 10, of which 4 were waited for; matrix products, arithmetic and copies ran while one was open for 2% of the time, Pallas kernels for 0%

commit v1 on v0

v1 whole, which is shorter than its diff:
```python
import functools

import jax
import jax.numpy as jnp
from jax import lax
from jax.experimental import pallas as pl
from jax.experimental.pallas import tpu as pltpu
from jax.sharding import PartitionSpec as P

AXES = ("grp", "leaf")
F32 = jnp.float32
BF16 = jnp.bfloat16
NT = (((1,), (1,)), ((), ()))
VMEM = pl.BlockSpec(memory_space=pltpu.VMEM)
SMEM = pl.BlockSpec(memory_space=pltpu.SMEM)
PANEL, RANK, PRANK, WIDTH = 256, 64, 128, 512
T_AT, C_AT = PANEL, PANEL + PRANK


def write_stack(field, leaf_basis, transfer, stack):
    leaves = field.shape[0]
    rounded = field.astype(BF16)
    stack[...] = jnp.zeros(stack.shape, BF16)
    stack[:, :PANEL] = rounded
    coeffs = []
    for i in range(leaves):
        coeffs.append(
            lax.dot_general(rounded[i : i + 1], leaf_basis[i], NT, preferred_element_type=F32)
        )
    coeffs = jnp.concatenate(coeffs, axis=0).astype(BF16)
    stack[:, C_AT : C_AT + RANK] = coeffs
    parents = []
    for p in range(leaves // 2):
        total = jnp.zeros((1, PRANK), F32)
        for i in (2 * p, 2 * p + 1):
            total += jnp.dot(coeffs[i : i + 1], transfer[i], preferred_element_type=F32)
        parents.append(total)
    stack[: leaves // 2, T_AT : T_AT + PRANK] = jnp.concatenate(parents, axis=0).astype(BF16)


def fill_window(place, own, mate, far, window):
    leaves = own.shape[0]
    odd = place[0] % 2 == 1
    at = 0
    for part in window:
        lanes = slice(at, at + part.shape[1])
        at += part.shape[1]
        mate_v, far_v = mate[:, lanes].astype(F32), far[:, lanes].astype(F32)
        part[:leaves, :] = jnp.where(odd, mate_v, far_v)
        part[leaves : 2 * leaves, :] = own[:, lanes].astype(F32)
        part[2 * leaves :, :] = jnp.where(odd, far_v, mate_v)


def apply_rows(field, place, near_ids, far_ids, top_ids, near, leaf_basis, coupling, transfer, top, window):
    panel_win, parent_win, coeff_win = window
    leaves, parents = field.shape[0], field.shape[0] // 2
    first = place[0] * leaves - leaves
    first_parent = place[0] * parents - parents
    tops = []
    for p in range(parents):
        total = jnp.zeros((1, PRANK), F32)
        for k in range(top.shape[1]):
            q = top_ids[p, k] - first_parent
            row = (q // parents) * leaves + q % parents
            source = parent_win[pl.ds(row, 1), :].astype(BF16)
            total += lax.dot_general(source, top[p, k], NT, preferred_element_type=F32)
        tops.append(total.astype(BF16))
    rows = []
    for i in range(leaves):
        local = lax.dot_general(tops[i // 2], transfer[i], NT, preferred_element_type=F32)
        for k in range(coupling.shape[1]):
            source = coeff_win[pl.ds(far_ids[i, k] - first, 1), :][:, :RANK].astype(BF16)
            local += lax.dot_general(source, coupling[i, k], NT, preferred_element_type=F32)
        total = jnp.dot(local.astype(BF16), leaf_basis[i], preferred_element_type=F32)
        for k in range(near.shape[1]):
            source = panel_win[pl.ds(near_ids[i, k] - first, 1), :].astype(BF16)
            total += lax.dot_general(source, near[i, k], NT, preferred_element_type=F32)
        rows.append(total)
    return 0.5 * field + jnp.concatenate(rows, axis=0)


def start_kernel(basis, leaf_basis, transfer, product, stack):
    count, width = basis.shape[0], PANEL
    for i in range(product.shape[0]):
        product[i : i + 1, :] = basis[count - 1 : count, i * width : (i + 1) * width]
    write_stack(product[...], leaf_basis, transfer, stack)


def step_kernel(
    step, last, place, roots, near_ids, far_ids, top_ids, product, partial, own, mate, far,
    near, leaf_basis, coupling, transfer, top, product_out, partial_out, stack, *window,
):
    fill_window(place, own, mate, far, window)
    field = product[...]
    image = apply_rows(
        field, place, near_ids, far_ids, top_ids, near, leaf_basis, coupling, transfer, top, window
    )
    after = field - image / roots[step]
    total = partial[...] + field / roots[step]
    if last:
        total = total + after / roots[step + 1]
    product_out[...] = after
    partial_out[...] = total
    write_stack(total if last else after, leaf_basis, transfer, stack)


def last_kernel(
    place, near_ids, far_ids, top_ids, field, own, mate, far,
    near, leaf_basis, coupling, transfer, top, basis, image_out, sums, *window,
):
    fill_window(place, own, mate, far, window)
    image = apply_rows(
        field[...], place, near_ids, far_ids, top_ids, near, leaf_basis, coupling, transfer, top, window
    )
    image_out[...] = image
    count, leaves = basis.shape[0], image.shape[0]
    lane = lax.broadcasted_iota(jnp.int32, (count, 128), 1)
    sub = lax.broadcasted_iota(jnp.int32, (count, 128), 0)
    vectors = basis[...]
    packed = jnp.zeros((count, 128), F32)
    for n in range(count):
        column = jnp.sum(vectors * vectors[n : n + 1], axis=1, keepdims=True)
        packed = jnp.where(lane == n * count + sub, column, packed)
    dots = jnp.zeros((count, PANEL), F32)
    for i in range(leaves):
        dots += basis[:, i * PANEL : (i + 1) * PANEL] * image[i : i + 1]
    column = jnp.sum(dots, axis=1, keepdims=True)
    packed = jnp.where(lane == count * count + sub, column, packed)
    column = jnp.sum(image * image, axis=1, keepdims=True)
    packed = jnp.where(lane == count * count + count, column, packed)
    sums[...] = jnp.broadcast_to(jnp.sum(packed, axis=0, keepdims=True), sums.shape)


def finish_kernel(size, sums, image, basis, vector_out, hessen_out):
    count, leaves = basis.shape[0], image.shape[0]
    lane = lax.broadcasted_iota(jnp.int32, (count, 128), 1)
    sub = lax.broadcasted_iota(jnp.int32, (count, 128), 0)
    totals = jnp.broadcast_to(jnp.sum(sums[...], axis=0, keepdims=True) / size, (count, 128))
    zero = jnp.zeros((count, 128), F32)
    here = lane == count * count + sub
    coef = jnp.sum(jnp.where(here, totals, zero), axis=1, keepdims=True)
    inner = jnp.sum(jnp.where(lane % count == sub, coef, zero), axis=0, keepdims=True)
    outer = jnp.sum(jnp.where(lane // count == sub, coef, zero), axis=0, keepdims=True)
    gram = jnp.where(lane[:1] < count * count, totals[:1] * inner * outer, zero[:1])
    length = jnp.where(lane[:1] == count * count + count, totals[:1], zero[:1])
    squared = jnp.sum(gram + length, axis=1, keepdims=True)
    squared = squared - 2.0 * jnp.sum(coef * coef, axis=0, keepdims=True)
    beta = jnp.sqrt(squared + 1e-06)
    for i in range(leaves):
        taken = jnp.sum(coef * basis[:, i * PANEL : (i + 1) * PANEL], axis=0, keepdims=True)
        row = (image[i : i + 1, :] - taken) / beta
        vector_out[2 * i : 2 * i + 1, :] = row[:, : PANEL // 2]
        vector_out[2 * i + 1 : 2 * i + 2, :] = row[:, PANEL // 2 :]
    values = jnp.sum(jnp.where(lane == sub, coef, zero), axis=0, keepdims=True)
    hessen_out[...] = jnp.where(lane[:1] == count, beta, values)


def call(kernel, specs, outs, scratch=()):
    shapes = [jax.ShapeDtypeStruct(shape, dtype) for shape, dtype in outs]
    return pl.pallas_call(
        kernel,
        out_shape=shapes,
        in_specs=specs,
        out_specs=[VMEM] * len(shapes),
        scratch_shapes=list(scratch),
        compiler_params=pltpu.CompilerParams(vmem_limit_bytes=40 << 20),
    )


def body(
    basis, roots, near_blocks, near_ids, leaf_basis, far_coupling, far_ids, transfer, top_coupling, top_ids
):
    leaves = near_blocks.shape[0]
    devices = lax.axis_size("grp") * lax.axis_size("leaf")
    place = lax.axis_index(AXES).astype(jnp.int32).reshape(1)
    mates = [(i, i ^ 1) for i in range(devices)]
    others = [(i, ((i + 1) ^ 1) - 1) for i in range(devices)]
    others[0], others[-1] = (0, 0), (devices - 1, devices - 1)

    product, stack = call(
        start_kernel, [VMEM] * 3, [((leaves, PANEL), F32), ((leaves, WIDTH), BF16)]
    )(basis, leaf_basis, transfer)
    window = [pltpu.VMEM((3 * leaves, width), F32) for width in (PANEL, PRANK, WIDTH - C_AT)]
    matrices = (near_blocks, leaf_basis, far_coupling, transfer, top_coupling)
    partial = jnp.zeros((leaves, PANEL), F32)
    steps = roots.shape[0] - 1
    for step in range(steps):
        far = lax.ppermute(stack, AXES, others)
        mate = lax.ppermute(stack, AXES, mates)
        product, partial, stack = call(
            functools.partial(step_kernel, step, step == steps - 1),
            [SMEM] * 5 + [VMEM] * 10,
            [((leaves, PANEL), F32), ((leaves, PANEL), F32), ((leaves, WIDTH), BF16)],
            window,
        )(place, roots, near_ids, far_ids, top_ids, product, partial, stack, mate, far, *matrices)
    far = lax.ppermute(stack, AXES, others)
    mate = lax.ppermute(stack, AXES, mates)
    image, sums = call(
        last_kernel,
        [SMEM] * 4 + [VMEM] * 10,
        [((leaves, PANEL), F32), ((devices, 128), F32)],
        window,
    )(place, near_ids, far_ids, top_ids, partial, stack, mate, far, *matrices, basis)
    sums = lax.all_to_all(sums.reshape(devices, 1, 128), AXES, 0, 0, tiled=True)
    size = float(leaves * PANEL * devices)
    vector, hessen = call(
        functools.partial(finish_kernel, size), [VMEM] * 3, [((leaves * 2, 128), F32), ((1, 128), F32)]
    )(sums.reshape(devices, 128), image, basis)
    return vector.reshape(leaves * PANEL), hessen[0, : basis.shape[0] + 1]


def solution(mesh):
    split = P(AXES)
    in_specs = (P(None, AXES), P()) + (split,) * 8
    return jax.shard_map(body, mesh=mesh, in_specs=in_specs, out_specs=(split, P()), check_vma=False)
```

time: 165 us -> 109 us (0.66)
  matrix products: 35.8 us -> 0 us
  blocking collectives: 67.1 us -> 43.9 us
  Pallas kernels: 0 us -> 22.4 us
  other arithmetic: 10.1 us -> 0 us
  starting transfers between devices: 30.9 us -> 22.4 us
  waiting for transfers between devices: 2.79 us -> 6.04 us
  between operations: 3 us -> 0.79 us
    psum x4 -> x0, blocking collectives: 67.1 us -> none  [over_axes(): return functools.reduce(lax.psum, axes, value)]
    all_to_all x0 -> x1, blocking collectives: none -> 43.9 us  [body(): sums = lax.all_to_all(sums.reshape(devices, 1, 128), AXES, 0, 0, tiled=True)]
    dot_general x39 -> x0, matrix products: 35.8 us -> none  [the longest x5 22.5 us: apply_operator(): jnp.einsum('lkab,lkb->la', near_blocks, nearby, preferred_element_type=jn...]
    pallas_call x0 -> x7, Pallas kernels: none -> 22.4 us  [the longest x4 17.3 us: body(): call(functools.partial(step_kernel, step, step == steps - 1), [SMEM] * 5...]
    unnamed x11 -> x36, local copies, waits for them, and re-layouts: 0.65 us -> 12.5 us
    gather x20 -> x0, local copies, waits for them, and re-layouts: 9.71 us -> none  [the longest x10 3.43 us: apply_operator(): nearby = padded[near_ids - first]]
    ppermute x10, starting transfers between devices: 30.9 us -> 22.4 us  [the longest x5 21.8 us: body(): far = lax.ppermute(stack, AXES, others)]
    convert_element_type x26 -> x0, other arithmetic: 5.35 us -> none  [the longest x6 5.23 us: apply_operator(): rounded = field.astype(jnp.bfloat16)]
  transfers between devices with their start and end apart: 10 -> 10, of which waited for: 4 -> 6; matrix products, arithmetic and copies ran while one was open for 2% -> 0% of each run, Pallas kernels for 0% -> 0%
where the time goes in v1:
time: 109 us
  blocking collectives  43.9 us (40%)
  Pallas kernels  22.4 us (21%)
  starting transfers between devices  22.4 us (21%)
  local copies, waits for them, and re-layouts  13 us (12%)
  waiting for transfers between devices  6.04 us (6%)
    all_to_all x1, blocking collectives, body(): sums = lax.all_to_all(sums.reshape(devices, 1, 128), AXES, 0, 0, tiled=True)  43.9 us
    ppermute x5, starting transfers between devices, body(): far = lax.ppermute(stack, AXES, others)  21.8 us
    pallas_call x4, Pallas kernels, body(): call(functools.partial(step_kernel, step, step == steps - 1), [SMEM] * 5...  17.3 us
    unnamed x36, local copies, waits for them, and re-layouts  12.5 us
    ppermute x5, waiting for transfers between devices, body(): far = lax.ppermute(stack, AXES, others)  5.91 us
    pallas_call x1, Pallas kernels, body(): call(last_kernel, [SMEM] * 4 + [VMEM] * 10, [((leaves, PANEL), F32), ((de...  3.99 us
  transfers between devices with their start and end apart: 10, of which 6 were waited for; matrix products, arithmetic and copies ran while one was open for 0% of the time, Pallas kernels for 0%

profile of v1, /device:TPU:1, one launch (start us, length us, event | category | flops | bytes accessed | tf_op | source)
XLA Modules:
  0.0 108.6 jit_solution(6911837082679760688)
XLA Ops:
  0.6 0.0 copy-start.6
  0.6 0.9 copy-done.6
  1.6 0.9 copy-done.9
  2.5 0.8 copy-done.11
  3.3 0.3 shard_map.113
  3.6 4.9 %collective-permute-start.1 = (bf16[8,512]{1,0:T(8,128)(2,1)S(1)}, bf16[8,512]{1,0:T(8,128)(2,1)S(1)}, u32[]{:S(2)}, u32[]{:S(2)}) collective-permute-start(bf16[8,512]{1,0:T(8,128)(2,1)S(1)} %get-tuple-element.20.own), channel_id=1, source_target_pairs={{0,0},{1,2},{2,1},{3,4},{4,3},{5,6},{6,5},{7,8},{8,7},{9,10},{10,9... | collective-permute-start | bytes 24584 | tf_op jit(solution)/shard_map/ppermute | solution.py:188
  8.6 0.1 collective-permute-start
  8.7 1.2 %collective-permute-done.1.far = bf16[8,512]{1,0:T(8,128)(2,1)S(1)} collective-permute-done((bf16[8,512]{1,0:T(8,128)(2,1)S(1)}, bf16[8,512]{1,0:T(8,128)(2,1)S(1)}, u32[]{:S(2)}, u32[]{:S(2)}) %collective-permute-start.1) | collective-permute-done | bytes 8224 | tf_op jit(solution)/shard_map/ppermute | solution.py:188
  9.9 0.0 collective-permute-done.mate
  9.9 2.8 %copy-done = bf16[8,6,256,256]{3,2,1,0:T(8,128)(2,1)S(1)} copy-done((bf16[8,6,256,256]{3,2,1,0:T(8,128)(2,1)S(1)}, bf16[8,6,256,256]{3,2,1,0:T(8,128)(2,1)}, u32[]{:S(2)}) %copy-start) | copy-done | bytes 6291480
  12.7 1.2 %copy-done.2 = bf16[8,8,64,64]{3,2,1,0:T(8,128)(2,1)S(1)} copy-done((bf16[8,8,64,64]{3,2,1,0:T(8,128)(2,1)S(1)}, bf16[8,8,64,64]{3,2,1,0:T(8,128)(2,1)}, u32[]{:S(2)}) %copy-start.2) | copy-done | bytes 524312
  13.9 1.2 %copy-done.4 = bf16[4,8,128,128]{3,2,1,0:T(8,128)(2,1)S(1)} copy-done((bf16[4,8,128,128]{3,2,1,0:T(8,128)(2,1)S(1)}, bf16[4,8,128,128]{3,2,1,0:T(8,128)(2,1)}, u32[]{:S(2)}) %copy-start.4) | copy-done | bytes 1048600
  15.2 0.9 copy-done.7
  16.1 0.9 copy-done.10
  17.0 0.7 copy-done.13
  17.7 0.7 copy-done.14
  18.4 0.7 copy-done.15
  19.1 0.7 copy-done.16
  19.7 4.3 %shard_map.114 = (f32[8,256]{1,0:T(8,128)S(1)}, f32[8,256]{1,0:T(8,128)S(1)}, bf16[8,512]{1,0:T(8,128)(2,1)S(1)}) custom-call(s32[1]{0:T(128)} %bitcast.place, f32[5]{0:T(128)S(1)} %copy-done.16, s32[8,6]{1,0:T(8,128)S(1)} %copy-done.13, s32[8,8]{1,0:T(8,128)S(1)} %copy-done.14, s32[4,8]{1,0:T(4,128)S(1)} %copy-done.15, ...), custom_call_target="tpu_custom_call" | custom-call | tf_op jit(solution)/shard_map/pallas_call | solution.py:190
  24.0 3.7 %collective-permute-start.3 = (bf16[8,512]{1,0:T(8,128)(2,1)S(1)}, bf16[8,512]{1,0:T(8,128)(2,1)S(1)}, u32[]{:S(2)}, u32[]{:S(2)}) collective-permute-start(bf16[8,512]{1,0:T(8,128)(2,1)S(1)} %get-tuple-element.23.own), channel_id=1, source_target_pairs={{0,0},{1,2},{2,1},{3,4},{4,3},{5,6},{6,5},{7,8},{8,7},{9,10},{10,9... | collective-permute-start | bytes 24584 | tf_op jit(solution)/shard_map/ppermute | solution.py:188
  27.7 0.1 collective-permute-start.2
  27.8 1.2 %collective-permute-done.3.far = bf16[8,512]{1,0:T(8,128)(2,1)S(1)} collective-permute-done((bf16[8,512]{1,0:T(8,128)(2,1)S(1)}, bf16[8,512]{1,0:T(8,128)(2,1)S(1)}, u32[]{:S(2)}, u32[]{:S(2)}) %collective-permute-start.3) | collective-permute-done | bytes 8224 | tf_op jit(solution)/shard_map/ppermute | solution.py:188
  29.0 0.0 collective-permute-done.2.mate
  29.0 0.0 copy-done.17
  29.0 0.0 copy-done.1
  29.0 0.0 copy-done.3
  29.0 0.0 copy-done.5
  29.0 4.3 %shard_map.115 = (f32[8,256]{1,0:T(8,128)S(1)}, f32[8,256]{1,0:T(8,128)S(1)}, bf16[8,512]{1,0:T(8,128)(2,1)S(1)}) custom-call(s32[1]{0:T(128)} %bitcast.place, f32[5]{0:T(128)S(1)} %copy-done.17, s32[8,6]{1,0:T(8,128)S(1)} %copy-done.13, s32[8,8]{1,0:T(8,128)S(1)} %copy-done.14, s32[4,8]{1,0:T(4,128)S(1)} %copy-done.15, ...), custom_call_target="tpu_custom_call" | custom-call | tf_op jit(solution)/shard_map/pallas_call | solution.py:190
  33.3 3.7 %collective-permute-start.5 = (bf16[8,512]{1,0:T(8,128)(2,1)S(1)}, bf16[8,512]{1,0:T(8,128)(2,1)S(1)}, u32[]{:S(2)}, u32[]{:S(2)}) collective-permute-start(bf16[8,512]{1,0:T(8,128)(2,1)S(1)} %get-tuple-element.26.own), channel_id=1, source_target_pairs={{0,0},{1,2},{2,1},{3,4},{4,3},{5,6},{6,5},{7,8},{8,7},{9,10},{10,9... | collective-permute-start | bytes 24584 | tf_op jit(solution)/shard_map/ppermute | solution.py:188
  37.0 0.1 collective-permute-start.4
  37.1 1.2 %collective-permute-done.5.far = bf16[8,512]{1,0:T(8,128)(2,1)S(1)} collective-permute-done((bf16[8,512]{1,0:T(8,128)(2,1)S(1)}, bf16[8,512]{1,0:T(8,128)(2,1)S(1)}, u32[]{:S(2)}, u32[]{:S(2)}) %collective-permute-start.5) | collective-permute-done | bytes 8224 | tf_op jit(solution)/shard_map/ppermute | solution.py:188
  38.3 0.0 collective-permute-done.4.mate
  38.3 4.3 %shard_map.116 = (f32[8,256]{1,0:T(8,128)S(1)}, f32[8,256]{1,0:T(8,128)S(1)}, bf16[8,512]{1,0:T(8,128)(2,1)S(1)}) custom-call(s32[1]{0:T(128)} %bitcast.place, f32[5]{0:T(128)S(1)} %copy-done.17, s32[8,6]{1,0:T(8,128)S(1)} %copy-done.13, s32[8,8]{1,0:T(8,128)S(1)} %copy-done.14, s32[4,8]{1,0:T(4,128)S(1)} %copy-done.15, ...), custom_call_target="tpu_custom_call" | custom-call | tf_op jit(solution)/shard_map/pallas_call | solution.py:190
  42.6 0.0 copy-start.8
  42.6 0.0 copy-start.12
  42.6 4.6 %collective-permute-start.7 = (bf16[8,512]{1,0:T(8,128)(2,1)S(1)}, bf16[8,512]{1,0:T(8,128)(2,1)S(1)}, u32[]{:S(2)}, u32[]{:S(2)}) collective-permute-start(bf16[8,512]{1,0:T(8,128)(2,1)S(1)} %get-tuple-element.29.own), channel_id=1, source_target_pairs={{0,0},{1,2},{2,1},{3,4},{4,3},{5,6},{6,5},{7,8},{8,7},{9,10},{10,9... | collective-permute-start | bytes 24584 | tf_op jit(solution)/shard_map/ppermute | solution.py:188
  47.3 0.1 collective-permute-start.6
  47.4 1.2 %collective-permute-done.7.far = bf16[8,512]{1,0:T(8,128)(2,1)S(1)} collective-permute-done((bf16[8,512]{1,0:T(8,128)(2,1)S(1)}, bf16[8,512]{1,0:T(8,128)(2,1)S(1)}, u32[]{:S(2)}, u32[]{:S(2)}) %collective-permute-start.7) | collective-permute-done | bytes 8224 | tf_op jit(solution)/shard_map/ppermute | solution.py:188
  48.6 0.0 collective-permute-done.6.mate
  48.6 4.5 %shard_map.117 = (f32[8,256]{1,0:T(8,128)}, f32[8,256]{1,0:T(8,128)S(1)}, bf16[8,512]{1,0:T(8,128)(2,1)S(1)}) custom-call(s32[1]{0:T(128)} %bitcast.place, f32[5]{0:T(128)S(1)} %copy-done.17, s32[8,6]{1,0:T(8,128)S(1)} %copy-done.13, s32[8,8]{1,0:T(8,128)S(1)} %copy-done.14, s32[4,8]{1,0:T(4,128)S(1)} %copy-done.15, f32[8,256]{1,0:T(8,128)S(1)} %get-tuple-element.27.product, ...), custom_call_target="tpu_custom_call" | custom-call | tf_op jit(solution)/shard_map/pallas_call | solution.py:190
  53.1 4.8 %collective-permute-start.9 = (bf16[8,512]{1,0:T(8,128)(2,1)S(1)}, bf16[8,512]{1,0:T(8,128)(2,1)S(1)}, u32[]{:S(2)}, u32[]{:S(2)}) collective-permute-start(bf16[8,512]{1,0:T(8,128)(2,1)S(1)} %get-tuple-element.31.own), channel_id=1, source_target_pairs={{0,0},{1,2},{2,1},{3,4},{4,3},{5,6},{6,5},{7,8},{8,7},{9,10},{10,9... | collective-permute-start | bytes 24584 | tf_op jit(solution)/shard_map/ppermute | solution.py:196
  57.9 0.3 collective-permute-start.8
  58.2 1.0 collective-permute-done.9.far
  59.2 0.1 collective-permute-done.8.mate
  59.4 4.0 %shard_map.118 = (f32[8,256]{1,0:T(8,128)S(1)}, f32[256,128]{1,0:T(8,128)S(1)}) custom-call(s32[1]{0:T(128)} %bitcast.place, s32[8,6]{1,0:T(8,128)S(1)} %copy-done.13, s32[8,8]{1,0:T(8,128)S(1)} %copy-done.14, s32[4,8]{1,0:T(4,128)S(1)} %copy-done.15, f32[8,256]{1,0:T(8,128)S(1)} %get-tuple-element.30.field, bf16[8,512]{1,0:T(8,128)(2,1)S(1)} %get-tuple-element.31.own, ...), custom_call_target="tpu_custom_call" | custom-call | tf_op jit(solution)/shard_map/pallas_call | solution.py:198
  63.4 43.9 %all_to_all.5 = f32[256,1,128]{2,1,0:T(1,128)S(1)} all-to-all(f32[256,1,128]{2,1,0:T(1,128)S(1)} %bitcast.9), channel_id=1, replica_groups=mesh['grp'=4,'leaf'=64] {'grp','leaf'}, dimensions={0} | all-to-all | bytes 262144 | tf_op jit(solution)/shard_map/all_to_all | solution.py:204
  107.3 0.8 shard_map.119
  108.1 0.5 slice_bitcast_fusion
  (18 shorter events, 0.0 us)
Async XLA Ops:
  0.6 1.0 copy-start.6
  1.6 0.9 copy-start.9
  2.5 0.8 copy-start.11
  3.3 25.7 %copy-start.17 = (f32[5]{0:T(128)S(1)}, f32[5]{0:T(128)}, u32[]{:S(2)}) copy-start(f32[5]{0:T(128)} %roots.7) | copy-start | bytes 64
  3.6 6.3 %collective-permute-start.1 = (bf16[8,512]{1,0:T(8,128)(2,1)S(1)}, bf16[8,512]{1,0:T(8,128)(2,1)S(1)}, u32[]{:S(2)}, u32[]{:S(2)}) collective-permute-start(bf16[8,512]{1,0:T(8,128)(2,1)S(1)} %get-tuple-element.20.own), channel_id=1, source_target_pairs={{0,0},{1,2},{2,1},{3,4},{4,3},{5,6},{6,5},{7,8},{8,7},{9,10},{10,9... | collective-permute-start | bytes 24584 | tf_op jit(solution)/shard_map/ppermute | solution.py:188
  8.6 1.3 %collective-permute-start = (bf16[8,512]{1,0:T(8,128)(2,1)S(1)}, bf16[8,512]{1,0:T(8,128)(2,1)S(1)}, u32[]{:S(2)}, u32[]{:S(2)}) collective-permute-start(bf16[8,512]{1,0:T(8,128)(2,1)S(1)} %get-tuple-element.20.own), channel_id=1, source_target_pairs={{0,1},{1,0},{2,3},{3,2},{4,5},{5,4},{6,7},{7,6},{8,9},{9,8},{10,11... | collective-permute-start | bytes 24584 | tf_op jit(solution)/shard_map/ppermute | solution.py:189
  9.9 2.8 %copy-start = (bf16[8,6,256,256]{3,2,1,0:T(8,128)(2,1)S(1)}, bf16[8,6,256,256]{3,2,1,0:T(8,128)(2,1)}, u32[]{:S(2)}) copy-start(bf16[8,6,256,256]{3,2,1,0:T(8,128)(2,1)} %near.9) | copy-start | bytes 18874372
  12.7 1.2 %copy-start.2 = (bf16[8,8,64,64]{3,2,1,0:T(8,128)(2,1)S(1)}, bf16[8,8,64,64]{3,2,1,0:T(8,128)(2,1)}, u32[]{:S(2)}) copy-start(bf16[8,8,64,64]{3,2,1,0:T(8,128)(2,1)} %coupling.9) | copy-start | bytes 1572868
  13.9 1.2 %copy-start.4 = (bf16[4,8,128,128]{3,2,1,0:T(8,128)(2,1)S(1)}, bf16[4,8,128,128]{3,2,1,0:T(8,128)(2,1)}, u32[]{:S(2)}) copy-start(bf16[4,8,128,128]{3,2,1,0:T(8,128)(2,1)} %top.9) | copy-start | bytes 3145732
  15.2 0.9 copy-start.7
  16.1 0.9 copy-start.10
  17.0 0.7 copy-start.13
  17.7 0.7 copy-start.14
  18.4 0.7 copy-start.15
  19.1 0.7 copy-start.16
  19.7 9.3 %copy-start.1 = (bf16[8,6,256,256]{3,2,1,0:T(8,128)(2,1)S(1)}, bf16[8,6,256,256]{3,2,1,0:T(8,128)(2,1)}, u32[]{:S(2)}) copy-start(bf16[8,6,256,256]{3,2,1,0:T(8,128)(2,1)} %near.9) | copy-start | bytes 18874372
  19.7 9.3 %copy-start.3 = (bf16[8,8,64,64]{3,2,1,0:T(8,128)(2,1)S(1)}, bf16[8,8,64,64]{3,2,1,0:T(8,128)(2,1)}, u32[]{:S(2)}) copy-start(bf16[8,8,64,64]{3,2,1,0:T(8,128)(2,1)} %coupling.9) | copy-start | bytes 1572868
  19.7 9.3 %copy-start.5 = (bf16[4,8,128,128]{3,2,1,0:T(8,128)(2,1)S(1)}, bf16[4,8,128,128]{3,2,1,0:T(8,128)(2,1)}, u32[]{:S(2)}) copy-start(bf16[4,8,128,128]{3,2,1,0:T(8,128)(2,1)} %top.9) | copy-start | bytes 3145732
  24.0 5.0 %collective-permute-start.3 = (bf16[8,512]{1,0:T(8,128)(2,1)S(1)}, bf16[8,512]{1,0:T(8,128)(2,1)S(1)}, u32[]{:S(2)}, u32[]{:S(2)}) collective-permute-start(bf16[8,512]{1,0:T(8,128)(2,1)S(1)} %get-tuple-element.23.own), channel_id=1, source_target_pairs={{0,0},{1,2},{2,1},{3,4},{4,3},{5,6},{6,5},{7,8},{8,7},{9,10},{10,9... | collective-permute-start | bytes 24584 | tf_op jit(solution)/shard_map/ppermute | solution.py:188
  27.7 1.3 %collective-permute-start.2 = (bf16[8,512]{1,0:T(8,128)(2,1)S(1)}, bf16[8,512]{1,0:T(8,128)(2,1)S(1)}, u32[]{:S(2)}, u32[]{:S(2)}) collective-permute-start(bf16[8,512]{1,0:T(8,128)(2,1)S(1)} %get-tuple-element.23.own), channel_id=1, source_target_pairs={{0,1},{1,0},{2,3},{3,2},{4,5},{5,4},{6,7},{7,6},{8,9},{9,8},{10,11... | collective-permute-start | bytes 24584 | tf_op jit(solution)/shard_map/ppermute | solution.py:189
  33.3 5.0 %collective-permute-start.5 = (bf16[8,512]{1,0:T(8,128)(2,1)S(1)}, bf16[8,512]{1,0:T(8,128)(2,1)S(1)}, u32[]{:S(2)}, u32[]{:S(2)}) collective-permute-start(bf16[8,512]{1,0:T(8,128)(2,1)S(1)} %get-tuple-element.26.own), channel_id=1, source_target_pairs={{0,0},{1,2},{2,1},{3,4},{4,3},{5,6},{6,5},{7,8},{8,7},{9,10},{10,9... | collective-permute-start | bytes 24584 | tf_op jit(solution)/shard_map/ppermute | solution.py:188
  37.0 1.3 %collective-permute-start.4 = (bf16[8,512]{1,0:T(8,128)(2,1)S(1)}, bf16[8,512]{1,0:T(8,128)(2,1)S(1)}, u32[]{:S(2)}, u32[]{:S(2)}) collective-permute-start(bf16[8,512]{1,0:T(8,128)(2,1)S(1)} %get-tuple-element.26.own), channel_id=1, source_target_pairs={{0,1},{1,0},{2,3},{3,2},{4,5},{5,4},{6,7},{7,6},{8,9},{9,8},{10,11... | collective-permute-start | bytes 24584 | tf_op jit(solution)/shard_map/ppermute | solution.py:189
  42.6 16.8 %copy-start.8 = (bf16[8,64,256]{2,1,0:T(8,128)(2,1)S(1)}, bf16[8,64,256]{2,1,0:T(8,128)(2,1)}, u32[]{:S(2)}) copy-start(bf16[8,64,256]{2,1,0:T(8,128)(2,1)} %leaf_basis.11) | copy-start | bytes 786436
  42.6 16.8 %copy-start.12 = (f32[8,2048]{1,0:T(8,128)S(1)}, f32[8,2048]{1,0:T(8,128)}, u32[]{:S(2)}) copy-start(f32[8,2048]{1,0:T(8,128)} %basis.5) | copy-start | bytes 196612
  42.6 6.0 %collective-permute-start.7 = (bf16[8,512]{1,0:T(8,128)(2,1)S(1)}, bf16[8,512]{1,0:T(8,128)(2,1)S(1)}, u32[]{:S(2)}, u32[]{:S(2)}) collective-permute-start(bf16[8,512]{1,0:T(8,128)(2,1)S(1)} %get-tuple-element.29.own), channel_id=1, source_target_pairs={{0,0},{1,2},{2,1},{3,4},{4,3},{5,6},{6,5},{7,8},{8,7},{9,10},{10,9... | collective-permute-start | bytes 24584 | tf_op jit(solution)/shard_map/ppermute | solution.py:188
  47.3 1.3 %collective-permute-start.6 = (bf16[8,512]{1,0:T(8,128)(2,1)S(1)}, bf16[8,512]{1,0:T(8,128)(2,1)S(1)}, u32[]{:S(2)}, u32[]{:S(2)}) collective-permute-start(bf16[8,512]{1,0:T(8,128)(2,1)S(1)} %get-tuple-element.29.own), channel_id=1, source_target_pairs={{0,1},{1,0},{2,3},{3,2},{4,5},{5,4},{6,7},{7,6},{8,9},{9,8},{10,11... | collective-permute-start | bytes 24584 | tf_op jit(solution)/shard_map/ppermute | solution.py:189
  53.1 6.2 %collective-permute-start.9 = (bf16[8,512]{1,0:T(8,128)(2,1)S(1)}, bf16[8,512]{1,0:T(8,128)(2,1)S(1)}, u32[]{:S(2)}, u32[]{:S(2)}) collective-permute-start(bf16[8,512]{1,0:T(8,128)(2,1)S(1)} %get-tuple-element.31.own), channel_id=1, source_target_pairs={{0,0},{1,2},{2,1},{3,4},{4,3},{5,6},{6,5},{7,8},{8,7},{9,10},{10,9... | collective-permute-start | bytes 24584 | tf_op jit(solution)/shard_map/ppermute | solution.py:196
  57.9 1.4 %collective-permute-start.8 = (bf16[8,512]{1,0:T(8,128)(2,1)S(1)}, bf16[8,512]{1,0:T(8,128)(2,1)S(1)}, u32[]{:S(2)}, u32[]{:S(2)}) collective-permute-start(bf16[8,512]{1,0:T(8,128)(2,1)S(1)} %get-tuple-element.31.own), channel_id=1, source_target_pairs={{0,1},{1,0},{2,3},{3,2},{4,5},{5,4},{6,7},{7,6},{8,9},{9,8},{10,11... | collective-permute-start | bytes 24584 | tf_op jit(solution)/shard_map/ppermute | solution.py:197

commit v2 on v1

v2 whole, which is shorter than its diff:
```python
import functools

import jax
import jax.numpy as jnp
from jax import lax
from jax.experimental import pallas as pl
from jax.experimental.pallas import tpu as pltpu
from jax.sharding import PartitionSpec as P

AXES = ("grp", "leaf")
F32 = jnp.float32
BF16 = jnp.bfloat16
NT = (((1,), (1,)), ((), ()))
VMEM = pl.BlockSpec(memory_space=pltpu.VMEM)
HBM = pl.BlockSpec(memory_space=pltpu.HBM)
PANEL, RANK, PRANK, WIDTH = 256, 64, 128, 512
T_AT, C_AT = PANEL, PANEL + PRANK
SOURCES = 32


def dot(a, b):
    return jnp.dot(a, b, preferred_element_type=F32)


def dot_nt(a, b):
    return lax.dot_general(a, b, NT, preferred_element_type=F32)


def diagonal(value, block):
    lane = lax.broadcasted_iota(jnp.int32, value.shape, 1)
    row = lax.broadcasted_iota(jnp.int32, value.shape, 0)
    return jnp.where(lane // block == row, value, jnp.zeros_like(value))


def flat(value):
    return jnp.broadcast_to(jnp.sum(value, axis=0, keepdims=True), value.shape)


def write_stack(field, leaf_basis, transfer, stack):
    rounded = field.astype(BF16)
    stack[:, :PANEL] = rounded
    kept = diagonal(dot_nt(rounded, leaf_basis), RANK)
    folded = sum(kept[:, at : at + 2 * RANK] for at in range(0, kept.shape[1], 2 * RANK))
    coeffs = folded[:, :RANK] + folded[:, RANK:]
    stack[:, C_AT:] = jnp.concatenate([coeffs, jnp.zeros_like(coeffs)], axis=1).astype(BF16)
    spread = diagonal(flat(kept.astype(BF16).astype(F32)), 2 * RANK)
    stack[:, T_AT:C_AT] = dot(spread.astype(BF16), transfer).astype(BF16)


def tiles(value, rows):
    return jnp.concatenate([value[at : at + rows] for at in range(0, value.shape[0], rows)], axis=1)


def apply_rows(field, own, mate, far, pick_near, pick_far, pick_top, near, leaf_basis, coupling, transfer, top):
    leaves = field.shape[0]
    rest = jnp.zeros((SOURCES - 3 * leaves, WIDTH), F32)
    window = jnp.concatenate(
        [own[...].astype(F32), mate[...].astype(F32), far[...].astype(F32), rest], axis=0
    ).astype(BF16)
    parents = tiles(dot(pick_top[...], window[:, T_AT:C_AT]), leaves).astype(BF16)
    coeffs = tiles(dot(pick_far[...], window[:, C_AT : C_AT + RANK]), leaves).astype(BF16)
    panels = dot(pick_near[...], window[:, :PANEL]).astype(BF16)
    tops = diagonal(dot(parents, top[...]), PRANK)
    tops = sum(tops[:, at : at + PRANK] for at in range(0, tops.shape[1], PRANK)).astype(BF16)
    local = diagonal(dot(coeffs, coupling[...]), RANK) + diagonal(dot_nt(tops, transfer), 2 * RANK)
    total = dot(diagonal(flat(local), RANK).astype(BF16), leaf_basis)
    row = lax.broadcasted_iota(jnp.int32, total.shape, 0)
    for i in range(leaves):
        image = jnp.zeros(total.shape, F32)
        for k in range(near.shape[1]):
            image += dot(panels[k * leaves : (k + 1) * leaves], near[i, k])
        total += jnp.where(row == i, image, jnp.zeros_like(image))
    return 0.5 * field + total


def stacked(ref):
    return ref[...].reshape(ref.shape[0] * ref.shape[1], ref.shape[2])


def start_kernel(basis, leaf_basis, transfer, product, stack, basis_in, leaf_basis_in, transfer_in, sems):
    copies = [
        pltpu.make_async_copy(source, target, sems.at[n])
        for n, (source, target) in enumerate(
            ((basis, basis_in), (leaf_basis, leaf_basis_in), (transfer, transfer_in))
        )
    ]
    for copy in copies:
        copy.start()
    for copy in copies:
        copy.wait()
    count = basis.shape[0]
    for i in range(product.shape[0]):
        product[i : i + 1, :] = basis_in[count - 1 : count, i * PANEL : (i + 1) * PANEL]
    write_stack(product[...], stacked(leaf_basis_in), stacked(transfer_in), stack)


def prepare_kernel(
    _, roots, near, near_ids, coupling, far_ids, top, top_ids,
    scales, near_out, coupling_out, top_out, pick_near, pick_far, pick_top,
    roots_in, near_in, coupling_in, top_in, near_ids_in, far_ids_in, top_ids_in, sems,
):
    leaves = near.shape[0]
    pairs = [
        (roots, roots_in), (near_ids, near_ids_in), (far_ids, far_ids_in), (top_ids, top_ids_in),
        (coupling, coupling_in), (top, top_in),
    ] + [(near.at[i], near_in.at[i]) for i in range(leaves)]
    copies = [
        pltpu.make_async_copy(source, target, sems.at[n]) for n, (source, target) in enumerate(pairs)
    ]
    for copy in copies:
        copy.start()
    for copy in copies[:4]:
        copy.wait()
    for k in range(roots.shape[1]):
        scales[k * leaves : (k + 1) * leaves, :] = jnp.broadcast_to(
            roots_in[:, k : k + 1], (leaves, scales.shape[1])
        )
    place = lax.axis_index(AXES)
    odd = place % 2 == 1
    left, right = jnp.where(odd, leaves, 2 * leaves), jnp.where(odd, 2 * leaves, leaves)
    for ids_in, pick, rows in (
        (near_ids_in, pick_near, leaves), (far_ids_in, pick_far, leaves), (top_ids_in, pick_top, leaves // 2),
    ):
        away = ids_in[...] - place * rows
        where = jnp.where(away < 0, away + rows + left, jnp.where(away < rows, away, away - rows + right))
        lane = lax.broadcasted_iota(jnp.int32, (rows, SOURCES), 1)
        for k in range(ids_in.shape[1]):
            hot = jnp.where(lane == where[:, k : k + 1], 1.0, 0.0)
            if rows < leaves:
                hot = jnp.concatenate([hot, jnp.zeros((leaves - rows, SOURCES), F32)], axis=0)
            pick[k * leaves : (k + 1) * leaves, :] = hot.astype(BF16)
    copies[4].wait()
    for i in range(leaves):
        for k in range(coupling.shape[1]):
            rows, lanes = slice(k * RANK, (k + 1) * RANK), slice(i * RANK, (i + 1) * RANK)
            coupling_out[rows, lanes] = coupling_in[i, k].T
    copies[5].wait()
    for p in range(top.shape[0]):
        for k in range(top.shape[1]):
            rows, lanes = slice(k * PRANK, (k + 1) * PRANK), slice(p * PRANK, (p + 1) * PRANK)
            top_out[rows, lanes] = top_in[p, k].T
    for i in range(leaves):
        copies[6 + i].wait()
        for k in range(near.shape[1]):
            near_out[i, k] = near_in[i, k].T


def step_kernel(
    step, last, scales, product, partial, own, mate, far, pick_near, pick_far, pick_top,
    near, leaf_basis, coupling, transfer, top, product_out, partial_out, stack,
):
    leaves = product.shape[0]
    basis_rows, transfer_rows = stacked(leaf_basis), stacked(transfer)
    field = product[...]
    image = apply_rows(
        field, own, mate, far, pick_near, pick_far, pick_top, near, basis_rows, coupling, transfer_rows, top
    )
    root = scales[step * leaves : (step + 1) * leaves, :]
    after = field - image / root
    total = field / root
    if step:
        total += partial[...]
    if last:
        total += after / scales[(step + 1) * leaves : (step + 2) * leaves, :]
    product_out[...] = after
    partial_out[...] = total
    write_stack(total if last else after, basis_rows, transfer_rows, stack)


def last_kernel(
    field, own, mate, far, pick_near, pick_far, pick_top,
    near, leaf_basis, coupling, transfer, top, basis, image_out, sums,
):
    image = apply_rows(
        field[...], own, mate, far, pick_near, pick_far, pick_top,
        near, stacked(leaf_basis), coupling, stacked(transfer), top,
    )
    image_out[...] = image
    count, leaves = basis.shape[0], image.shape[0]
    lane = lax.broadcasted_iota(jnp.int32, (count, 128), 1)
    sub = lax.broadcasted_iota(jnp.int32, (count, 128), 0)
    vectors = basis[...]
    packed = jnp.zeros((count, 128), F32)
    for n in range(count):
        column = jnp.sum(vectors * vectors[n : n + 1], axis=1, keepdims=True)
        packed = jnp.where(lane == n * count + sub, column, packed)
    dots = jnp.zeros((count, PANEL), F32)
    for i in range(leaves):
        dots += basis[:, i * PANEL : (i + 1) * PANEL] * image[i : i + 1]
    column = jnp.sum(dots, axis=1, keepdims=True)
    packed = jnp.where(lane == count * count + sub, column, packed)
    column = jnp.sum(image * image, axis=1, keepdims=True)
    packed = jnp.where(lane == count * count + count, column, packed)
    sums[...] = jnp.broadcast_to(jnp.sum(packed, axis=0, keepdims=True), sums.shape)


def finish_kernel(size, sums, image, basis, vector_out, hessen_out):
    count, leaves = basis.shape[0], image.shape[0]
    lane = lax.broadcasted_iota(jnp.int32, (count, 128), 1)
    sub = lax.broadcasted_iota(jnp.int32, (count, 128), 0)
    totals = jnp.broadcast_to(jnp.sum(sums[...], axis=0, keepdims=True) / size, (count, 128))
    zero = jnp.zeros((count, 128), F32)
    here = lane == count * count + sub
    coef = jnp.sum(jnp.where(here, totals, zero), axis=1, keepdims=True)
    inner = jnp.sum(jnp.where(lane % count == sub, coef, zero), axis=0, keepdims=True)
    outer = jnp.sum(jnp.where(lane // count == sub, coef, zero), axis=0, keepdims=True)
    gram = jnp.where(lane[:1] < count * count, totals[:1] * inner * outer, zero[:1])
    length = jnp.where(lane[:1] == count * count + count, totals[:1], zero[:1])
    squared = jnp.sum(gram + length, axis=1, keepdims=True)
    squared = squared - 2.0 * jnp.sum(coef * coef, axis=0, keepdims=True)
    beta = jnp.sqrt(squared + 1e-06)
    for i in range(leaves):
        taken = jnp.sum(coef * basis[:, i * PANEL : (i + 1) * PANEL], axis=0, keepdims=True)
        row = (image[i : i + 1, :] - taken) / beta
        vector_out[2 * i : 2 * i + 1, :] = row[:, : PANEL // 2]
        vector_out[2 * i + 1 : 2 * i + 2, :] = row[:, PANEL // 2 :]
    values = jnp.sum(jnp.where(lane == sub, coef, zero), axis=0, keepdims=True)
    hessen_out[...] = jnp.where(lane[:1] == count, beta, values)


def call(kernel, specs, outs, scratch=()):
    shapes = [jax.ShapeDtypeStruct(shape, dtype) for shape, dtype in outs]
    return pl.pallas_call(
        kernel,
        out_shape=shapes,
        in_specs=specs,
        out_specs=[VMEM] * len(shapes),
        scratch_shapes=list(scratch),
        compiler_params=pltpu.CompilerParams(vmem_limit_bytes=24 << 20),
    )


def like(array):
    return pltpu.VMEM(array.shape, array.dtype)


def body(
    basis, roots, near_blocks, near_ids, leaf_basis, far_coupling, far_ids, transfer, top_coupling, top_ids
):
    leaves, nears = near_blocks.shape[:2]
    fars, parents, tops = far_coupling.shape[1], *top_coupling.shape[:2]
    devices = lax.axis_size("grp") * lax.axis_size("leaf")
    mates = [(i, i ^ 1) for i in range(devices)]
    others = [(i, (((i + 1) ^ 1) - 1) % devices) for i in range(devices)]

    product, stack, basis, leaf_basis, transfer = call(
        start_kernel,
        [HBM] * 3,
        [((leaves, PANEL), F32), ((leaves, WIDTH), BF16)] + [(a.shape, a.dtype) for a in (basis, leaf_basis, transfer)],
        [pltpu.SemaphoreType.DMA((3,))],
    )(basis, leaf_basis, transfer)
    far = lax.ppermute(stack, AXES, others)
    mate = lax.ppermute(stack, AXES, mates)
    roots = roots.reshape(1, -1)
    scales, near, coupling, top, *picks = call(
        prepare_kernel,
        [VMEM] + [HBM] * 7,
        [
            ((roots.shape[1] * leaves, PANEL), F32),
            (near_blocks.shape, BF16),
            ((fars * RANK, leaves * RANK), BF16),
            ((tops * PRANK, parents * PRANK), BF16),
            ((nears * leaves, SOURCES), BF16),
            ((fars * leaves, SOURCES), BF16),
            ((tops * leaves, SOURCES), BF16),
        ],
        [like(a) for a in (roots, near_blocks, far_coupling, top_coupling, near_ids, far_ids, top_ids)]
        + [pltpu.SemaphoreType.DMA((6 + leaves,))],
    )(product, roots, near_blocks, near_ids, far_coupling, far_ids, top_coupling, top_ids)
    matrices = (*picks, near, leaf_basis, coupling, transfer, top)
    partial = product
    steps = roots.shape[1] - 1
    for step in range(steps):
        product, partial, stack = call(
            functools.partial(step_kernel, step, step == steps - 1),
            [VMEM] * 14,
            [((leaves, PANEL), F32), ((leaves, PANEL), F32), ((leaves, WIDTH), BF16)],
        )(scales, product, partial, stack, mate, far, *matrices)
        far = lax.ppermute(stack, AXES, others)
        mate = lax.ppermute(stack, AXES, mates)
    image, sums = call(
        last_kernel, [VMEM] * 13, [((leaves, PANEL), F32), ((devices, 128), F32)]
    )(partial, stack, mate, far, *matrices, basis)
    sums = lax.all_to_all(sums.reshape(devices, 1, 128), AXES, 0, 0, tiled=True)
    size = float(leaves * PANEL * devices)
    vector, hessen = call(
        functools.partial(finish_kernel, size), [VMEM] * 3, [((leaves * 2, 128), F32), ((1, 128), F32)]
    )(sums.reshape(devices, 128), image, basis)
    return vector.reshape(leaves * PANEL), hessen[0, : basis.shape[0] + 1]


def solution(mesh):
    split = P(AXES)
    in_specs = (P(None, AXES), P()) + (split,) * 8
    return jax.shard_map(body, mesh=mesh, in_specs=in_specs, out_specs=(split, P()), check_vma=False)
```

time: 109 us -> 89.9 us (0.82)
  blocking collectives: 43.9 us -> 24.3 us
  starting transfers between devices: 22.4 us -> 34.6 us
  Pallas kernels: 22.4 us -> 14.3 us
  local copies, waits for them, and re-layouts: 13 us -> 11.1 us
  waiting for transfers between devices: 6.04 us -> 4.44 us
    ppermute x5, starting transfers between devices: 0.64 us -> 31.4 us  [body(): mate = lax.ppermute(stack, AXES, mates)]
    all_to_all x1, blocking collectives: 43.9 us -> 24.3 us  [body(): sums = lax.all_to_all(sums.reshape(devices, 1, 128), AXES, 0, 0, tiled=True)]
    ppermute x5, starting transfers between devices: 21.8 us -> 3.19 us  [body(): far = lax.ppermute(stack, AXES, others)]
    pallas_call x6 -> x7, Pallas kernels: 21.6 us -> 13.5 us  [the longest x4 7.48 us: body(): call(functools.partial(step_kernel, step, step == steps - 1), [VMEM] * 14...]
    ppermute x5, waiting for transfers between devices: 5.91 us -> 1.96 us  [body(): far = lax.ppermute(stack, AXES, others)]
    ppermute x5, waiting for transfers between devices: 0.13 us -> 2.48 us  [body(): mate = lax.ppermute(stack, AXES, mates)]
    unnamed x36 -> x20, local copies, waits for them, and re-layouts: 12.5 us -> 10.6 us
  transfers between devices with their start and end apart: 10 -> 10, of which waited for: 6 -> 4; matrix products, arithmetic and copies ran while one was open for 0% -> 0% of each run, Pallas kernels for 0% -> 4%
where the time goes in v2:
time: 89.9 us; the launch traced here: 89.5 us
  starting transfers between devices  34.6 us (38%)
  blocking collectives  24.3 us (27%)
  Pallas kernels  14.3 us (16%)
  local copies, waits for them, and re-layouts  11.1 us (12%)
  waiting for transfers between devices  4.44 us (5%)
    ppermute x5, starting transfers between devices, body(): mate = lax.ppermute(stack, AXES, mates)  31.4 us
    all_to_all x1, blocking collectives, body(): sums = lax.all_to_all(sums.reshape(devices, 1, 128), AXES, 0, 0, tiled=True)  24.3 us
    unnamed x20, local copies, waits for them, and re-layouts  10.6 us
    pallas_call x4, Pallas kernels, body(): call(functools.partial(step_kernel, step, step == steps - 1), [VMEM] * 14...  7.48 us
    pallas_call x1, Pallas kernels, body(): call(prepare_kernel, [VMEM] + [HBM] * 7, [((roots.shape[1] * leaves, PANE...  3.82 us
    ppermute x5, starting transfers between devices, body(): far = lax.ppermute(stack, AXES, others)  3.19 us
    ppermute x5, waiting for transfers between devices, body(): mate = lax.ppermute(stack, AXES, mates)  2.48 us
    ppermute x5, waiting for transfers between devices, body(): far = lax.ppermute(stack, AXES, others)  1.96 us
  transfers between devices with their start and end apart: 10, of which 4 were waited for; matrix products, arithmetic and copies ran while one was open for 0% of the time, Pallas kernels for 4%

profile of v2, /device:TPU:1, one launch (start us, length us, event | category | flops | bytes accessed | tf_op | source)
XLA Modules:
  0.0 89.5 jit_solution(13704294199537420782)
XLA Ops:
  0.6 0.0 copy-start.3
  0.6 0.9 %copy-done.3 = bf16[8,64,256]{2,1,0:T(8,128)(2,1)S(1)} copy-done((bf16[8,64,256]{2,1,0:T(8,128)(2,1)S(1)}, bf16[8,64,256]{2,1,0:T(8,128)(2,1)}, u32[]{:S(2)}) %copy-start.3) | copy-done | bytes 262168
  1.6 0.0 copy-start.4
  1.6 0.9 %copy-done.4 = bf16[8,64,128]{2,1,0:T(8,128)(2,1)S(1)} copy-done((bf16[8,64,128]{2,1,0:T(8,128)(2,1)S(1)}, bf16[8,64,128]{2,1,0:T(8,128)(2,1)}, u32[]{:S(2)}) %copy-start.4) | copy-done | bytes 131096
  2.5 0.0 copy-start.5
  2.5 0.8 copy-done.5
  3.3 0.6 shard_map.113
  3.9 3.1 %collective-permute-start.1 = (bf16[8,512]{1,0:T(8,128)(2,1)S(1)}, bf16[8,512]{1,0:T(8,128)(2,1)S(1)}, u32[]{:S(2)}, u32[]{:S(2)}) collective-permute-start(bf16[8,512]{1,0:T(8,128)(2,1)S(1)} %get-tuple-element.31.own), channel_id=1, source_target_pairs={{0,255},{1,2},{2,1},{3,4},{4,3},{5,6},{6,5},{7,8},{8,7},{9,10},{10... | collective-permute-start | bytes 24584 | tf_op jit(solution)/shard_map/ppermute | solution.py:252
  7.0 8.4 %collective-permute-start = (bf16[8,512]{1,0:T(8,128)(2,1)S(1)}, bf16[8,512]{1,0:T(8,128)(2,1)S(1)}, u32[]{:S(2)}, u32[]{:S(2)}) collective-permute-start(bf16[8,512]{1,0:T(8,128)(2,1)S(1)} %get-tuple-element.31.own), channel_id=1, source_target_pairs={{0,1},{1,0},{2,3},{3,2},{4,5},{5,4},{6,7},{7,6},{8,9},{9,8},{10,11... | collective-permute-start | bytes 24584 | tf_op jit(solution)/shard_map/ppermute | solution.py:253
  15.4 0.0 copy-start
  15.4 2.8 %copy-done = bf16[8,6,256,256]{3,2,1,0:T(8,128)(2,1)S(1)} copy-done((bf16[8,6,256,256]{3,2,1,0:T(8,128)(2,1)S(1)}, bf16[8,6,256,256]{3,2,1,0:T(8,128)(2,1)}, u32[]{:S(2)}) %copy-start) | copy-done | bytes 6291480
  18.2 0.0 copy-start.1
  18.2 1.2 %copy-done.1 = bf16[8,8,64,64]{3,2,1,0:T(8,128)(2,1)S(1)} copy-done((bf16[8,8,64,64]{3,2,1,0:T(8,128)(2,1)S(1)}, bf16[8,8,64,64]{3,2,1,0:T(8,128)(2,1)}, u32[]{:S(2)}) %copy-start.1) | copy-done | bytes 524312
  19.5 0.0 copy-start.2
  19.5 1.2 %copy-done.2 = bf16[4,8,128,128]{3,2,1,0:T(8,128)(2,1)S(1)} copy-done((bf16[4,8,128,128]{3,2,1,0:T(8,128)(2,1)S(1)}, bf16[4,8,128,128]{3,2,1,0:T(8,128)(2,1)}, u32[]{:S(2)}) %copy-start.2) | copy-done | bytes 1048600
  20.7 0.0 copy-start.6
  20.7 0.7 copy-done.6
  21.4 0.0 copy-start.7
  21.4 0.7 copy-done.7
  22.1 0.7 copy-done.8
  22.7 0.7 copy-done.9
  23.4 3.8 %shard_map.114 = (f32[40,256]{1,0:T(8,128)S(1)}, bf16[8,6,256,256]{3,2,1,0:T(8,128)(2,1)S(1)}, bf16[512,512]{1,0:T(8,128)(2,1)S(1)}, bf16[1024,512]{1,0:T(8,128)...) custom-call(f32[8,256]{1,0:T(8,128)S(1)} %get-tuple-element.29._.product.partial, ...), custom_call_target="tpu_custom_call" | custom-call | tf_op jit(solution)/shard_map/pallas_call | solution.py:255
  27.2 0.0 collective-permute-done.1.far
  27.2 0.0 collective-permute-done.mate
  27.2 1.8 %shard_map.115 = (f32[8,256]{1,0:T(8,128)S(1)}, f32[8,256]{1,0:T(8,128)S(1)}, bf16[8,512]{1,0:T(8,128)(2,1)S(1)}) custom-call(f32[40,256]{1,0:T(8,128)S(1)} %get-tuple-element.30.scales, f32[8,256]{1,0:T(8,128)S(1)} %get-tuple-element.29._.product.partial, f32[8,256]{1,0:T(8,128)S(1)} %get-tuple-element.29._.product.partial, ...), custom_call_target="tpu_custom_call" | custom-call | tf_op jit(solution)/shard_map/pallas_call | solution.py:274
  29.0 0.0 collective-permute-start.3
  29.0 1.1 %collective-permute-start.2 = (bf16[8,512]{1,0:T(8,128)(2,1)S(1)}, bf16[8,512]{1,0:T(8,128)(2,1)S(1)}, u32[]{:S(2)}, u32[]{:S(2)}) collective-permute-start(bf16[8,512]{1,0:T(8,128)(2,1)S(1)} %get-tuple-element.42.own), channel_id=1, source_target_pairs={{0,1},{1,0},{2,3},{3,2},{4,5},{5,4},{6,7},{7,6},{8,9},{9,8},{10,11... | collective-permute-start | bytes 24584 | tf_op jit(solution)/shard_map/ppermute | solution.py:280
  30.1 2.0 %collective-permute-done.3.far = bf16[8,512]{1,0:T(8,128)(2,1)S(1)} collective-permute-done((bf16[8,512]{1,0:T(8,128)(2,1)S(1)}, bf16[8,512]{1,0:T(8,128)(2,1)S(1)}, u32[]{:S(2)}, u32[]{:S(2)}) %collective-permute-start.3) | collective-permute-done | bytes 8224 | tf_op jit(solution)/shard_map/ppermute | solution.py:279
  32.1 0.0 collective-permute-done.2.mate
  32.1 1.8 %shard_map.116 = (f32[8,256]{1,0:T(8,128)S(1)}, f32[8,256]{1,0:T(8,128)S(1)}, bf16[8,512]{1,0:T(8,128)(2,1)S(1)}) custom-call(f32[40,256]{1,0:T(8,128)S(1)} %get-tuple-element.30.scales, f32[8,256]{1,0:T(8,128)S(1)} %get-tuple-element.40.product, f32[8,256]{1,0:T(8,128)S(1)} %get-tuple-element.41.partial, bf16[8,512]{1,0:T(8,128)(2,1)S(1)} %get-tuple-element.42.own, ...), custom_call_target="tpu_custom_call" | custom-call | tf_op jit(solution)/shard_map/pallas_call | solution.py:274
  33.8 0.0 collective-permute-start.5
  33.9 6.5 %collective-permute-start.4 = (bf16[8,512]{1,0:T(8,128)(2,1)S(1)}, bf16[8,512]{1,0:T(8,128)(2,1)S(1)}, u32[]{:S(2)}, u32[]{:S(2)}) collective-permute-start(bf16[8,512]{1,0:T(8,128)(2,1)S(1)} %get-tuple-element.45.own), channel_id=1, source_target_pairs={{0,1},{1,0},{2,3},{3,2},{4,5},{5,4},{6,7},{7,6},{8,9},{9,8},{10,11... | collective-permute-start | bytes 24584 | tf_op jit(solution)/shard_map/ppermute | solution.py:280
  40.4 0.0 collective-permute-done.5.far
  40.4 0.8 collective-permute-done.4.mate
  41.2 1.7 %shard_map.117 = (f32[8,256]{1,0:T(8,128)S(1)}, f32[8,256]{1,0:T(8,128)S(1)}, bf16[8,512]{1,0:T(8,128)(2,1)S(1)}) custom-call(f32[40,256]{1,0:T(8,128)S(1)} %get-tuple-element.30.scales, f32[8,256]{1,0:T(8,128)S(1)} %get-tuple-element.43.product, f32[8,256]{1,0:T(8,128)S(1)} %get-tuple-element.44.partial, bf16[8,512]{1,0:T(8,128)(2,1)S(1)} %get-tuple-element.45.own, ...), custom_call_target="tpu_custom_call" | custom-call | tf_op jit(solution)/shard_map/pallas_call | solution.py:274
  43.0 0.0 collective-permute-start.7
  43.0 7.7 %collective-permute-start.6 = (bf16[8,512]{1,0:T(8,128)(2,1)S(1)}, bf16[8,512]{1,0:T(8,128)(2,1)S(1)}, u32[]{:S(2)}, u32[]{:S(2)}) collective-permute-start(bf16[8,512]{1,0:T(8,128)(2,1)S(1)} %get-tuple-element.48.own), channel_id=1, source_target_pairs={{0,1},{1,0},{2,3},{3,2},{4,5},{5,4},{6,7},{7,6},{8,9},{9,8},{10,11... | collective-permute-start | bytes 24584 | tf_op jit(solution)/shard_map/ppermute | solution.py:280
  50.7 0.0 collective-permute-done.7.far
  50.7 0.8 collective-permute-done.6.mate
  51.5 2.2 %shard_map.118 = (f32[8,256]{1,0:T(8,128)}, f32[8,256]{1,0:T(8,128)S(1)}, bf16[8,512]{1,0:T(8,128)(2,1)S(1)}) custom-call(f32[40,256]{1,0:T(8,128)S(1)} %get-tuple-element.30.scales, f32[8,256]{1,0:T(8,128)S(1)} %get-tuple-element.46.product, f32[8,256]{1,0:T(8,128)S(1)} %get-tuple-element.47.partial, bf16[8,512]{1,0:T(8,128)(2,1)S(1)} %get-tuple-element.48.own, ...), custom_call_target="tpu_custom_call" | custom-call | tf_op jit(solution)/shard_map/pallas_call | solution.py:274
  53.7 0.0 collective-permute-start.9
  53.7 7.7 %collective-permute-start.8 = (bf16[8,512]{1,0:T(8,128)(2,1)S(1)}, bf16[8,512]{1,0:T(8,128)(2,1)S(1)}, u32[]{:S(2)}, u32[]{:S(2)}) collective-permute-start(bf16[8,512]{1,0:T(8,128)(2,1)S(1)} %get-tuple-element.50.own), channel_id=1, source_target_pairs={{0,1},{1,0},{2,3},{3,2},{4,5},{5,4},{6,7},{7,6},{8,9},{9,8},{10,11... | collective-permute-start | bytes 24584 | tf_op jit(solution)/shard_map/ppermute | solution.py:280
  61.4 0.0 collective-permute-done.9.far
  61.4 0.8 collective-permute-done.8.mate
  62.2 1.6 %shard_map.119 = (f32[8,256]{1,0:T(8,128)S(1)}, f32[256,128]{1,0:T(8,128)S(1)}) custom-call(f32[8,256]{1,0:T(8,128)S(1)} %get-tuple-element.49.field, bf16[8,512]{1,0:T(8,128)(2,1)S(1)} %get-tuple-element.50.own, bf16[8,512]{1,0:T(8,128)(2,1)S(1)} %collective-permute-done.8.mate, bf16[8,512]{1,0:T(8,128)(2,1)S(1)} %collective-permute-done.9.far, ...), custom_call_target="tpu_custom_call" | custom-call | tf_op jit(solution)/shard_map/pallas_call | solution.py:281
  63.8 24.3 %all_to_all.5 = f32[256,1,128]{2,1,0:T(1,128)S(1)} all-to-all(f32[256,1,128]{2,1,0:T(1,128)S(1)} %bitcast.9), channel_id=1, replica_groups=mesh['grp'=4,'leaf'=64] {'grp','leaf'}, dimensions={0} | all-to-all | bytes 262144 | tf_op jit(solution)/shard_map/all_to_all | solution.py:284
  88.2 0.8 shard_map.120
  89.0 0.5 slice_bitcast_fusion
  (2 shorter events, 0.0 us)
Async XLA Ops:
  0.6 1.0 %copy-start.3 = (bf16[8,64,256]{2,1,0:T(8,128)(2,1)S(1)}, bf16[8,64,256]{2,1,0:T(8,128)(2,1)}, u32[]{:S(2)}) copy-start(bf16[8,64,256]{2,1,0:T(8,128)(2,1)} %leaf_basis.1) | copy-start | bytes 786436
  1.6 0.9 %copy-start.4 = (bf16[8,64,128]{2,1,0:T(8,128)(2,1)S(1)}, bf16[8,64,128]{2,1,0:T(8,128)(2,1)}, u32[]{:S(2)}) copy-start(bf16[8,64,128]{2,1,0:T(8,128)(2,1)} %transfer.1) | copy-start | bytes 393220
  2.5 0.8 copy-start.5
  3.9 23.3 %collective-permute-start.1 = (bf16[8,512]{1,0:T(8,128)(2,1)S(1)}, bf16[8,512]{1,0:T(8,128)(2,1)S(1)}, u32[]{:S(2)}, u32[]{:S(2)}) collective-permute-start(bf16[8,512]{1,0:T(8,128)(2,1)S(1)} %get-tuple-element.31.own), channel_id=1, source_target_pairs={{0,255},{1,2},{2,1},{3,4},{4,3},{5,6},{6,5},{7,8},{8,7},{9,10},{10... | collective-permute-start | bytes 24584 | tf_op jit(solution)/shard_map/ppermute | solution.py:252
  7.0 20.2 %collective-permute-start = (bf16[8,512]{1,0:T(8,128)(2,1)S(1)}, bf16[8,512]{1,0:T(8,128)(2,1)S(1)}, u32[]{:S(2)}, u32[]{:S(2)}) collective-permute-start(bf16[8,512]{1,0:T(8,128)(2,1)S(1)} %get-tuple-element.31.own), channel_id=1, source_target_pairs={{0,1},{1,0},{2,3},{3,2},{4,5},{5,4},{6,7},{7,6},{8,9},{9,8},{10,11... | collective-permute-start | bytes 24584 | tf_op jit(solution)/shard_map/ppermute | solution.py:253
  15.4 2.8 %copy-start = (bf16[8,6,256,256]{3,2,1,0:T(8,128)(2,1)S(1)}, bf16[8,6,256,256]{3,2,1,0:T(8,128)(2,1)}, u32[]{:S(2)}) copy-start(bf16[8,6,256,256]{3,2,1,0:T(8,128)(2,1)} %near.1) | copy-start | bytes 18874372
  18.2 1.2 %copy-start.1 = (bf16[8,8,64,64]{3,2,1,0:T(8,128)(2,1)S(1)}, bf16[8,8,64,64]{3,2,1,0:T(8,128)(2,1)}, u32[]{:S(2)}) copy-start(bf16[8,8,64,64]{3,2,1,0:T(8,128)(2,1)} %coupling.1) | copy-start | bytes 1572868
  19.5 1.2 %copy-start.2 = (bf16[4,8,128,128]{3,2,1,0:T(8,128)(2,1)S(1)}, bf16[4,8,128,128]{3,2,1,0:T(8,128)(2,1)}, u32[]{:S(2)}) copy-start(bf16[4,8,128,128]{3,2,1,0:T(8,128)(2,1)} %top.1) | copy-start | bytes 3145732
  20.7 0.7 copy-start.6
  21.4 0.7 copy-start.7
  22.1 0.7 copy-start.8
  22.7 0.7 copy-start.9
  29.0 3.1 %collective-permute-start.3 = (bf16[8,512]{1,0:T(8,128)(2,1)S(1)}, bf16[8,512]{1,0:T(8,128)(2,1)S(1)}, u32[]{:S(2)}, u32[]{:S(2)}) collective-permute-start(bf16[8,512]{1,0:T(8,128)(2,1)S(1)} %get-tuple-element.42.own), channel_id=1, source_target_pairs={{0,255},{1,2},{2,1},{3,4},{4,3},{5,6},{6,5},{7,8},{8,7},{9,10},{10... | collective-permute-start | bytes 24584 | tf_op jit(solution)/shard_map/ppermute | solution.py:279
  29.0 3.1 %collective-permute-start.2 = (bf16[8,512]{1,0:T(8,128)(2,1)S(1)}, bf16[8,512]{1,0:T(8,128)(2,1)S(1)}, u32[]{:S(2)}, u32[]{:S(2)}) collective-permute-start(bf16[8,512]{1,0:T(8,128)(2,1)S(1)} %get-tuple-element.42.own), channel_id=1, source_target_pairs={{0,1},{1,0},{2,3},{3,2},{4,5},{5,4},{6,7},{7,6},{8,9},{9,8},{10,11... | collective-permute-start | bytes 24584 | tf_op jit(solution)/shard_map/ppermute | solution.py:280
  33.8 6.6 %collective-permute-start.5 = (bf16[8,512]{1,0:T(8,128)(2,1)S(1)}, bf16[8,512]{1,0:T(8,128)(2,1)S(1)}, u32[]{:S(2)}, u32[]{:S(2)}) collective-permute-start(bf16[8,512]{1,0:T(8,128)(2,1)S(1)} %get-tuple-element.45.own), channel_id=1, source_target_pairs={{0,255},{1,2},{2,1},{3,4},{4,3},{5,6},{6,5},{7,8},{8,7},{9,10},{10... | collective-permute-start | bytes 24584 | tf_op jit(solution)/shard_map/ppermute | solution.py:279
  33.9 7.3 %collective-permute-start.4 = (bf16[8,512]{1,0:T(8,128)(2,1)S(1)}, bf16[8,512]{1,0:T(8,128)(2,1)S(1)}, u32[]{:S(2)}, u32[]{:S(2)}) collective-permute-start(bf16[8,512]{1,0:T(8,128)(2,1)S(1)} %get-tuple-element.45.own), channel_id=1, source_target_pairs={{0,1},{1,0},{2,3},{3,2},{4,5},{5,4},{6,7},{7,6},{8,9},{9,8},{10,11... | collective-permute-start | bytes 24584 | tf_op jit(solution)/shard_map/ppermute | solution.py:280
  43.0 7.7 %collective-permute-start.7 = (bf16[8,512]{1,0:T(8,128)(2,1)S(1)}, bf16[8,512]{1,0:T(8,128)(2,1)S(1)}, u32[]{:S(2)}, u32[]{:S(2)}) collective-permute-start(bf16[8,512]{1,0:T(8,128)(2,1)S(1)} %get-tuple-element.48.own), channel_id=1, source_target_pairs={{0,255},{1,2},{2,1},{3,4},{4,3},{5,6},{6,5},{7,8},{8,7},{9,10},{10... | collective-permute-start | bytes 24584 | tf_op jit(solution)/shard_map/ppermute | solution.py:279
  43.0 8.5 %collective-permute-start.6 = (bf16[8,512]{1,0:T(8,128)(2,1)S(1)}, bf16[8,512]{1,0:T(8,128)(2,1)S(1)}, u32[]{:S(2)}, u32[]{:S(2)}) collective-permute-start(bf16[8,512]{1,0:T(8,128)(2,1)S(1)} %get-tuple-element.48.own), channel_id=1, source_target_pairs={{0,1},{1,0},{2,3},{3,2},{4,5},{5,4},{6,7},{7,6},{8,9},{9,8},{10,11... | collective-permute-start | bytes 24584 | tf_op jit(solution)/shard_map/ppermute | solution.py:280
  53.7 7.7 %collective-permute-start.9 = (bf16[8,512]{1,0:T(8,128)(2,1)S(1)}, bf16[8,512]{1,0:T(8,128)(2,1)S(1)}, u32[]{:S(2)}, u32[]{:S(2)}) collective-permute-start(bf16[8,512]{1,0:T(8,128)(2,1)S(1)} %get-tuple-element.50.own), channel_id=1, source_target_pairs={{0,255},{1,2},{2,1},{3,4},{4,3},{5,6},{6,5},{7,8},{8,7},{9,10},{10... | collective-permute-start | bytes 24584 | tf_op jit(solution)/shard_map/ppermute | solution.py:279
  53.7 8.5 %collective-permute-start.8 = (bf16[8,512]{1,0:T(8,128)(2,1)S(1)}, bf16[8,512]{1,0:T(8,128)(2,1)S(1)}, u32[]{:S(2)}, u32[]{:S(2)}) collective-permute-start(bf16[8,512]{1,0:T(8,128)(2,1)S(1)} %get-tuple-element.50.own), channel_id=1, source_target_pairs={{0,1},{1,0},{2,3},{3,2},{4,5},{5,4},{6,7},{7,6},{8,9},{9,8},{10,11... | collective-permute-start | bytes 24584 | tf_op jit(solution)/shard_map/ppermute | solution.py:280

commit v3 on v2

--- a/solution.py
+++ b/solution.py
@@ -230,6 +230,10 @@
     )
 
 
+def pinned(*arrays):
+    return [pltpu.with_memory_space_constraint(a, pltpu.HBM) for a in arrays]
+
+
 def like(array):
     return pltpu.VMEM(array.shape, array.dtype)
 
@@ -248,7 +252,7 @@
         [HBM] * 3,
         [((leaves, PANEL), F32), ((leaves, WIDTH), BF16)] + [(a.shape, a.dtype) for a in (basis, leaf_basis, transfer)],
         [pltpu.SemaphoreType.DMA((3,))],
-    )(basis, leaf_basis, transfer)
+    )(*pinned(basis, leaf_basis, transfer))
     far = lax.ppermute(stack, AXES, others)
     mate = lax.ppermute(stack, AXES, mates)
     roots = roots.reshape(1, -1)
@@ -266,7 +270,7 @@
         ],
         [like(a) for a in (roots, near_blocks, far_coupling, top_coupling, near_ids, far_ids, top_ids)]
         + [pltpu.SemaphoreType.DMA((6 + leaves,))],
-    )(product, roots, near_blocks, near_ids, far_coupling, far_ids, top_coupling, top_ids)
+    )(product, *pinned(roots, near_blocks, near_ids, far_coupling, far_ids, top_coupling, top_ids))
     matrices = (*picks, near, leaf_basis, coupling, transfer, top)
     partial = product
     steps = roots.shape[1] - 1

time: 89.9 us -> 81.2 us (0.903)
  local copies, waits for them, and re-layouts: 11.1 us -> 0.51 us
  starting transfers between devices: 34.6 us -> 38.6 us
  blocking collectives: 24.3 us -> 22.3 us
  Pallas kernels: 14.3 us -> 15.6 us
  waiting for transfers between devices: 4.44 us -> 3.32 us
    unnamed x20 -> x0, local copies, waits for them, and re-layouts: 10.6 us -> none
    ppermute x5, starting transfers between devices: 31.4 us -> 35.5 us  [body(): mate = lax.ppermute(stack, AXES, mates)]
    all_to_all x1, blocking collectives: 24.3 us -> 22.3 us  [body(): sums = lax.all_to_all(sums.reshape(devices, 1, 128), AXES, 0, 0, tiled=True)]
    ppermute x5, waiting for transfers between devices: 1.96 us -> 0.01 us  [body(): far = lax.ppermute(stack, AXES, others)]
  transfers between devices with their start and end apart: 10 -> 10, of which waited for: 4 -> 4; matrix products, arithmetic and copies ran while one was open for 0% -> 0% of each run, Pallas kernels for 4% -> 5%
where the time goes in v3:
time: 81.2 us; the launch traced here: 81.1 us
  starting transfers between devices  38.6 us (48%)
  blocking collectives  22.3 us (27%)
  Pallas kernels  15.6 us (19%)
  waiting for transfers between devices  3.32 us (4%)
    ppermute x5, starting transfers between devices, body(): mate = lax.ppermute(stack, AXES, mates)  35.5 us
    all_to_all x1, blocking collectives, body(): sums = lax.all_to_all(sums.reshape(devices, 1, 128), AXES, 0, 0, tiled=True)  22.3 us
    pallas_call x4, Pallas kernels, body(): call(functools.partial(step_kernel, step, step == steps - 1), [VMEM] * 14...  7.48 us
    pallas_call x1, Pallas kernels, body(): call(prepare_kernel, [VMEM] + [HBM] * 7, [((roots.shape[1] * leaves, PANE...  4.41 us
    ppermute x5, waiting for transfers between devices, body(): mate = lax.ppermute(stack, AXES, mates)  3.3 us
    ppermute x5, starting transfers between devices, body(): far = lax.ppermute(stack, AXES, others)  3.15 us
  transfers between devices with their start and end apart: 10, of which 4 were waited for; matrix products, arithmetic and copies ran while one was open for 0% of the time, Pallas kernels for 5%

profile of v3, /device:TPU:1, one launch (start us, length us, event | category | flops | bytes accessed | tf_op | source)
XLA Modules:
  0.0 81.1 jit_solution(14913023664845171572)
XLA Ops:
  0.6 1.4 %shard_map.113 = (f32[8,256]{1,0:T(8,128)S(1)}, bf16[8,512]{1,0:T(8,128)(2,1)S(1)}, f32[8,2048]{1,0:T(8,128)S(1)}, bf16[8,64,256]{2,1,0:T(8,128)(2,1)S(1)}, bf16[8,64,128]{2,1,0:T(8,128)(2,1)S(1)}) custom-call(f32[8,2048]{1,0:T(8,128)} %basis.1, bf16[8,64,256]{2,1,0:T(8,128)(2,1)} %leaf_basis.1, bf16[8,64,128]{2,1,0:T(8,128)(2,1)} %transfer.1), custom_call_target="tpu_custom_call" | custom-call | tf_op jit(solution)/shard_map/pallas_call | solution.py:250
  2.0 3.1 %collective-permute-start.1 = (bf16[8,512]{1,0:T(8,128)(2,1)S(1)}, bf16[8,512]{1,0:T(8,128)(2,1)S(1)}, u32[]{:S(2)}, u32[]{:S(2)}) collective-permute-start(bf16[8,512]{1,0:T(8,128)(2,1)S(1)} %get-tuple-element.31.own), channel_id=1, source_target_pairs={{0,255},{1,2},{2,1},{3,4},{4,3},{5,6},{6,5},{7,8},{8,7},{9,10},{10... | collective-permute-start | bytes 24584 | tf_op jit(solution)/shard_map/ppermute | solution.py:256
  5.1 8.4 %collective-permute-start = (bf16[8,512]{1,0:T(8,128)(2,1)S(1)}, bf16[8,512]{1,0:T(8,128)(2,1)S(1)}, u32[]{:S(2)}, u32[]{:S(2)}) collective-permute-start(bf16[8,512]{1,0:T(8,128)(2,1)S(1)} %get-tuple-element.31.own), channel_id=1, source_target_pairs={{0,1},{1,0},{2,3},{3,2},{4,5},{5,4},{6,7},{7,6},{8,9},{9,8},{10,11... | collective-permute-start | bytes 24584 | tf_op jit(solution)/shard_map/ppermute | solution.py:257
  13.5 4.4 %shard_map.114 = (f32[40,256]{1,0:T(8,128)S(1)}, bf16[8,6,256,256]{3,2,1,0:T(8,128)(2,1)S(1)}, bf16[512,512]{1,0:T(8,128)(2,1)S(1)}, bf16[1024,512]{1,0:T(8,128)...) custom-call(f32[8,256]{1,0:T(8,128)S(1)} %get-tuple-element.29._.product.partial, ...), custom_call_target="tpu_custom_call" | custom-call | tf_op jit(solution)/shard_map/pallas_call | solution.py:259
  18.0 0.0 collective-permute-done.1.far
  18.0 0.0 collective-permute-done.mate
  18.0 1.8 %shard_map.115 = (f32[8,256]{1,0:T(8,128)S(1)}, f32[8,256]{1,0:T(8,128)S(1)}, bf16[8,512]{1,0:T(8,128)(2,1)S(1)}) custom-call(f32[40,256]{1,0:T(8,128)S(1)} %get-tuple-element.30.scales, f32[8,256]{1,0:T(8,128)S(1)} %get-tuple-element.29._.product.partial, f32[8,256]{1,0:T(8,128)S(1)} %get-tuple-element.29._.product.partial, ...), custom_call_target="tpu_custom_call" | custom-call | tf_op jit(solution)/shard_map/pallas_call | solution.py:278
  19.7 0.0 collective-permute-start.3
  19.7 4.1 %collective-permute-start.2 = (bf16[8,512]{1,0:T(8,128)(2,1)S(1)}, bf16[8,512]{1,0:T(8,128)(2,1)S(1)}, u32[]{:S(2)}, u32[]{:S(2)}) collective-permute-start(bf16[8,512]{1,0:T(8,128)(2,1)S(1)} %get-tuple-element.42.own), channel_id=1, source_target_pairs={{0,1},{1,0},{2,3},{3,2},{4,5},{5,4},{6,7},{7,6},{8,9},{9,8},{10,11... | collective-permute-start | bytes 24584 | tf_op jit(solution)/shard_map/ppermute | solution.py:284
  23.8 0.0 collective-permute-done.3.far
  23.8 0.8 %collective-permute-done.2.mate = bf16[8,512]{1,0:T(8,128)(2,1)S(1)} collective-permute-done((bf16[8,512]{1,0:T(8,128)(2,1)S(1)}, bf16[8,512]{1,0:T(8,128)(2,1)S(1)}, u32[]{:S(2)}, u32[]{:S(2)}) %collective-permute-start.2) | collective-permute-done | bytes 8224 | tf_op jit(solution)/shard_map/ppermute | solution.py:284
  24.6 1.7 %shard_map.116 = (f32[8,256]{1,0:T(8,128)S(1)}, f32[8,256]{1,0:T(8,128)S(1)}, bf16[8,512]{1,0:T(8,128)(2,1)S(1)}) custom-call(f32[40,256]{1,0:T(8,128)S(1)} %get-tuple-element.30.scales, f32[8,256]{1,0:T(8,128)S(1)} %get-tuple-element.40.product, f32[8,256]{1,0:T(8,128)S(1)} %get-tuple-element.41.partial, bf16[8,512]{1,0:T(8,128)(2,1)S(1)} %get-tuple-element.42.own, ...), custom_call_target="tpu_custom_call" | custom-call | tf_op jit(solution)/shard_map/pallas_call | solution.py:278
  26.4 0.0 collective-permute-start.5
  26.4 7.7 %collective-permute-start.4 = (bf16[8,512]{1,0:T(8,128)(2,1)S(1)}, bf16[8,512]{1,0:T(8,128)(2,1)S(1)}, u32[]{:S(2)}, u32[]{:S(2)}) collective-permute-start(bf16[8,512]{1,0:T(8,128)(2,1)S(1)} %get-tuple-element.45.own), channel_id=1, source_target_pairs={{0,1},{1,0},{2,3},{3,2},{4,5},{5,4},{6,7},{7,6},{8,9},{9,8},{10,11... | collective-permute-start | bytes 24584 | tf_op jit(solution)/shard_map/ppermute | solution.py:284
  34.1 0.0 collective-permute-done.5.far
  34.1 0.8 %collective-permute-done.4.mate = bf16[8,512]{1,0:T(8,128)(2,1)S(1)} collective-permute-done((bf16[8,512]{1,0:T(8,128)(2,1)S(1)}, bf16[8,512]{1,0:T(8,128)(2,1)S(1)}, u32[]{:S(2)}, u32[]{:S(2)}) %collective-permute-start.4) | collective-permute-done | bytes 8224 | tf_op jit(solution)/shard_map/ppermute | solution.py:284
  34.9 1.8 %shard_map.117 = (f32[8,256]{1,0:T(8,128)S(1)}, f32[8,256]{1,0:T(8,128)S(1)}, bf16[8,512]{1,0:T(8,128)(2,1)S(1)}) custom-call(f32[40,256]{1,0:T(8,128)S(1)} %get-tuple-element.30.scales, f32[8,256]{1,0:T(8,128)S(1)} %get-tuple-element.43.product, f32[8,256]{1,0:T(8,128)S(1)} %get-tuple-element.44.partial, bf16[8,512]{1,0:T(8,128)(2,1)S(1)} %get-tuple-element.45.own, ...), custom_call_target="tpu_custom_call" | custom-call | tf_op jit(solution)/shard_map/pallas_call | solution.py:278
  36.6 0.0 collective-permute-start.7
  36.7 7.7 %collective-permute-start.6 = (bf16[8,512]{1,0:T(8,128)(2,1)S(1)}, bf16[8,512]{1,0:T(8,128)(2,1)S(1)}, u32[]{:S(2)}, u32[]{:S(2)}) collective-permute-start(bf16[8,512]{1,0:T(8,128)(2,1)S(1)} %get-tuple-element.48.own), channel_id=1, source_target_pairs={{0,1},{1,0},{2,3},{3,2},{4,5},{5,4},{6,7},{7,6},{8,9},{9,8},{10,11... | collective-permute-start | bytes 24584 | tf_op jit(solution)/shard_map/ppermute | solution.py:284
  44.3 0.0 collective-permute-done.7.far
  44.3 0.8 %collective-permute-done.6.mate = bf16[8,512]{1,0:T(8,128)(2,1)S(1)} collective-permute-done((bf16[8,512]{1,0:T(8,128)(2,1)S(1)}, bf16[8,512]{1,0:T(8,128)(2,1)S(1)}, u32[]{:S(2)}, u32[]{:S(2)}) %collective-permute-start.6) | collective-permute-done | bytes 8224 | tf_op jit(solution)/shard_map/ppermute | solution.py:284
  45.2 2.2 %shard_map.118 = (f32[8,256]{1,0:T(8,128)}, f32[8,256]{1,0:T(8,128)S(1)}, bf16[8,512]{1,0:T(8,128)(2,1)S(1)}) custom-call(f32[40,256]{1,0:T(8,128)S(1)} %get-tuple-element.30.scales, f32[8,256]{1,0:T(8,128)S(1)} %get-tuple-element.46.product, f32[8,256]{1,0:T(8,128)S(1)} %get-tuple-element.47.partial, bf16[8,512]{1,0:T(8,128)(2,1)S(1)} %get-tuple-element.48.own, ...), custom_call_target="tpu_custom_call" | custom-call | tf_op jit(solution)/shard_map/pallas_call | solution.py:278
  47.4 0.0 collective-permute-start.9
  47.4 7.7 %collective-permute-start.8 = (bf16[8,512]{1,0:T(8,128)(2,1)S(1)}, bf16[8,512]{1,0:T(8,128)(2,1)S(1)}, u32[]{:S(2)}, u32[]{:S(2)}) collective-permute-start(bf16[8,512]{1,0:T(8,128)(2,1)S(1)} %get-tuple-element.50.own), channel_id=1, source_target_pairs={{0,1},{1,0},{2,3},{3,2},{4,5},{5,4},{6,7},{7,6},{8,9},{9,8},{10,11... | collective-permute-start | bytes 24584 | tf_op jit(solution)/shard_map/ppermute | solution.py:284
  55.1 0.0 collective-permute-done.9.far
  55.1 0.8 %collective-permute-done.8.mate = bf16[8,512]{1,0:T(8,128)(2,1)S(1)} collective-permute-done((bf16[8,512]{1,0:T(8,128)(2,1)S(1)}, bf16[8,512]{1,0:T(8,128)(2,1)S(1)}, u32[]{:S(2)}, u32[]{:S(2)}) %collective-permute-start.8) | collective-permute-done | bytes 8224 | tf_op jit(solution)/shard_map/ppermute | solution.py:284
  55.9 1.6 %shard_map.119 = (f32[8,256]{1,0:T(8,128)S(1)}, f32[256,128]{1,0:T(8,128)S(1)}) custom-call(f32[8,256]{1,0:T(8,128)S(1)} %get-tuple-element.49.field, bf16[8,512]{1,0:T(8,128)(2,1)S(1)} %get-tuple-element.50.own, bf16[8,512]{1,0:T(8,128)(2,1)S(1)} %collective-permute-done.8.mate, bf16[8,512]{1,0:T(8,128)(2,1)S(1)} %collective-permute-done.9.far, ...), custom_call_target="tpu_custom_call" | custom-call | tf_op jit(solution)/shard_map/pallas_call | solution.py:285
  57.5 22.3 %all_to_all.5 = f32[256,1,128]{2,1,0:T(1,128)S(1)} all-to-all(f32[256,1,128]{2,1,0:T(1,128)S(1)} %bitcast.9), channel_id=1, replica_groups=mesh['grp'=4,'leaf'=64] {'grp','leaf'}, dimensions={0} | all-to-all | bytes 262144 | tf_op jit(solution)/shard_map/all_to_all | solution.py:288
  79.8 0.8 %shard_map.120 = (f32[16,128]{1,0:T(8,128)}, f32[1,128]{1,0:T(1,128)S(1)}) custom-call(f32[256,128]{1,0:T(8,128)S(1)} %bitcast.8, f32[8,256]{1,0:T(8,128)S(1)} %get-tuple-element.53.image, f32[8,2048]{1,0:T(8,128)S(1)} %get-tuple-element.51.basis), custom_call_target="tpu_custom_call" | custom-call | tf_op jit(solution)/shard_map/pallas_call | solution.py:290
  80.6 0.5 slice_bitcast_fusion
Async XLA Ops:
  2.0 16.0 %collective-permute-start.1 = (bf16[8,512]{1,0:T(8,128)(2,1)S(1)}, bf16[8,512]{1,0:T(8,128)(2,1)S(1)}, u32[]{:S(2)}, u32[]{:S(2)}) collective-permute-start(bf16[8,512]{1,0:T(8,128)(2,1)S(1)} %get-tuple-element.31.own), channel_id=1, source_target_pairs={{0,255},{1,2},{2,1},{3,4},{4,3},{5,6},{6,5},{7,8},{8,7},{9,10},{10... | collective-permute-start | bytes 24584 | tf_op jit(solution)/shard_map/ppermute | solution.py:256
  5.1 12.9 %collective-permute-start = (bf16[8,512]{1,0:T(8,128)(2,1)S(1)}, bf16[8,512]{1,0:T(8,128)(2,1)S(1)}, u32[]{:S(2)}, u32[]{:S(2)}) collective-permute-start(bf16[8,512]{1,0:T(8,128)(2,1)S(1)} %get-tuple-element.31.own), channel_id=1, source_target_pairs={{0,1},{1,0},{2,3},{3,2},{4,5},{5,4},{6,7},{7,6},{8,9},{9,8},{10,11... | collective-permute-start | bytes 24584 | tf_op jit(solution)/shard_map/ppermute | solution.py:257
  19.7 4.1 %collective-permute-start.3 = (bf16[8,512]{1,0:T(8,128)(2,1)S(1)}, bf16[8,512]{1,0:T(8,128)(2,1)S(1)}, u32[]{:S(2)}, u32[]{:S(2)}) collective-permute-start(bf16[8,512]{1,0:T(8,128)(2,1)S(1)} %get-tuple-element.42.own), channel_id=1, source_target_pairs={{0,255},{1,2},{2,1},{3,4},{4,3},{5,6},{6,5},{7,8},{8,7},{9,10},{10... | collective-permute-start | bytes 24584 | tf_op jit(solution)/shard_map/ppermute | solution.py:283
  19.7 4.9 %collective-permute-start.2 = (bf16[8,512]{1,0:T(8,128)(2,1)S(1)}, bf16[8,512]{1,0:T(8,128)(2,1)S(1)}, u32[]{:S(2)}, u32[]{:S(2)}) collective-permute-start(bf16[8,512]{1,0:T(8,128)(2,1)S(1)} %get-tuple-element.42.own), channel_id=1, source_target_pairs={{0,1},{1,0},{2,3},{3,2},{4,5},{5,4},{6,7},{7,6},{8,9},{9,8},{10,11... | collective-permute-start | bytes 24584 | tf_op jit(solution)/shard_map/ppermute | solution.py:284
  26.4 7.7 %collective-permute-start.5 = (bf16[8,512]{1,0:T(8,128)(2,1)S(1)}, bf16[8,512]{1,0:T(8,128)(2,1)S(1)}, u32[]{:S(2)}, u32[]{:S(2)}) collective-permute-start(bf16[8,512]{1,0:T(8,128)(2,1)S(1)} %get-tuple-element.45.own), channel_id=1, source_target_pairs={{0,255},{1,2},{2,1},{3,4},{4,3},{5,6},{6,5},{7,8},{8,7},{9,10},{10... | collective-permute-start | bytes 24584 | tf_op jit(solution)/shard_map/ppermute | solution.py:283
  26.4 8.5 %collective-permute-start.4 = (bf16[8,512]{1,0:T(8,128)(2,1)S(1)}, bf16[8,512]{1,0:T(8,128)(2,1)S(1)}, u32[]{:S(2)}, u32[]{:S(2)}) collective-permute-start(bf16[8,512]{1,0:T(8,128)(2,1)S(1)} %get-tuple-element.45.own), channel_id=1, source_target_pairs={{0,1},{1,0},{2,3},{3,2},{4,5},{5,4},{6,7},{7,6},{8,9},{9,8},{10,11... | collective-permute-start | bytes 24584 | tf_op jit(solution)/shard_map/ppermute | solution.py:284
  36.6 7.7 %collective-permute-start.7 = (bf16[8,512]{1,0:T(8,128)(2,1)S(1)}, bf16[8,512]{1,0:T(8,128)(2,1)S(1)}, u32[]{:S(2)}, u32[]{:S(2)}) collective-permute-start(bf16[8,512]{1,0:T(8,128)(2,1)S(1)} %get-tuple-element.48.own), channel_id=1, source_target_pairs={{0,255},{1,2},{2,1},{3,4},{4,3},{5,6},{6,5},{7,8},{8,7},{9,10},{10... | collective-permute-start | bytes 24584 | tf_op jit(solution)/shard_map/ppermute | solution.py:283
  36.7 8.5 %collective-permute-start.6 = (bf16[8,512]{1,0:T(8,128)(2,1)S(1)}, bf16[8,512]{1,0:T(8,128)(2,1)S(1)}, u32[]{:S(2)}, u32[]{:S(2)}) collective-permute-start(bf16[8,512]{1,0:T(8,128)(2,1)S(1)} %get-tuple-element.48.own), channel_id=1, source_target_pairs={{0,1},{1,0},{2,3},{3,2},{4,5},{5,4},{6,7},{7,6},{8,9},{9,8},{10,11... | collective-permute-start | bytes 24584 | tf_op jit(solution)/shard_map/ppermute | solution.py:284
  47.4 7.7 %collective-permute-start.9 = (bf16[8,512]{1,0:T(8,128)(2,1)S(1)}, bf16[8,512]{1,0:T(8,128)(2,1)S(1)}, u32[]{:S(2)}, u32[]{:S(2)}) collective-permute-start(bf16[8,512]{1,0:T(8,128)(2,1)S(1)} %get-tuple-element.50.own), channel_id=1, source_target_pairs={{0,255},{1,2},{2,1},{3,4},{4,3},{5,6},{6,5},{7,8},{8,7},{9,10},{10... | collective-permute-start | bytes 24584 | tf_op jit(solution)/shard_map/ppermute | solution.py:283
  47.4 8.5 %collective-permute-start.8 = (bf16[8,512]{1,0:T(8,128)(2,1)S(1)}, bf16[8,512]{1,0:T(8,128)(2,1)S(1)}, u32[]{:S(2)}, u32[]{:S(2)}) collective-permute-start(bf16[8,512]{1,0:T(8,128)(2,1)S(1)} %get-tuple-element.50.own), channel_id=1, source_target_pairs={{0,1},{1,0},{2,3},{3,2},{4,5},{5,4},{6,7},{7,6},{8,9},{9,8},{10,11... | collective-permute-start | bytes 24584 | tf_op jit(solution)/shard_map/ppermute | solution.py:284

commit v4 on v3

--- a/solution.py
+++ b/solution.py
@@ -145,16 +145,13 @@
             near_out[i, k] = near_in[i, k].T
 
 
-def step_kernel(
-    step, last, scales, product, partial, own, mate, far, pick_near, pick_far, pick_top,
-    near, leaf_basis, coupling, transfer, top, product_out, partial_out, stack,
-):
-    leaves = product.shape[0]
-    basis_rows, transfer_rows = stacked(leaf_basis), stacked(transfer)
-    field = product[...]
-    image = apply_rows(
-        field, own, mate, far, pick_near, pick_far, pick_top, near, basis_rows, coupling, transfer_rows, top
-    )
+def at_an_end():
+    place = lax.axis_index(AXES)
+    return jnp.logical_or(place == 0, place == lax.axis_size(AXES) - 1)
+
+
+def advance(step, last, image, field, scales, partial, leaf_basis, transfer, product_out, partial_out, stack):
+    leaves = field.shape[0]
     root = scales[step * leaves : (step + 1) * leaves, :]
     after = field - image / root
     total = field / root
@@ -164,18 +161,63 @@
         total += after / scales[(step + 1) * leaves : (step + 2) * leaves, :]
     product_out[...] = after
     partial_out[...] = total
-    write_stack(total if last else after, basis_rows, transfer_rows, stack)
-
-
-def last_kernel(
-    field, own, mate, far, pick_near, pick_far, pick_top,
-    near, leaf_basis, coupling, transfer, top, basis, image_out, sums,
+    write_stack(total if last else after, leaf_basis, transfer, stack)
+
+
+def step_kernel(
+    step, last, early, scales, product, partial, own, mate, far, picks, matrices, outs, ready=()
 ):
-    image = apply_rows(
-        field[...], own, mate, far, pick_near, pick_far, pick_top,
-        near, stacked(leaf_basis), coupling, stacked(transfer), top,
-    )
-    image_out[...] = image
+    near, leaf_basis, coupling, transfer, top = matrices
+
+    @pl.when(at_an_end() if early else jnp.logical_not(at_an_end()))
+    def _():
+        basis_rows, transfer_rows = stacked(leaf_basis), stacked(transfer)
+        field = product[...]
+        image = apply_rows(
+            field, own, mate, far, *picks, near, basis_rows, coupling, transfer_rows, top
+        )
+        advance(step, last, image, field, scales, partial, basis_rows, transfer_rows, *outs)
+
+    if not early:
+
+        @pl.when(at_an_end())
+        def _():
+            for source, target in zip(ready, outs):
+                target[...] = source[...]
+
+
+def step_early(step, last, scales, product, partial, own, mate, *rest):
+    step_kernel(step, last, True, scales, product, partial, own, mate, own, rest[:3], rest[3:8], rest[8:])
+
+
+def step_late(step, last, scales, product, partial, own, mate, far, *rest):
+    picks, matrices, ready, outs = rest[:3], rest[3:8], rest[8:11], rest[11:]
+    step_kernel(step, last, False, scales, product, partial, own, mate, far, picks, matrices, outs, ready)
+
+
+def last_image(early, field, own, mate, far, picks, matrices, image_out):
+    near, leaf_basis, coupling, transfer, top = matrices
+
+    @pl.when(at_an_end() if early else jnp.logical_not(at_an_end()))
+    def _():
+        image_out[...] = apply_rows(
+            field[...], own, mate, far, *picks, near, stacked(leaf_basis), coupling, stacked(transfer), top
+        )
+
+
+def last_early(field, own, mate, *rest):
+    last_image(True, field, own, mate, own, rest[:3], rest[3:8], rest[8])
+
+
+def last_late(field, own, mate, far, *rest):
+    picks, matrices, (basis, ready, image_out, sums) = rest[:3], rest[3:8], rest[8:]
+    last_image(False, field, own, mate, far, picks, matrices, image_out)
+
+    @pl.when(at_an_end())
+    def _():
+        image_out[...] = ready[...]
+
+    image = image_out[...]
     count, leaves = basis.shape[0], image.shape[0]
     lane = lax.broadcasted_iota(jnp.int32, (count, 128), 1)
     sub = lax.broadcasted_iota(jnp.int32, (count, 128), 0)
@@ -274,17 +316,21 @@
     matrices = (*picks, near, leaf_basis, coupling, transfer, top)
     partial = product
     steps = roots.shape[1] - 1
+    outs = [((leaves, PANEL), F32), ((leaves, PANEL), F32), ((leaves, WIDTH), BF16)]
     for step in range(steps):
-        product, partial, stack = call(
-            functools.partial(step_kernel, step, step == steps - 1),
-            [VMEM] * 14,
-            [((leaves, PANEL), F32), ((leaves, PANEL), F32), ((leaves, WIDTH), BF16)],
-        )(scales, product, partial, stack, mate, far, *matrices)
+        last = step == steps - 1
+        state = (scales, product, partial, stack, mate)
+        ready = call(functools.partial(step_early, step, last), [VMEM] * 13, outs)(*state, *matrices)
+        product, partial, stack = call(functools.partial(step_late, step, last), [VMEM] * 17, outs)(
+            *state, far, *matrices, *ready
+        )
         far = lax.ppermute(stack, AXES, others)
         mate = lax.ppermute(stack, AXES, mates)
-    image, sums = call(
-        last_kernel, [VMEM] * 13, [((leaves, PANEL), F32), ((devices, 128), F32)]
-    )(partial, stack, mate, far, *matrices, basis)
+    state = (partial, stack, mate)
+    ready = call(last_early, [VMEM] * 11, outs[:1])(*state, *matrices)
+    image, sums = call(last_late, [VMEM] * 14, [outs[0], ((devices, 128), F32)])(
+        *state, far, *matrices, basis, *ready
+    )
     sums = lax.all_to_all(sums.reshape(devices, 1, 128), AXES, 0, 0, tiled=True)
     size = float(leaves * PANEL * devices)
     vector, hessen = call(

time: 81.2 us -> 76.6 us (0.943)
  starting transfers between devices: 38.6 us -> 23.4 us
  waiting for transfers between devices: 3.32 us -> 12.3 us
  blocking collectives: 22.3 us -> 23.7 us
    ppermute x5, starting transfers between devices: 35.5 us -> 23.4 us  [body(): mate = lax.ppermute(stack, AXES, mates)]
    ppermute x5, waiting for transfers between devices: 0.01 us -> 8.99 us  [body(): far = lax.ppermute(stack, AXES, others)]
    ppermute x5, starting transfers between devices: 3.15 us -> 0.01 us  [body(): far = lax.ppermute(stack, AXES, others)]
    all_to_all x1, blocking collectives: 22.3 us -> 23.7 us  [body(): sums = lax.all_to_all(sums.reshape(devices, 1, 128), AXES, 0, 0, tiled=True)]
    pallas_call x5 -> x10, Pallas kernels: 9.05 us -> 9.24 us  [the longest x4 7.61 us: body(): call(functools.partial(step_late, step, last), [VMEM] * 17, outs)]
  transfers between devices with their start and end apart: 10 -> 10, of which waited for: 4 -> 8; matrix products, arithmetic and copies ran while one was open for 0% -> 0% of each run, Pallas kernels for 5% -> 6%
where the time goes in v4:
time: 76.6 us; the launch traced here: 76.4 us
  blocking collectives  23.7 us (31%)
  starting transfers between devices  23.4 us (31%)
  Pallas kernels  15.8 us (21%)
  waiting for transfers between devices  12.3 us (16%)
    all_to_all x1, blocking collectives, body(): sums = lax.all_to_all(sums.reshape(devices, 1, 128), AXES, 0, 0, tiled=True)  23.7 us
    ppermute x5, starting transfers between devices, body(): mate = lax.ppermute(stack, AXES, mates)  23.4 us
    ppermute x5, waiting for transfers between devices, body(): far = lax.ppermute(stack, AXES, others)  8.99 us
    pallas_call x4, Pallas kernels, body(): call(functools.partial(step_late, step, last), [VMEM] * 17, outs)  7.61 us
    pallas_call x1, Pallas kernels, body(): call(prepare_kernel, [VMEM] + [HBM] * 7, [((roots.shape[1] * leaves, PANE...  4.41 us
    ppermute x5, waiting for transfers between devices, body(): mate = lax.ppermute(stack, AXES, mates)  3.3 us
    pallas_call x1, Pallas kernels, body(): call(last_late, [VMEM] * 14, [outs[0], ((devices, 128), F32)])  1.6 us
  transfers between devices with their start and end apart: 10, of which 8 were waited for; matrix products, arithmetic and copies ran while one was open for 0% of the time, Pallas kernels for 6%

profile of v4, /device:TPU:1, one launch (start us, length us, event | category | flops | bytes accessed | tf_op | source)
XLA Modules:
  0.0 76.4 jit_solution(17390716838522485159)
XLA Ops:
  0.6 1.4 %shard_map.113 = (f32[8,256]{1,0:T(8,128)S(1)}, bf16[8,512]{1,0:T(8,128)(2,1)S(1)}, f32[8,2048]{1,0:T(8,128)S(1)}, bf16[8,64,256]{2,1,0:T(8,128)(2,1)S(1)}, bf16[8,64,128]{2,1,0:T(8,128)(2,1)S(1)}) custom-call(f32[8,2048]{1,0:T(8,128)} %basis.1, bf16[8,64,256]{2,1,0:T(8,128)(2,1)} %leaf_basis.1, bf16[8,64,128]{2,1,0:T(8,128)(2,1)} %transfer.1), custom_call_target="tpu_custom_call" | custom-call | tf_op jit(solution)/shard_map/pallas_call | solution.py:292
  2.0 3.3 %collective-permute-start = (bf16[8,512]{1,0:T(8,128)(2,1)S(1)}, bf16[8,512]{1,0:T(8,128)(2,1)S(1)}, u32[]{:S(2)}, u32[]{:S(2)}) collective-permute-start(bf16[8,512]{1,0:T(8,128)(2,1)S(1)} %get-tuple-element.43.own), channel_id=1, source_target_pairs={{0,1},{1,0},{2,3},{3,2},{4,5},{5,4},{6,7},{7,6},{8,9},{9,8},{10,11... | collective-permute-start | bytes 24584 | tf_op jit(solution)/shard_map/ppermute | solution.py:299
  5.3 0.0 collective-permute-start.1
  5.3 4.4 %shard_map.114 = (f32[40,256]{1,0:T(8,128)S(1)}, bf16[8,6,256,256]{3,2,1,0:T(8,128)(2,1)S(1)}, bf16[512,512]{1,0:T(8,128)(2,1)S(1)}, bf16[1024,512]{1,0:T(8,128)...) custom-call(f32[8,256]{1,0:T(8,128)S(1)} %get-tuple-element.41._.product.partial, ...), custom_call_target="tpu_custom_call" | custom-call | tf_op jit(solution)/shard_map/pallas_call | solution.py:301
  9.8 0.0 collective-permute-done.mate
  9.8 0.0 collective-permute-done.1.far
  9.8 1.8 %shard_map.116 = (f32[8,256]{1,0:T(8,128)S(1)}, f32[8,256]{1,0:T(8,128)S(1)}, bf16[8,512]{1,0:T(8,128)(2,1)S(1)}) custom-call(f32[40,256]{1,0:T(8,128)S(1)} %get-tuple-element.42.scales, f32[8,256]{1,0:T(8,128)S(1)} %get-tuple-element.41._.product.partial, f32[8,256]{1,0:T(8,128)S(1)} %get-tuple-element.41._.product.partial, ...), custom_call_target="tpu_custom_call" | custom-call | tf_op jit(solution)/shard_map/pallas_call | solution.py:324
  11.6 8.9 %collective-permute-start.2 = (bf16[8,512]{1,0:T(8,128)(2,1)S(1)}, bf16[8,512]{1,0:T(8,128)(2,1)S(1)}, u32[]{:S(2)}, u32[]{:S(2)}) collective-permute-start(bf16[8,512]{1,0:T(8,128)(2,1)S(1)} %get-tuple-element.57.own), channel_id=1, source_target_pairs={{0,1},{1,0},{2,3},{3,2},{4,5},{5,4},{6,7},{7,6},{8,9},{9,8},{10,11... | collective-permute-start | bytes 24584 | tf_op jit(solution)/shard_map/ppermute | solution.py:328
  20.5 0.0 collective-permute-start.3
  20.5 0.8 %collective-permute-done.2.mate = bf16[8,512]{1,0:T(8,128)(2,1)S(1)} collective-permute-done((bf16[8,512]{1,0:T(8,128)(2,1)S(1)}, bf16[8,512]{1,0:T(8,128)(2,1)S(1)}, u32[]{:S(2)}, u32[]{:S(2)}) %collective-permute-start.2) | collective-permute-done | bytes 8224 | tf_op jit(solution)/shard_map/ppermute | solution.py:328
  21.3 2.2 %collective-permute-done.3.far = bf16[8,512]{1,0:T(8,128)(2,1)S(1)} collective-permute-done((bf16[8,512]{1,0:T(8,128)(2,1)S(1)}, bf16[8,512]{1,0:T(8,128)(2,1)S(1)}, u32[]{:S(2)}, u32[]{:S(2)}) %collective-permute-start.3) | collective-permute-done | bytes 8224 | tf_op jit(solution)/shard_map/ppermute | solution.py:327
  23.6 1.7 %shard_map.118 = (f32[8,256]{1,0:T(8,128)S(1)}, f32[8,256]{1,0:T(8,128)S(1)}, bf16[8,512]{1,0:T(8,128)(2,1)S(1)}) custom-call(f32[40,256]{1,0:T(8,128)S(1)} %get-tuple-element.42.scales, f32[8,256]{1,0:T(8,128)S(1)} %get-tuple-element.55.product, f32[8,256]{1,0:T(8,128)S(1)} %get-tuple-element.56.partial, bf16[8,512]{1,0:T(8,128)(2,1)S(1)} %get-tuple-element.57.own, ...), custom_call_target="tpu_custom_call" | custom-call | tf_op jit(solution)/shard_map/pallas_call | solution.py:324
  25.3 3.8 %collective-permute-start.4 = (bf16[8,512]{1,0:T(8,128)(2,1)S(1)}, bf16[8,512]{1,0:T(8,128)(2,1)S(1)}, u32[]{:S(2)}, u32[]{:S(2)}) collective-permute-start(bf16[8,512]{1,0:T(8,128)(2,1)S(1)} %get-tuple-element.63.own), channel_id=1, source_target_pairs={{0,1},{1,0},{2,3},{3,2},{4,5},{5,4},{6,7},{7,6},{8,9},{9,8},{10,11... | collective-permute-start | bytes 24584 | tf_op jit(solution)/shard_map/ppermute | solution.py:328
  29.1 0.0 collective-permute-start.5
  29.1 0.8 %collective-permute-done.4.mate = bf16[8,512]{1,0:T(8,128)(2,1)S(1)} collective-permute-done((bf16[8,512]{1,0:T(8,128)(2,1)S(1)}, bf16[8,512]{1,0:T(8,128)(2,1)S(1)}, u32[]{:S(2)}, u32[]{:S(2)}) %collective-permute-start.4) | collective-permute-done | bytes 8224 | tf_op jit(solution)/shard_map/ppermute | solution.py:328
  29.9 2.2 %collective-permute-done.5.far = bf16[8,512]{1,0:T(8,128)(2,1)S(1)} collective-permute-done((bf16[8,512]{1,0:T(8,128)(2,1)S(1)}, bf16[8,512]{1,0:T(8,128)(2,1)S(1)}, u32[]{:S(2)}, u32[]{:S(2)}) %collective-permute-start.5) | collective-permute-done | bytes 8224 | tf_op jit(solution)/shard_map/ppermute | solution.py:327
  32.2 1.7 %shard_map.120 = (f32[8,256]{1,0:T(8,128)S(1)}, f32[8,256]{1,0:T(8,128)S(1)}, bf16[8,512]{1,0:T(8,128)(2,1)S(1)}) custom-call(f32[40,256]{1,0:T(8,128)S(1)} %get-tuple-element.42.scales, f32[8,256]{1,0:T(8,128)S(1)} %get-tuple-element.61.product, f32[8,256]{1,0:T(8,128)S(1)} %get-tuple-element.62.partial, bf16[8,512]{1,0:T(8,128)(2,1)S(1)} %get-tuple-element.63.own, ...), custom_call_target="tpu_custom_call" | custom-call | tf_op jit(solution)/shard_map/pallas_call | solution.py:324
  33.9 3.7 %collective-permute-start.6 = (bf16[8,512]{1,0:T(8,128)(2,1)S(1)}, bf16[8,512]{1,0:T(8,128)(2,1)S(1)}, u32[]{:S(2)}, u32[]{:S(2)}) collective-permute-start(bf16[8,512]{1,0:T(8,128)(2,1)S(1)} %get-tuple-element.69.own), channel_id=1, source_target_pairs={{0,1},{1,0},{2,3},{3,2},{4,5},{5,4},{6,7},{7,6},{8,9},{9,8},{10,11... | collective-permute-start | bytes 24584 | tf_op jit(solution)/shard_map/ppermute | solution.py:328
  37.6 0.0 collective-permute-start.7
  37.6 0.8 %collective-permute-done.6.mate = bf16[8,512]{1,0:T(8,128)(2,1)S(1)} collective-permute-done((bf16[8,512]{1,0:T(8,128)(2,1)S(1)}, bf16[8,512]{1,0:T(8,128)(2,1)S(1)}, u32[]{:S(2)}, u32[]{:S(2)}) %collective-permute-start.6) | collective-permute-done | bytes 8224 | tf_op jit(solution)/shard_map/ppermute | solution.py:328
  38.5 2.2 %collective-permute-done.7.far = bf16[8,512]{1,0:T(8,128)(2,1)S(1)} collective-permute-done((bf16[8,512]{1,0:T(8,128)(2,1)S(1)}, bf16[8,512]{1,0:T(8,128)(2,1)S(1)}, u32[]{:S(2)}, u32[]{:S(2)}) %collective-permute-start.7) | collective-permute-done | bytes 8224 | tf_op jit(solution)/shard_map/ppermute | solution.py:327
  40.7 2.4 %shard_map.122 = (f32[8,256]{1,0:T(8,128)}, f32[8,256]{1,0:T(8,128)S(1)}, bf16[8,512]{1,0:T(8,128)(2,1)S(1)}) custom-call(f32[40,256]{1,0:T(8,128)S(1)} %get-tuple-element.42.scales, f32[8,256]{1,0:T(8,128)S(1)} %get-tuple-element.67.product, f32[8,256]{1,0:T(8,128)S(1)} %get-tuple-element.68.partial, bf16[8,512]{1,0:T(8,128)(2,1)S(1)} %get-tuple-element.69.own, ...), custom_call_target="tpu_custom_call" | custom-call | tf_op jit(solution)/shard_map/pallas_call | solution.py:324
  43.1 3.7 %collective-permute-start.8 = (bf16[8,512]{1,0:T(8,128)(2,1)S(1)}, bf16[8,512]{1,0:T(8,128)(2,1)S(1)}, u32[]{:S(2)}, u32[]{:S(2)}) collective-permute-start(bf16[8,512]{1,0:T(8,128)(2,1)S(1)} %get-tuple-element.74.own), channel_id=1, source_target_pairs={{0,1},{1,0},{2,3},{3,2},{4,5},{5,4},{6,7},{7,6},{8,9},{9,8},{10,11... | collective-permute-start | bytes 24584 | tf_op jit(solution)/shard_map/ppermute | solution.py:328
  46.7 0.0 collective-permute-start.9
  46.7 0.8 %collective-permute-done.8.mate = bf16[8,512]{1,0:T(8,128)(2,1)S(1)} collective-permute-done((bf16[8,512]{1,0:T(8,128)(2,1)S(1)}, bf16[8,512]{1,0:T(8,128)(2,1)S(1)}, u32[]{:S(2)}, u32[]{:S(2)}) %collective-permute-start.8) | collective-permute-done | bytes 8224 | tf_op jit(solution)/shard_map/ppermute | solution.py:328
  47.6 2.2 %collective-permute-done.9.far = bf16[8,512]{1,0:T(8,128)(2,1)S(1)} collective-permute-done((bf16[8,512]{1,0:T(8,128)(2,1)S(1)}, bf16[8,512]{1,0:T(8,128)(2,1)S(1)}, u32[]{:S(2)}, u32[]{:S(2)}) %collective-permute-start.9) | collective-permute-done | bytes 8224 | tf_op jit(solution)/shard_map/ppermute | solution.py:327
  49.8 1.6 %shard_map.124 = (f32[8,256]{1,0:T(8,128)S(1)}, f32[256,128]{1,0:T(8,128)S(1)}) custom-call(f32[8,256]{1,0:T(8,128)S(1)} %get-tuple-element.73.field, bf16[8,512]{1,0:T(8,128)(2,1)S(1)} %get-tuple-element.74.own, bf16[8,512]{1,0:T(8,128)(2,1)S(1)} %collective-permute-done.8.mate, bf16[8,512]{1,0:T(8,128)(2,1)S(1)} %collective-permute-done.9.far, ...), custom_call_target="tpu_custom_call" | custom-call | tf_op jit(solution)/shard_map/pallas_call | solution.py:331
  51.4 23.7 %all_to_all.5 = f32[256,1,128]{2,1,0:T(1,128)S(1)} all-to-all(f32[256,1,128]{2,1,0:T(1,128)S(1)} %bitcast.9), channel_id=1, replica_groups=mesh['grp'=4,'leaf'=64] {'grp','leaf'}, dimensions={0} | all-to-all | bytes 262144 | tf_op jit(solution)/shard_map/all_to_all | solution.py:334
  75.1 0.8 %shard_map.125 = (f32[16,128]{1,0:T(8,128)}, f32[1,128]{1,0:T(1,128)S(1)}) custom-call(f32[256,128]{1,0:T(8,128)S(1)} %bitcast.8, f32[8,256]{1,0:T(8,128)S(1)} %get-tuple-element.77.image, f32[8,2048]{1,0:T(8,128)S(1)} %get-tuple-element.75.rest_8_.basis), custom_call_target="tpu_custom_call" | custom-call | tf_op jit(solution)/shard_map/pallas_call | solution.py:336
  75.9 0.5 slice_bitcast_fusion
  (5 shorter events, 0.0 us)
Async XLA Ops:
  2.0 7.8 %collective-permute-start = (bf16[8,512]{1,0:T(8,128)(2,1)S(1)}, bf16[8,512]{1,0:T(8,128)(2,1)S(1)}, u32[]{:S(2)}, u32[]{:S(2)}) collective-permute-start(bf16[8,512]{1,0:T(8,128)(2,1)S(1)} %get-tuple-element.43.own), channel_id=1, source_target_pairs={{0,1},{1,0},{2,3},{3,2},{4,5},{5,4},{6,7},{7,6},{8,9},{9,8},{10,11... | collective-permute-start | bytes 24584 | tf_op jit(solution)/shard_map/ppermute | solution.py:299
  5.3 4.5 %collective-permute-start.1 = (bf16[8,512]{1,0:T(8,128)(2,1)S(1)}, bf16[8,512]{1,0:T(8,128)(2,1)S(1)}, u32[]{:S(2)}, u32[]{:S(2)}) collective-permute-start(bf16[8,512]{1,0:T(8,128)(2,1)S(1)} %get-tuple-element.43.own), channel_id=1, source_target_pairs={{0,255},{1,2},{2,1},{3,4},{4,3},{5,6},{6,5},{7,8},{8,7},{9,10},{10... | collective-permute-start | bytes 24584 | tf_op jit(solution)/shard_map/ppermute | solution.py:298
  11.6 9.8 %collective-permute-start.2 = (bf16[8,512]{1,0:T(8,128)(2,1)S(1)}, bf16[8,512]{1,0:T(8,128)(2,1)S(1)}, u32[]{:S(2)}, u32[]{:S(2)}) collective-permute-start(bf16[8,512]{1,0:T(8,128)(2,1)S(1)} %get-tuple-element.57.own), channel_id=1, source_target_pairs={{0,1},{1,0},{2,3},{3,2},{4,5},{5,4},{6,7},{7,6},{8,9},{9,8},{10,11... | collective-permute-start | bytes 24584 | tf_op jit(solution)/shard_map/ppermute | solution.py:328
  20.5 3.1 %collective-permute-start.3 = (bf16[8,512]{1,0:T(8,128)(2,1)S(1)}, bf16[8,512]{1,0:T(8,128)(2,1)S(1)}, u32[]{:S(2)}, u32[]{:S(2)}) collective-permute-start(bf16[8,512]{1,0:T(8,128)(2,1)S(1)} %get-tuple-element.57.own), channel_id=1, source_target_pairs={{0,255},{1,2},{2,1},{3,4},{4,3},{5,6},{6,5},{7,8},{8,7},{9,10},{10... | collective-permute-start | bytes 24584 | tf_op jit(solution)/shard_map/ppermute | solution.py:327
  25.3 4.6 %collective-permute-start.4 = (bf16[8,512]{1,0:T(8,128)(2,1)S(1)}, bf16[8,512]{1,0:T(8,128)(2,1)S(1)}, u32[]{:S(2)}, u32[]{:S(2)}) collective-permute-start(bf16[8,512]{1,0:T(8,128)(2,1)S(1)} %get-tuple-element.63.own), channel_id=1, source_target_pairs={{0,1},{1,0},{2,3},{3,2},{4,5},{5,4},{6,7},{7,6},{8,9},{9,8},{10,11... | collective-permute-start | bytes 24584 | tf_op jit(solution)/shard_map/ppermute | solution.py:328
  29.1 3.1 %collective-permute-start.5 = (bf16[8,512]{1,0:T(8,128)(2,1)S(1)}, bf16[8,512]{1,0:T(8,128)(2,1)S(1)}, u32[]{:S(2)}, u32[]{:S(2)}) collective-permute-start(bf16[8,512]{1,0:T(8,128)(2,1)S(1)} %get-tuple-element.63.own), channel_id=1, source_target_pairs={{0,255},{1,2},{2,1},{3,4},{4,3},{5,6},{6,5},{7,8},{8,7},{9,10},{10... | collective-permute-start | bytes 24584 | tf_op jit(solution)/shard_map/ppermute | solution.py:327
  33.9 4.5 %collective-permute-start.6 = (bf16[8,512]{1,0:T(8,128)(2,1)S(1)}, bf16[8,512]{1,0:T(8,128)(2,1)S(1)}, u32[]{:S(2)}, u32[]{:S(2)}) collective-permute-start(bf16[8,512]{1,0:T(8,128)(2,1)S(1)} %get-tuple-element.69.own), channel_id=1, source_target_pairs={{0,1},{1,0},{2,3},{3,2},{4,5},{5,4},{6,7},{7,6},{8,9},{9,8},{10,11... | collective-permute-start | bytes 24584 | tf_op jit(solution)/shard_map/ppermute | solution.py:328
  37.6 3.1 %collective-permute-start.7 = (bf16[8,512]{1,0:T(8,128)(2,1)S(1)}, bf16[8,512]{1,0:T(8,128)(2,1)S(1)}, u32[]{:S(2)}, u32[]{:S(2)}) collective-permute-start(bf16[8,512]{1,0:T(8,128)(2,1)S(1)} %get-tuple-element.69.own), channel_id=1, source_target_pairs={{0,255},{1,2},{2,1},{3,4},{4,3},{5,6},{6,5},{7,8},{8,7},{9,10},{10... | collective-permute-start | bytes 24584 | tf_op jit(solution)/shard_map/ppermute | solution.py:327
  43.1 4.5 %collective-permute-start.8 = (bf16[8,512]{1,0:T(8,128)(2,1)S(1)}, bf16[8,512]{1,0:T(8,128)(2,1)S(1)}, u32[]{:S(2)}, u32[]{:S(2)}) collective-permute-start(bf16[8,512]{1,0:T(8,128)(2,1)S(1)} %get-tuple-element.74.own), channel_id=1, source_target_pairs={{0,1},{1,0},{2,3},{3,2},{4,5},{5,4},{6,7},{7,6},{8,9},{9,8},{10,11... | collective-permute-start | bytes 24584 | tf_op jit(solution)/shard_map/ppermute | solution.py:328
  46.7 3.1 %collective-permute-start.9 = (bf16[8,512]{1,0:T(8,128)(2,1)S(1)}, bf16[8,512]{1,0:T(8,128)(2,1)S(1)}, u32[]{:S(2)}, u32[]{:S(2)}) collective-permute-start(bf16[8,512]{1,0:T(8,128)(2,1)S(1)} %get-tuple-element.74.own), channel_id=1, source_target_pairs={{0,255},{1,2},{2,1},{3,4},{4,3},{5,6},{6,5},{7,8},{8,7},{9,10},{10... | collective-permute-start | bytes 24584 | tf_op jit(solution)/shard_map/ppermute | solution.py:327

commit v5 on v4

--- a/solution.py
+++ b/solution.py
@@ -16,6 +16,7 @@
 PANEL, RANK, PRANK, WIDTH = 256, 64, 128, 512
 T_AT, C_AT = PANEL, PANEL + PRANK
 SOURCES = 32
+SLOTS = 18
 
 
 def dot(a, b):
@@ -51,26 +52,41 @@
     return jnp.concatenate([value[at : at + rows] for at in range(0, value.shape[0], rows)], axis=1)
 
 
-def apply_rows(field, own, mate, far, pick_near, pick_far, pick_top, near, leaf_basis, coupling, transfer, top):
-    leaves = field.shape[0]
-    rest = jnp.zeros((SOURCES - 3 * leaves, WIDTH), F32)
-    window = jnp.concatenate(
-        [own[...].astype(F32), mate[...].astype(F32), far[...].astype(F32), rest], axis=0
-    ).astype(BF16)
+def window_of(*stacks):
+    rest = jnp.zeros((SOURCES - sum(part.shape[0] for part in stacks), WIDTH), F32)
+    return jnp.concatenate([part.astype(F32) for part in stacks] + [rest], axis=0).astype(BF16)
+
+
+def far_sums(window, pick_far, pick_top, coupling, top):
+    leaves = pick_far.shape[0] // (coupling.shape[0] // RANK)
     parents = tiles(dot(pick_top[...], window[:, T_AT:C_AT]), leaves).astype(BF16)
     coeffs = tiles(dot(pick_far[...], window[:, C_AT : C_AT + RANK]), leaves).astype(BF16)
+    tops = diagonal(dot(parents, top[...]), PRANK)
+    tops = sum(tops[:, at : at + PRANK] for at in range(0, tops.shape[1], PRANK))
+    return tops, diagonal(dot(coeffs, coupling[...]), RANK)
+
+
+def far_rows(tops, local, leaf_basis, transfer):
+    local = local + diagonal(dot_nt(tops.astype(BF16), transfer), 2 * RANK)
+    return dot(diagonal(flat(local), RANK).astype(BF16), leaf_basis)
+
+
+def near_rows(window, pick_near, near):
+    leaves = near.shape[0]
     panels = dot(pick_near[...], window[:, :PANEL]).astype(BF16)
-    tops = diagonal(dot(parents, top[...]), PRANK)
-    tops = sum(tops[:, at : at + PRANK] for at in range(0, tops.shape[1], PRANK)).astype(BF16)
-    local = diagonal(dot(coeffs, coupling[...]), RANK) + diagonal(dot_nt(tops, transfer), 2 * RANK)
-    total = dot(diagonal(flat(local), RANK).astype(BF16), leaf_basis)
+    total = jnp.zeros((leaves, PANEL), F32)
     row = lax.broadcasted_iota(jnp.int32, total.shape, 0)
     for i in range(leaves):
         image = jnp.zeros(total.shape, F32)
         for k in range(near.shape[1]):
             image += dot(panels[k * leaves : (k + 1) * leaves], near[i, k])
         total += jnp.where(row == i, image, jnp.zeros_like(image))
-    return 0.5 * field + total
+    return total
+
+
+def slot_rows(window, pick_slots, slots, leaves):
+    panels = tiles(dot(pick_slots[...], window[:, :PANEL]), leaves).astype(BF16)
+    return dot(panels, slots[:SLOTS].reshape(SLOTS * PANEL, PANEL))
 
 
 def stacked(ref):
@@ -94,22 +110,29 @@
     write_stack(product[...], stacked(leaf_basis_in), stacked(transfer_in), stack)
 
 
+def identity(size):
+    row = lax.broadcasted_iota(jnp.int32, (size, size), 0)
+    return jnp.where(row == lax.broadcasted_iota(jnp.int32, (size, size), 1), 1.0, 0.0).astype(BF16)
+
+
 def prepare_kernel(
     _, roots, near, near_ids, coupling, far_ids, top, top_ids,
-    scales, near_out, coupling_out, top_out, pick_near, pick_far, pick_top,
-    roots_in, near_in, coupling_in, top_in, near_ids_in, far_ids_in, top_ids_in, sems,
+    scales, crowded, near_out, slots, coupling_out, top_out, pick_slots, pick_near, pick_far, pick_top,
+    roots_in, near_in, coupling_in, top_in, near_ids_in, far_ids_in, top_ids_in, near_ids_at, hot_rows, sems,
 ):
     leaves = near.shape[0]
     pairs = [
         (roots, roots_in), (near_ids, near_ids_in), (far_ids, far_ids_in), (top_ids, top_ids_in),
-        (coupling, coupling_in), (top, top_in),
+        (near_ids, near_ids_at), (coupling, coupling_in), (top, top_in),
     ] + [(near.at[i], near_in.at[i]) for i in range(leaves)]
     copies = [
         pltpu.make_async_copy(source, target, sems.at[n]) for n, (source, target) in enumerate(pairs)
     ]
     for copy in copies:
         copy.start()
-    for copy in copies[:4]:
+    hot_rows[...] = jnp.zeros_like(hot_rows)
+    slots[...] = jnp.zeros_like(slots)
+    for copy in copies[:5]:
         copy.wait()
     for k in range(roots.shape[1]):
         scales[k * leaves : (k + 1) * leaves, :] = jnp.broadcast_to(
@@ -129,20 +152,34 @@
             if rows < leaves:
                 hot = jnp.concatenate([hot, jnp.zeros((leaves - rows, SOURCES), F32)], axis=0)
             pick[k * leaves : (k + 1) * leaves, :] = hot.astype(BF16)
-    copies[4].wait()
-    for i in range(leaves):
-        for k in range(coupling.shape[1]):
-            rows, lanes = slice(k * RANK, (k + 1) * RANK), slice(i * RANK, (i + 1) * RANK)
-            coupling_out[rows, lanes] = coupling_in[i, k].T
     copies[5].wait()
+    for k in range(coupling.shape[1]):
+        rows = jnp.concatenate([coupling_in[i, k] for i in range(leaves)], axis=0)
+        coupling_out[k * RANK : (k + 1) * RANK, :] = rows.T
+    copies[6].wait()
     for p in range(top.shape[0]):
         for k in range(top.shape[1]):
             rows, lanes = slice(k * PRANK, (k + 1) * PRANK), slice(p * PRANK, (p + 1) * PRANK)
             top_out[rows, lanes] = top_in[p, k].T
+    unit = identity(PANEL)
+    lane = lax.broadcasted_iota(jnp.int32, (1, hot_rows.shape[1]), 1)
+    count = jnp.int32(0)
     for i in range(leaves):
-        copies[6 + i].wait()
+        copies[7 + i].wait()
         for k in range(near.shape[1]):
-            near_out[i, k] = near_in[i, k].T
+            block = dot_nt(unit, near_in[i, k]).astype(BF16) if k % 2 else near_in[i, k].T
+            near_out[i, k] = block
+            if k == 0:
+                continue
+            away = near_ids_at[i, k] - place * leaves
+            outside = jnp.where(odd, away >= leaves, away < 0)
+            slot = jnp.where(jnp.logical_and(outside, count < SLOTS), count, SLOTS)
+            slots[slot] = block
+            source = jnp.where(odd, away + leaves, away + 3 * leaves)
+            hot_rows[pl.ds(slot * leaves + i, 1), :] = jnp.where(lane == source, 1.0, 0.0)
+            count += outside.astype(jnp.int32)
+    pick_slots[...] = hot_rows[: SLOTS * leaves, :SOURCES].astype(BF16)
+    crowded[...] = jnp.full(crowded.shape, jnp.maximum(count - SLOTS, 0), jnp.int32)
 
 
 def at_an_end():
@@ -164,59 +201,98 @@
     write_stack(total if last else after, leaf_basis, transfer, stack)
 
 
-def step_kernel(
-    step, last, early, scales, product, partial, own, mate, far, picks, matrices, outs, ready=()
-):
+def early_sums(field, own, mate, picks, matrices, sums):
+    near, _, coupling, _, top = matrices
+    window = window_of(own[...], mate[...])
+    tops, local = far_sums(window, *picks[1:], coupling, top)
+    base = 0.5 * field + near_rows(window, picks[0], near)
+    for target, value in zip(sums, (tops, local, base)):
+        target[...] = value
+    return tops, local, base
+
+
+def whole_image(field, own, mate, far, picks, matrices):
     near, leaf_basis, coupling, transfer, top = matrices
-
-    @pl.when(at_an_end() if early else jnp.logical_not(at_an_end()))
-    def _():
-        basis_rows, transfer_rows = stacked(leaf_basis), stacked(transfer)
-        field = product[...]
-        image = apply_rows(
-            field, own, mate, far, *picks, near, basis_rows, coupling, transfer_rows, top
-        )
-        advance(step, last, image, field, scales, partial, basis_rows, transfer_rows, *outs)
-
-    if not early:
-
-        @pl.when(at_an_end())
-        def _():
-            for source, target in zip(ready, outs):
-                target[...] = source[...]
+    window = window_of(own[...], mate[...], far[...])
+    tops, local = far_sums(window, *picks[1:], coupling, top)
+    rows = far_rows(tops, local, stacked(leaf_basis), stacked(transfer))
+    return 0.5 * field + near_rows(window, picks[0], near) + rows
+
+
+def late_image(far, sums, pick_slots, slots, picks, matrices):
+    _, leaf_basis, coupling, transfer, top = matrices
+    leaves = far.shape[0]
+    nothing = jnp.zeros((2 * leaves, WIDTH), F32)
+    window = window_of(nothing, far[...])
+    tops, local = far_sums(window, *picks[1:], coupling, top)
+    rows = far_rows(tops + sums[0][...], local + sums[1][...], stacked(leaf_basis), stacked(transfer))
+    return sums[2][...] + slot_rows(window, pick_slots, slots, leaves) + rows
+
+
+def late_paths(crowded, late, whole, ready):
+    many = jnp.max(crowded[...]) > 0
+    end = at_an_end()
+    inner = jnp.logical_not(end)
+    pl.when(jnp.logical_and(inner, jnp.logical_not(many)))(late)
+    pl.when(jnp.logical_and(inner, many))(whole)
+    pl.when(end)(ready)
 
 
 def step_early(step, last, scales, product, partial, own, mate, *rest):
-    step_kernel(step, last, True, scales, product, partial, own, mate, own, rest[:3], rest[3:8], rest[8:])
-
-
-def step_late(step, last, scales, product, partial, own, mate, far, *rest):
-    picks, matrices, ready, outs = rest[:3], rest[3:8], rest[8:11], rest[11:]
-    step_kernel(step, last, False, scales, product, partial, own, mate, far, picks, matrices, outs, ready)
-
-
-def last_image(early, field, own, mate, far, picks, matrices, image_out):
-    near, leaf_basis, coupling, transfer, top = matrices
-
-    @pl.when(at_an_end() if early else jnp.logical_not(at_an_end()))
-    def _():
-        image_out[...] = apply_rows(
-            field[...], own, mate, far, *picks, near, stacked(leaf_basis), coupling, stacked(transfer), top
-        )
-
-
-def last_early(field, own, mate, *rest):
-    last_image(True, field, own, mate, own, rest[:3], rest[3:8], rest[8])
-
-
-def last_late(field, own, mate, far, *rest):
-    picks, matrices, (basis, ready, image_out, sums) = rest[:3], rest[3:8], rest[8:]
-    last_image(False, field, own, mate, far, picks, matrices, image_out)
+    picks, matrices, sums, outs = rest[:3], rest[3:8], rest[8:11], rest[11:]
+    field = product[...]
+    tops, local, base = early_sums(field, own, mate, picks, matrices, sums)
 
     @pl.when(at_an_end())
     def _():
+        leaf_basis, transfer = stacked(matrices[1]), stacked(matrices[3])
+        image = base + far_rows(tops, local, leaf_basis, transfer)
+        advance(step, last, image, field, scales, partial, leaf_basis, transfer, *outs)
+
+
+def step_late(step, last, scales, product, partial, own, mate, far, crowded, pick_slots, slots, *rest):
+    picks, matrices, sums, ready, outs = rest[:3], rest[3:8], rest[8:11], rest[11:14], rest[14:]
+
+    def go_on(image):
+        leaf_basis, transfer = stacked(matrices[1]), stacked(matrices[3])
+        advance(step, last, image, product[...], scales, partial, leaf_basis, transfer, *outs)
+
+    def late():
+        go_on(late_image(far, sums, pick_slots, slots, picks, matrices))
+
+    def whole():
+        go_on(whole_image(product[...], own, mate, far, picks, matrices))
+
+    def copy():
+        for source, target in zip(ready, outs):
+            target[...] = source[...]
+
+    late_paths(crowded, late, whole, copy)
+
+
+def last_early(field, own, mate, *rest):
+    picks, matrices, sums, image_out = rest[:3], rest[3:8], rest[8:11], rest[11]
+    tops, local, base = early_sums(field[...], own, mate, picks, matrices, sums)
+
+    @pl.when(at_an_end())
+    def _():
+        image_out[...] = base + far_rows(tops, local, stacked(matrices[1]), stacked(matrices[3]))
+
+
+def last_late(field, own, mate, far, crowded, pick_slots, slots, *rest):
+    picks, matrices, early = rest[:3], rest[3:8], rest[8:11]
+    ready, basis, image_out, sums = rest[11:]
+
+    def late():
+        image_out[...] = late_image(far, early, pick_slots, slots, picks, matrices)
+
+    def whole():
+        image_out[...] = whole_image(field[...], own, mate, far, picks, matrices)
+
+    def copy():
         image_out[...] = ready[...]
 
+    late_paths(crowded, late, whole, copy)
     image = image_out[...]
     count, leaves = basis.shape[0], image.shape[0]
     lane = lax.broadcasted_iota(jnp.int32, (count, 128), 1)
@@ -298,38 +374,44 @@
     far = lax.ppermute(stack, AXES, others)
     mate = lax.ppermute(stack, AXES, mates)
     roots = roots.reshape(1, -1)
-    scales, near, coupling, top, *picks = call(
+    scales, crowded, near, slots, coupling, top, pick_slots, *picks = call(
         prepare_kernel,
         [VMEM] + [HBM] * 7,
         [
             ((roots.shape[1] * leaves, PANEL), F32),
+            ((1, 128), jnp.int32),
             (near_blocks.shape, BF16),
+            ((SLOTS + 1, PANEL, PANEL), BF16),
             ((fars * RANK, leaves * RANK), BF16),
             ((tops * PRANK, parents * PRANK), BF16),
+            ((SLOTS * leaves, SOURCES), BF16),
             ((nears * leaves, SOURCES), BF16),
             ((fars * leaves, SOURCES), BF16),
             ((tops * leaves, SOURCES), BF16),
         ],
         [like(a) for a in (roots, near_blocks, far_coupling, top_coupling, near_ids, far_ids, top_ids)]
-        + [pltpu.SemaphoreType.DMA((6 + leaves,))],
+        + [pltpu.SMEM(near_ids.shape, near_ids.dtype), pltpu.VMEM(((SLOTS + 1) * leaves, 128), F32)]
+        + [pltpu.SemaphoreType.DMA((7 + leaves,))],
     )(product, *pinned(roots, near_blocks, near_ids, far_coupling, far_ids, top_coupling, top_ids))
     matrices = (*picks, near, leaf_basis, coupling, transfer, top)
     partial = product
     steps = roots.shape[1] - 1
     outs = [((leaves, PANEL), F32), ((leaves, PANEL), F32), ((leaves, WIDTH), BF16)]
+    early = [((leaves, PRANK), F32), ((leaves, leaves * RANK), F32), ((leaves, PANEL), F32)]
+    packed = (crowded, pick_slots, slots)
     for step in range(steps):
         last = step == steps - 1
         state = (scales, product, partial, stack, mate)
-        ready = call(functools.partial(step_early, step, last), [VMEM] * 13, outs)(*state, *matrices)
-        product, partial, stack = call(functools.partial(step_late, step, last), [VMEM] * 17, outs)(
-            *state, far, *matrices, *ready
+        ready = call(functools.partial(step_early, step, last), [VMEM] * 13, early + outs)(*state, *matrices)
+        product, partial, stack = call(functools.partial(step_late, step, last), [VMEM] * 23, outs)(
+            *state, far, *packed, *matrices, *ready
         )
         far = lax.ppermute(stack, AXES, others)
         mate = lax.ppermute(stack, AXES, mates)
     state = (partial, stack, mate)
-    ready = call(last_early, [VMEM] * 11, outs[:1])(*state, *matrices)
-    image, sums = call(last_late, [VMEM] * 14, [outs[0], ((devices, 128), F32)])(
-        *state, far, *matrices, basis, *ready
+    ready = call(last_early, [VMEM] * 11, early + outs[:1])(*state, *matrices)
+    image, sums = call(last_late, [VMEM] * 20, [outs[0], ((devices, 128), F32)])(
+        *state, far, *packed, *matrices, *ready, basis
     )
     sums = lax.all_to_all(sums.reshape(devices, 1, 128), AXES, 0, 0, tiled=True)
     size = float(leaves * PANEL * devices)

time: 76.6 us -> 77.6 us (1.013)
  Pallas kernels: 15.8 us -> 23.6 us
  waiting for transfers between devices: 12.3 us -> 7.07 us
  blocking collectives: 23.7 us -> 22.7 us
    pallas_call x10, Pallas kernels: 9.24 us -> 16.6 us  [the longest x4 8.28 us: body(): call(functools.partial(step_late, step, last), [VMEM] * 23, outs)]
    ppermute x5, waiting for transfers between devices: 8.99 us -> 3.77 us  [body(): far = lax.ppermute(stack, AXES, others)]
    all_to_all x1, blocking collectives: 23.7 us -> 22.7 us  [body(): sums = lax.all_to_all(sums.reshape(devices, 1, 128), AXES, 0, 0, tiled=True)]
  transfers between devices with their start and end apart: 10 -> 10, of which waited for: 8 -> 8; matrix products, arithmetic and copies ran while one was open for 0% -> 0% of each run, Pallas kernels for 6% -> 15%
where the time goes in v5:
time: 77.6 us; the launch traced here: 77.5 us
  Pallas kernels  23.6 us (30%)
  starting transfers between devices  23 us (30%)
  blocking collectives  22.7 us (29%)
  waiting for transfers between devices  7.07 us (9%)
    ppermute x5, starting transfers between devices, body(): mate = lax.ppermute(stack, AXES, mates)  22.9 us
    all_to_all x1, blocking collectives, body(): sums = lax.all_to_all(sums.reshape(devices, 1, 128), AXES, 0, 0, tiled=True)  22.7 us
    pallas_call x4, Pallas kernels, body(): call(functools.partial(step_late, step, last), [VMEM] * 23, outs)  8.28 us
    pallas_call x4, Pallas kernels, body(): call(functools.partial(step_early, step, last), [VMEM] * 13, early + outs)  5.23 us
    pallas_call x1, Pallas kernels, body(): call(prepare_kernel, [VMEM] + [HBM] * 7, [((roots.shape[1] * leaves, PANE...  4.79 us
    ppermute x5, waiting for transfers between devices, body(): far = lax.ppermute(stack, AXES, others)  3.77 us
    ppermute x5, waiting for transfers between devices, body(): mate = lax.ppermute(stack, AXES, mates)  3.3 us
    pallas_call x1, Pallas kernels, body(): call(last_late, [VMEM] * 20, [outs[0], ((devices, 128), F32)])  1.8 us
  transfers between devices with their start and end apart: 10, of which 8 were waited for; matrix products, arithmetic and copies ran while one was open for 0% of the time, Pallas kernels for 15%

profile of v5, /device:TPU:1, one launch (start us, length us, event | category | flops | bytes accessed | tf_op | source)
XLA Modules:
  0.0 77.5 jit_solution(6777997101898897167)
XLA Ops:
  0.6 1.4 %shard_map.113 = (f32[8,256]{1,0:T(8,128)S(1)}, bf16[8,512]{1,0:T(8,128)(2,1)S(1)}, f32[8,2048]{1,0:T(8,128)S(1)}, bf16[8,64,256]{2,1,0:T(8,128)(2,1)S(1)}, bf16[8,64,128]{2,1,0:T(8,128)(2,1)S(1)}) custom-call(f32[8,2048]{1,0:T(8,128)} %basis.1, bf16[8,64,256]{2,1,0:T(8,128)(2,1)} %leaf_basis.1, bf16[8,64,128]{2,1,0:T(8,128)(2,1)} %transfer.1), custom_call_target="tpu_custom_call" | custom-call | tf_op jit(solution)/shard_map/pallas_call | solution.py:368
  2.0 3.3 %collective-permute-start = (bf16[8,512]{1,0:T(8,128)(2,1)S(1)}, bf16[8,512]{1,0:T(8,128)(2,1)S(1)}, u32[]{:S(2)}, u32[]{:S(2)}) collective-permute-start(bf16[8,512]{1,0:T(8,128)(2,1)S(1)} %get-tuple-element.62.own), channel_id=1, source_target_pairs={{0,1},{1,0},{2,3},{3,2},{4,5},{5,4},{6,7},{7,6},{8,9},{9,8},{10,11... | collective-permute-start | bytes 24584 | tf_op jit(solution)/shard_map/ppermute | solution.py:375
  5.3 0.0 collective-permute-start.1
  5.3 4.8 %shard_map.114 = (f32[40,256]{1,0:T(8,128)S(1)}, s32[1,128]{1,0:T(1,128)S(1)}, bf16[8,6,256,256]{3,2,1,0:T(8,128)(2,1)S(1)}, bf16[19,256,256]{2,1,0:T(8,128)(2,1...) custom-call(f32[8,256]{1,0:T(8,128)S(1)} %get-tuple-element.60._.pro, ...), custom_call_target="tpu_custom_call" | custom-call | tf_op jit(solution)/shard_map/pallas_call | solution.py:377
  10.1 0.0 collective-permute-done.mate
  10.1 1.3 %shard_map.115 = (f32[8,128]{1,0:T(8,128)S(1)}, f32[8,512]{1,0:T(8,128)S(1)}, f32[8,256]{1,0:T(8,128)S(1)}, f32[8,256]{1,0:T(8,128)S(1)}, f32[8,256]{1,0:T(8,128)S(1)}, /*index=5*/bf16[8,512]{1,0:T(8,128)(2,1)S(1)}) custom-call(f32[40,256]{1,0:T(8,128)S(1)} %get-tuple-element.61.scales, f32[8,256]{1,0:T(8,128)S(1)} %get-tuple-element.60._.product.partial, ...), custom_call_target="tpu_custom_call" | custom-call | tf_op jit(solution)/shard_map/pallas_call | solution.py:405
  11.5 0.0 collective-permute-done.1.far
  11.5 1.9 %shard_map.116 = (f32[8,256]{1,0:T(8,128)S(1)}, f32[8,256]{1,0:T(8,128)S(1)}, bf16[8,512]{1,0:T(8,128)(2,1)S(1)}) custom-call(f32[40,256]{1,0:T(8,128)S(1)} %get-tuple-element.61.scales, f32[8,256]{1,0:T(8,128)S(1)} %get-tuple-element.60._.product.partial, f32[8,256]{1,0:T(8,128)S(1)} %get-tuple-element.60._.product.partial, ...), custom_call_target="tpu_custom_call" | custom-call | tf_op jit(solution)/shard_map/pallas_call | solution.py:406
  13.4 7.8 %collective-permute-start.2 = (bf16[8,512]{1,0:T(8,128)(2,1)S(1)}, bf16[8,512]{1,0:T(8,128)(2,1)S(1)}, u32[]{:S(2)}, u32[]{:S(2)}) collective-permute-start(bf16[8,512]{1,0:T(8,128)(2,1)S(1)} %get-tuple-element.82.own), channel_id=1, source_target_pairs={{0,1},{1,0},{2,3},{3,2},{4,5},{5,4},{6,7},{7,6},{8,9},{9,8},{10,11... | collective-permute-start | bytes 24584 | tf_op jit(solution)/shard_map/ppermute | solution.py:410
  21.2 0.0 collective-permute-start.3
  21.2 0.8 %collective-permute-done.2.mate = bf16[8,512]{1,0:T(8,128)(2,1)S(1)} collective-permute-done((bf16[8,512]{1,0:T(8,128)(2,1)S(1)}, bf16[8,512]{1,0:T(8,128)(2,1)S(1)}, u32[]{:S(2)}, u32[]{:S(2)}) %collective-permute-start.2) | collective-permute-done | bytes 8224 | tf_op jit(solution)/shard_map/ppermute | solution.py:410
  22.0 1.3 %shard_map.117 = (f32[8,128]{1,0:T(8,128)S(1)}, f32[8,512]{1,0:T(8,128)S(1)}, f32[8,256]{1,0:T(8,128)S(1)}, f32[8,256]{1,0:T(8,128)S(1)}, f32[8,256]{1,0:T(8,128)S(1)}, /*index=5*/bf16[8,512]{1,0:T(8,128)(2,1)S(1)}) custom-call(f32[40,256]{1,0:T(8,128)S(1)} %get-tuple-element.61.scales, f32[8,256]{1,0:T(8,128)S(1)} %get-tuple-element.80.product, ...), custom_call_target="tpu_custom_call" | custom-call | tf_op jit(solution)/shard_map/pallas_call | solution.py:405
  23.3 0.9 %collective-permute-done.3.far = bf16[8,512]{1,0:T(8,128)(2,1)S(1)} collective-permute-done((bf16[8,512]{1,0:T(8,128)(2,1)S(1)}, bf16[8,512]{1,0:T(8,128)(2,1)S(1)}, u32[]{:S(2)}, u32[]{:S(2)}) %collective-permute-start.3) | collective-permute-done | bytes 8224 | tf_op jit(solution)/shard_map/ppermute | solution.py:409
  24.2 1.9 %shard_map.118 = (f32[8,256]{1,0:T(8,128)S(1)}, f32[8,256]{1,0:T(8,128)S(1)}, bf16[8,512]{1,0:T(8,128)(2,1)S(1)}) custom-call(f32[40,256]{1,0:T(8,128)S(1)} %get-tuple-element.61.scales, f32[8,256]{1,0:T(8,128)S(1)} %get-tuple-element.80.product, f32[8,256]{1,0:T(8,128)S(1)} %get-tuple-element.81.partial, bf16[8,512]{1,0:T(8,128)(2,1)S(1)} %get-tuple-element.82.own, ...), custom_call_target="tpu_custom_call" | custom-call | tf_op jit(solution)/shard_map/pallas_call | solution.py:406
  26.2 3.9 %collective-permute-start.4 = (bf16[8,512]{1,0:T(8,128)(2,1)S(1)}, bf16[8,512]{1,0:T(8,128)(2,1)S(1)}, u32[]{:S(2)}, u32[]{:S(2)}) collective-permute-start(bf16[8,512]{1,0:T(8,128)(2,1)S(1)} %get-tuple-element.91.own), channel_id=1, source_target_pairs={{0,1},{1,0},{2,3},{3,2},{4,5},{5,4},{6,7},{7,6},{8,9},{9,8},{10,11... | collective-permute-start | bytes 24584 | tf_op jit(solution)/shard_map/ppermute | solution.py:410
  30.1 0.0 collective-permute-start.5
  30.1 0.8 %collective-permute-done.4.mate = bf16[8,512]{1,0:T(8,128)(2,1)S(1)} collective-permute-done((bf16[8,512]{1,0:T(8,128)(2,1)S(1)}, bf16[8,512]{1,0:T(8,128)(2,1)S(1)}, u32[]{:S(2)}, u32[]{:S(2)}) %collective-permute-start.4) | collective-permute-done | bytes 8224 | tf_op jit(solution)/shard_map/ppermute | solution.py:410
  30.9 1.3 %shard_map.119 = (f32[8,128]{1,0:T(8,128)S(1)}, f32[8,512]{1,0:T(8,128)S(1)}, f32[8,256]{1,0:T(8,128)S(1)}, f32[8,256]{1,0:T(8,128)S(1)}, f32[8,256]{1,0:T(8,128)S(1)}, /*index=5*/bf16[8,512]{1,0:T(8,128)(2,1)S(1)}) custom-call(f32[40,256]{1,0:T(8,128)S(1)} %get-tuple-element.61.scales, f32[8,256]{1,0:T(8,128)S(1)} %get-tuple-element.89.product, ...), custom_call_target="tpu_custom_call" | custom-call | tf_op jit(solution)/shard_map/pallas_call | solution.py:405
  32.2 0.9 %collective-permute-done.5.far = bf16[8,512]{1,0:T(8,128)(2,1)S(1)} collective-permute-done((bf16[8,512]{1,0:T(8,128)(2,1)S(1)}, bf16[8,512]{1,0:T(8,128)(2,1)S(1)}, u32[]{:S(2)}, u32[]{:S(2)}) %collective-permute-start.5) | collective-permute-done | bytes 8224 | tf_op jit(solution)/shard_map/ppermute | solution.py:409
  33.2 1.9 %shard_map.120 = (f32[8,256]{1,0:T(8,128)S(1)}, f32[8,256]{1,0:T(8,128)S(1)}, bf16[8,512]{1,0:T(8,128)(2,1)S(1)}) custom-call(f32[40,256]{1,0:T(8,128)S(1)} %get-tuple-element.61.scales, f32[8,256]{1,0:T(8,128)S(1)} %get-tuple-element.89.product, f32[8,256]{1,0:T(8,128)S(1)} %get-tuple-element.90.partial, bf16[8,512]{1,0:T(8,128)(2,1)S(1)} %get-tuple-element.91.own, ...), custom_call_target="tpu_custom_call" | custom-call | tf_op jit(solution)/shard_map/pallas_call | solution.py:406
  35.1 4.1 %collective-permute-start.6 = (bf16[8,512]{1,0:T(8,128)(2,1)S(1)}, bf16[8,512]{1,0:T(8,128)(2,1)S(1)}, u32[]{:S(2)}, u32[]{:S(2)}) collective-permute-start(bf16[8,512]{1,0:T(8,128)(2,1)S(1)} %get-tuple-element.100.own), channel_id=1, source_target_pairs={{0,1},{1,0},{2,3},{3,2},{4,5},{5,4},{6,7},{7,6},{8,9},{9,8},{10,11... | collective-permute-start | bytes 24584 | tf_op jit(solution)/shard_map/ppermute | solution.py:410
  39.2 0.0 collective-permute-start.7
  39.2 0.8 %collective-permute-done.6.mate = bf16[8,512]{1,0:T(8,128)(2,1)S(1)} collective-permute-done((bf16[8,512]{1,0:T(8,128)(2,1)S(1)}, bf16[8,512]{1,0:T(8,128)(2,1)S(1)}, u32[]{:S(2)}, u32[]{:S(2)}) %collective-permute-start.6) | collective-permute-done | bytes 8224 | tf_op jit(solution)/shard_map/ppermute | solution.py:410
  40.0 1.3 %shard_map.121 = (f32[8,128]{1,0:T(8,128)S(1)}, f32[8,512]{1,0:T(8,128)S(1)}, f32[8,256]{1,0:T(8,128)S(1)}, f32[8,256]{1,0:T(8,128)S(1)}, f32[8,256]{1,0:T(8,128)S(1)}, /*index=5*/bf16[8,512]{1,0:T(8,128)(2,1)S(1)}) custom-call(f32[40,256]{1,0:T(8,128)S(1)} %get-tuple-element.61.scales, f32[8,256]{1,0:T(8,128)S(1)} %get-tuple-element.98.product, ...), custom_call_target="tpu_custom_call" | custom-call | tf_op jit(solution)/shard_map/pallas_call | solution.py:405
  41.3 0.9 %collective-permute-done.7.far = bf16[8,512]{1,0:T(8,128)(2,1)S(1)} collective-permute-done((bf16[8,512]{1,0:T(8,128)(2,1)S(1)}, bf16[8,512]{1,0:T(8,128)(2,1)S(1)}, u32[]{:S(2)}, u32[]{:S(2)}) %collective-permute-start.7) | collective-permute-done | bytes 8224 | tf_op jit(solution)/shard_map/ppermute | solution.py:409
  42.2 2.5 %shard_map.122 = (f32[8,256]{1,0:T(8,128)}, f32[8,256]{1,0:T(8,128)S(1)}, bf16[8,512]{1,0:T(8,128)(2,1)S(1)}) custom-call(f32[40,256]{1,0:T(8,128)S(1)} %get-tuple-element.61.scales, f32[8,256]{1,0:T(8,128)S(1)} %get-tuple-element.98.product, f32[8,256]{1,0:T(8,128)S(1)} %get-tuple-element.99.partial, bf16[8,512]{1,0:T(8,128)(2,1)S(1)} %get-tuple-element.100.own, ...), custom_call_target="tpu_custom_call" | custom-call | tf_op jit(solution)/shard_map/pallas_call | solution.py:406
  44.8 3.8 %collective-permute-start.8 = (bf16[8,512]{1,0:T(8,128)(2,1)S(1)}, bf16[8,512]{1,0:T(8,128)(2,1)S(1)}, u32[]{:S(2)}, u32[]{:S(2)}) collective-permute-start(bf16[8,512]{1,0:T(8,128)(2,1)S(1)} %get-tuple-element.108.own), channel_id=1, source_target_pairs={{0,1},{1,0},{2,3},{3,2},{4,5},{5,4},{6,7},{7,6},{8,9},{9,8},{10,11... | collective-permute-start | bytes 24584 | tf_op jit(solution)/shard_map/ppermute | solution.py:410
  48.6 0.0 collective-permute-start.9
  48.6 0.8 %collective-permute-done.8.mate = bf16[8,512]{1,0:T(8,128)(2,1)S(1)} collective-permute-done((bf16[8,512]{1,0:T(8,128)(2,1)S(1)}, bf16[8,512]{1,0:T(8,128)(2,1)S(1)}, u32[]{:S(2)}, u32[]{:S(2)}) %collective-permute-start.8) | collective-permute-done | bytes 8224 | tf_op jit(solution)/shard_map/ppermute | solution.py:410
  49.4 1.3 %shard_map.123 = (f32[8,128]{1,0:T(8,128)S(1)}, f32[8,512]{1,0:T(8,128)S(1)}, f32[8,256]{1,0:T(8,128)S(1)}, f32[8,256]{1,0:T(8,128)S(1)}) custom-call(f32[8,256]{1,0:T(8,128)S(1)} %get-tuple-element.107.field, bf16[8,512]{1,0:T(8,128)(2,1)S(1)} %get-tuple-element.108.own, bf16[8,512]{1,0:T(8,128)(2,1)S(1)} %collective-permute-done.8.mate, ...), custom_call_target="tpu_custom_call" | custom-call | tf_op jit(solution)/shard_map/pallas_call | solution.py:412
  50.7 0.9 %collective-permute-done.9.far = bf16[8,512]{1,0:T(8,128)(2,1)S(1)} collective-permute-done((bf16[8,512]{1,0:T(8,128)(2,1)S(1)}, bf16[8,512]{1,0:T(8,128)(2,1)S(1)}, u32[]{:S(2)}, u32[]{:S(2)}) %collective-permute-start.9) | collective-permute-done | bytes 8224 | tf_op jit(solution)/shard_map/ppermute | solution.py:409
  51.7 1.8 %shard_map.124 = (f32[8,256]{1,0:T(8,128)S(1)}, f32[256,128]{1,0:T(8,128)S(1)}) custom-call(f32[8,256]{1,0:T(8,128)S(1)} %get-tuple-element.107.field, bf16[8,512]{1,0:T(8,128)(2,1)S(1)} %get-tuple-element.108.own, bf16[8,512]{1,0:T(8,128)(2,1)S(1)} %collective-permute-done.8.mate, bf16[8,512]{1,0:T(8,128)(2,1)S(1)} %collective-permute-done.9.far, ...), custom_call_target="tpu_custom_call" | custom-call | tf_op jit(solution)/shard_map/pallas_call | solution.py:413
  53.5 22.7 %all_to_all.5 = f32[256,1,128]{2,1,0:T(1,128)S(1)} all-to-all(f32[256,1,128]{2,1,0:T(1,128)S(1)} %bitcast.9), channel_id=1, replica_groups=mesh['grp'=4,'leaf'=64] {'grp','leaf'}, dimensions={0} | all-to-all | bytes 262144 | tf_op jit(solution)/shard_map/all_to_all | solution.py:416
  76.2 0.8 %shard_map.125 = (f32[16,128]{1,0:T(8,128)}, f32[1,128]{1,0:T(1,128)S(1)}) custom-call(f32[256,128]{1,0:T(8,128)S(1)} %bitcast.8, f32[8,256]{1,0:T(8,128)S(1)} %get-tuple-element.115.image, f32[8,2048]{1,0:T(8,128)S(1)} %get-tuple-element.113.rest_12_.basis), custom_call_target="tpu_custom_call" | custom-call | tf_op jit(solution)/shard_map/pallas_call | solution.py:418
  77.0 0.5 slice_bitcast_fusion
Async XLA Ops:
  2.0 8.1 %collective-permute-start = (bf16[8,512]{1,0:T(8,128)(2,1)S(1)}, bf16[8,512]{1,0:T(8,128)(2,1)S(1)}, u32[]{:S(2)}, u32[]{:S(2)}) collective-permute-start(bf16[8,512]{1,0:T(8,128)(2,1)S(1)} %get-tuple-element.62.own), channel_id=1, source_target_pairs={{0,1},{1,0},{2,3},{3,2},{4,5},{5,4},{6,7},{7,6},{8,9},{9,8},{10,11... | collective-permute-start | bytes 24584 | tf_op jit(solution)/shard_map/ppermute | solution.py:375
  5.3 6.1 %collective-permute-start.1 = (bf16[8,512]{1,0:T(8,128)(2,1)S(1)}, bf16[8,512]{1,0:T(8,128)(2,1)S(1)}, u32[]{:S(2)}, u32[]{:S(2)}) collective-permute-start(bf16[8,512]{1,0:T(8,128)(2,1)S(1)} %get-tuple-element.62.own), channel_id=1, source_target_pairs={{0,255},{1,2},{2,1},{3,4},{4,3},{5,6},{6,5},{7,8},{8,7},{9,10},{10... | collective-permute-start | bytes 24584 | tf_op jit(solution)/shard_map/ppermute | solution.py:374
  13.4 8.6 %collective-permute-start.2 = (bf16[8,512]{1,0:T(8,128)(2,1)S(1)}, bf16[8,512]{1,0:T(8,128)(2,1)S(1)}, u32[]{:S(2)}, u32[]{:S(2)}) collective-permute-start(bf16[8,512]{1,0:T(8,128)(2,1)S(1)} %get-tuple-element.82.own), channel_id=1, source_target_pairs={{0,1},{1,0},{2,3},{3,2},{4,5},{5,4},{6,7},{7,6},{8,9},{9,8},{10,11... | collective-permute-start | bytes 24584 | tf_op jit(solution)/shard_map/ppermute | solution.py:410
  21.2 3.1 %collective-permute-start.3 = (bf16[8,512]{1,0:T(8,128)(2,1)S(1)}, bf16[8,512]{1,0:T(8,128)(2,1)S(1)}, u32[]{:S(2)}, u32[]{:S(2)}) collective-permute-start(bf16[8,512]{1,0:T(8,128)(2,1)S(1)} %get-tuple-element.82.own), channel_id=1, source_target_pairs={{0,255},{1,2},{2,1},{3,4},{4,3},{5,6},{6,5},{7,8},{8,7},{9,10},{10... | collective-permute-start | bytes 24584 | tf_op jit(solution)/shard_map/ppermute | solution.py:409
  26.2 4.8 %collective-permute-start.4 = (bf16[8,512]{1,0:T(8,128)(2,1)S(1)}, bf16[8,512]{1,0:T(8,128)(2,1)S(1)}, u32[]{:S(2)}, u32[]{:S(2)}) collective-permute-start(bf16[8,512]{1,0:T(8,128)(2,1)S(1)} %get-tuple-element.91.own), channel_id=1, source_target_pairs={{0,1},{1,0},{2,3},{3,2},{4,5},{5,4},{6,7},{7,6},{8,9},{9,8},{10,11... | collective-permute-start | bytes 24584 | tf_op jit(solution)/shard_map/ppermute | solution.py:410
  30.1 3.1 %collective-permute-start.5 = (bf16[8,512]{1,0:T(8,128)(2,1)S(1)}, bf16[8,512]{1,0:T(8,128)(2,1)S(1)}, u32[]{:S(2)}, u32[]{:S(2)}) collective-permute-start(bf16[8,512]{1,0:T(8,128)(2,1)S(1)} %get-tuple-element.91.own), channel_id=1, source_target_pairs={{0,255},{1,2},{2,1},{3,4},{4,3},{5,6},{6,5},{7,8},{8,7},{9,10},{10... | collective-permute-start | bytes 24584 | tf_op jit(solution)/shard_map/ppermute | solution.py:409
  35.1 4.9 %collective-permute-start.6 = (bf16[8,512]{1,0:T(8,128)(2,1)S(1)}, bf16[8,512]{1,0:T(8,128)(2,1)S(1)}, u32[]{:S(2)}, u32[]{:S(2)}) collective-permute-start(bf16[8,512]{1,0:T(8,128)(2,1)S(1)} %get-tuple-element.100.own), channel_id=1, source_target_pairs={{0,1},{1,0},{2,3},{3,2},{4,5},{5,4},{6,7},{7,6},{8,9},{9,8},{10,11... | collective-permute-start | bytes 24584 | tf_op jit(solution)/shard_map/ppermute | solution.py:410
  39.2 3.1 %collective-permute-start.7 = (bf16[8,512]{1,0:T(8,128)(2,1)S(1)}, bf16[8,512]{1,0:T(8,128)(2,1)S(1)}, u32[]{:S(2)}, u32[]{:S(2)}) collective-permute-start(bf16[8,512]{1,0:T(8,128)(2,1)S(1)} %get-tuple-element.100.own), channel_id=1, source_target_pairs={{0,255},{1,2},{2,1},{3,4},{4,3},{5,6},{6,5},{7,8},{8,7},{9,10},{10... | collective-permute-start | bytes 24584 | tf_op jit(solution)/shard_map/ppermute | solution.py:409
  44.8 4.6 %collective-permute-start.8 = (bf16[8,512]{1,0:T(8,128)(2,1)S(1)}, bf16[8,512]{1,0:T(8,128)(2,1)S(1)}, u32[]{:S(2)}, u32[]{:S(2)}) collective-permute-start(bf16[8,512]{1,0:T(8,128)(2,1)S(1)} %get-tuple-element.108.own), channel_id=1, source_target_pairs={{0,1},{1,0},{2,3},{3,2},{4,5},{5,4},{6,7},{7,6},{8,9},{9,8},{10,11... | collective-permute-start | bytes 24584 | tf_op jit(solution)/shard_map/ppermute | solution.py:410
  48.6 3.1 %collective-permute-start.9 = (bf16[8,512]{1,0:T(8,128)(2,1)S(1)}, bf16[8,512]{1,0:T(8,128)(2,1)S(1)}, u32[]{:S(2)}, u32[]{:S(2)}) collective-permute-start(bf16[8,512]{1,0:T(8,128)(2,1)S(1)} %get-tuple-element.108.own), channel_id=1, source_target_pairs={{0,255},{1,2},{2,1},{3,4},{4,3},{5,6},{6,5},{7,8},{8,7},{9,10},{10... | collective-permute-start | bytes 24584 | tf_op jit(solution)/shard_map/ppermute | solution.py:409

commit v6 on v3

--- a/solution.py
+++ b/solution.py
@@ -36,10 +36,11 @@
     return jnp.broadcast_to(jnp.sum(value, axis=0, keepdims=True), value.shape)
 
 
-def write_stack(field, leaf_basis, transfer, stack):
+def write_stack(field, leaf_basis, transfer, stack, turned=None):
     rounded = field.astype(BF16)
     stack[:, :PANEL] = rounded
-    kept = diagonal(dot_nt(rounded, leaf_basis), RANK)
+    coeffs = dot(rounded, turned[...]) if turned is not None else dot_nt(rounded, leaf_basis)
+    kept = diagonal(coeffs, RANK)
     folded = sum(kept[:, at : at + 2 * RANK] for at in range(0, kept.shape[1], 2 * RANK))
     coeffs = folded[:, :RANK] + folded[:, RANK:]
     stack[:, C_AT:] = jnp.concatenate([coeffs, jnp.zeros_like(coeffs)], axis=1).astype(BF16)
@@ -51,7 +52,7 @@
     return jnp.concatenate([value[at : at + rows] for at in range(0, value.shape[0], rows)], axis=1)
 
 
-def apply_rows(field, own, mate, far, pick_near, pick_far, pick_top, near, leaf_basis, coupling, transfer, top):
+def apply_rows(field, own, mate, far, pick_near, pick_far, pick_top, near, leaf_basis, coupling, transfer_turned, top):
     leaves = field.shape[0]
     rest = jnp.zeros((SOURCES - 3 * leaves, WIDTH), F32)
     window = jnp.concatenate(
@@ -62,7 +63,7 @@
     panels = dot(pick_near[...], window[:, :PANEL]).astype(BF16)
     tops = diagonal(dot(parents, top[...]), PRANK)
     tops = sum(tops[:, at : at + PRANK] for at in range(0, tops.shape[1], PRANK)).astype(BF16)
-    local = diagonal(dot(coeffs, coupling[...]), RANK) + diagonal(dot_nt(tops, transfer), 2 * RANK)
+    local = diagonal(dot(coeffs, coupling[...]), RANK) + diagonal(dot(tops, transfer_turned[...]), 2 * RANK)
     total = dot(diagonal(flat(local), RANK).astype(BF16), leaf_basis)
     row = lax.broadcasted_iota(jnp.int32, total.shape, 0)
     for i in range(leaves):
@@ -94,9 +95,14 @@
     write_stack(product[...], stacked(leaf_basis_in), stacked(transfer_in), stack)
 
 
+def identity(size):
+    row = lax.broadcasted_iota(jnp.int32, (size, size), 0)
+    return jnp.where(row == lax.broadcasted_iota(jnp.int32, (size, size), 1), 1.0, 0.0).astype(BF16)
+
+
 def prepare_kernel(
-    _, roots, near, near_ids, coupling, far_ids, top, top_ids,
-    scales, near_out, coupling_out, top_out, pick_near, pick_far, pick_top,
+    _, leaf_basis, transfer, roots, near, near_ids, coupling, far_ids, top, top_ids,
+    scales, basis_turned, transfer_turned, near_out, coupling_out, top_out, pick_near, pick_far, pick_top,
     roots_in, near_in, coupling_in, top_in, near_ids_in, far_ids_in, top_ids_in, sems,
 ):
     leaves = near.shape[0]
@@ -109,6 +115,9 @@
     ]
     for copy in copies:
         copy.start()
+    basis_turned[...] = stacked(leaf_basis).T
+    transfer_turned[...] = stacked(transfer).T
+    unit = identity(PANEL)
     for copy in copies[:4]:
         copy.wait()
     for k in range(roots.shape[1]):
@@ -130,10 +139,9 @@
                 hot = jnp.concatenate([hot, jnp.zeros((leaves - rows, SOURCES), F32)], axis=0)
             pick[k * leaves : (k + 1) * leaves, :] = hot.astype(BF16)
     copies[4].wait()
-    for i in range(leaves):
-        for k in range(coupling.shape[1]):
-            rows, lanes = slice(k * RANK, (k + 1) * RANK), slice(i * RANK, (i + 1) * RANK)
-            coupling_out[rows, lanes] = coupling_in[i, k].T
+    for k in range(coupling.shape[1]):
+        rows = jnp.concatenate([coupling_in[i, k] for i in range(leaves)], axis=0)
+        coupling_out[k * RANK : (k + 1) * RANK, :] = rows.T
     copies[5].wait()
     for p in range(top.shape[0]):
         for k in range(top.shape[1]):
@@ -142,19 +150,16 @@
     for i in range(leaves):
         copies[6 + i].wait()
         for k in range(near.shape[1]):
-            near_out[i, k] = near_in[i, k].T
-
-
-def step_kernel(
-    step, last, scales, product, partial, own, mate, far, pick_near, pick_far, pick_top,
-    near, leaf_basis, coupling, transfer, top, product_out, partial_out, stack,
-):
-    leaves = product.shape[0]
-    basis_rows, transfer_rows = stacked(leaf_basis), stacked(transfer)
-    field = product[...]
-    image = apply_rows(
-        field, own, mate, far, pick_near, pick_far, pick_top, near, basis_rows, coupling, transfer_rows, top
-    )
+            near_out[i, k] = dot_nt(unit, near_in[i, k]).astype(BF16) if k % 2 else near_in[i, k].T
+
+
+def at_an_end():
+    place = lax.axis_index(AXES)
+    return jnp.logical_or(place == 0, place == lax.axis_size(AXES) - 1)
+
+
+def advance(step, last, image, field, scales, partial, matrices, outs):
+    leaves = field.shape[0]
     root = scales[step * leaves : (step + 1) * leaves, :]
     after = field - image / root
     total = field / root
@@ -162,28 +167,83 @@
         total += partial[...]
     if last:
         total += after / scales[(step + 1) * leaves : (step + 2) * leaves, :]
-    product_out[...] = after
-    partial_out[...] = total
-    write_stack(total if last else after, basis_rows, transfer_rows, stack)
-
-
-def last_kernel(
-    field, own, mate, far, pick_near, pick_far, pick_top,
-    near, leaf_basis, coupling, transfer, top, basis, image_out, sums,
-):
-    image = apply_rows(
-        field[...], own, mate, far, pick_near, pick_far, pick_top,
-        near, stacked(leaf_basis), coupling, stacked(transfer), top,
+    else:
+        outs[2][...] = after
+    outs[0][...] = total
+    write_stack(total if last else after, stacked(matrices[1]), stacked(matrices[3]), outs[1], matrices[5])
+
+
+def image_of(field, own, mate, far, picks, matrices):
+    near, leaf_basis, coupling, _, top, _, transfer_turned = matrices
+    return apply_rows(
+        field, own, mate, far, *picks, near, stacked(leaf_basis), coupling, transfer_turned, top
     )
-    image_out[...] = image
-    count, leaves = basis.shape[0], image.shape[0]
+
+
+def step_early(step, last, scales, product, partial, own, mate, *rest):
+    picks, matrices, outs = rest[:3], rest[3:10], rest[10:]
+
+    @pl.when(at_an_end())
+    def _():
+        field = product[...]
+        image = image_of(field, own, mate, own, picks, matrices)
+        advance(step, last, image, field, scales, partial, matrices, outs)
+
+
+def step_late(step, last, scales, product, partial, own, mate, far, *rest):
+    picks, matrices, rest = rest[:3], rest[3:10], rest[10:]
+    ready, outs = rest[: len(rest) // 2], rest[len(rest) // 2 :]
+    end = at_an_end()
+
+    @pl.when(jnp.logical_not(end))
+    def _():
+        field = product[...]
+        image = image_of(field, own, mate, far, picks, matrices)
+        advance(step, last, image, field, scales, partial, matrices, outs)
+
+    @pl.when(end)
+    def _():
+        for source, target in zip(ready, outs):
+            target[...] = source[...]
+
+
+def pack_iota(count):
     lane = lax.broadcasted_iota(jnp.int32, (count, 128), 1)
-    sub = lax.broadcasted_iota(jnp.int32, (count, 128), 0)
+    return lane, lax.broadcasted_iota(jnp.int32, (count, 128), 0)
+
+
+def last_early(field, own, mate, *rest):
+    picks, matrices, (basis, image_out, gram) = rest[:3], rest[3:10], rest[10:]
+    count = basis.shape[0]
+    lane, sub = pack_iota(count)
     vectors = basis[...]
     packed = jnp.zeros((count, 128), F32)
     for n in range(count):
         column = jnp.sum(vectors * vectors[n : n + 1], axis=1, keepdims=True)
         packed = jnp.where(lane == n * count + sub, column, packed)
+    gram[...] = packed
+
+    @pl.when(at_an_end())
+    def _():
+        image_out[...] = image_of(field[...], own, mate, own, picks, matrices)
+
+
+def last_late(field, own, mate, far, *rest):
+    picks, matrices, (basis, ready, gram, image_out, sums) = rest[:3], rest[3:10], rest[10:]
+    end = at_an_end()
+
+    @pl.when(jnp.logical_not(end))
+    def _():
+        image_out[...] = image_of(field[...], own, mate, far, picks, matrices)
+
+    @pl.when(end)
+    def _():
+        image_out[...] = ready[...]
+
+    image = image_out[...]
+    count, leaves = basis.shape[0], image.shape[0]
+    lane, sub = pack_iota(count)
+    packed = gram[...]
     dots = jnp.zeros((count, PANEL), F32)
     for i in range(leaves):
         dots += basis[:, i * PANEL : (i + 1) * PANEL] * image[i : i + 1]
@@ -215,7 +275,7 @@
         vector_out[2 * i : 2 * i + 1, :] = row[:, : PANEL // 2]
         vector_out[2 * i + 1 : 2 * i + 2, :] = row[:, PANEL // 2 :]
     values = jnp.sum(jnp.where(lane == sub, coef, zero), axis=0, keepdims=True)
-    hessen_out[...] = jnp.where(lane[:1] == count, beta, values)
+    hessen_out[...] = jnp.where(lane[:1] == count, beta, values)[0, : count + 1]
 
 
 def call(kernel, specs, outs, scratch=()):
@@ -256,11 +316,13 @@
     far = lax.ppermute(stack, AXES, others)
     mate = lax.ppermute(stack, AXES, mates)
     roots = roots.reshape(1, -1)
-    scales, near, coupling, top, *picks = call(
+    scales, basis_turned, transfer_turned, near, coupling, top, *picks = call(
         prepare_kernel,
-        [VMEM] + [HBM] * 7,
+        [VMEM] * 3 + [HBM] * 7,
         [
             ((roots.shape[1] * leaves, PANEL), F32),
+            ((PANEL, leaves * RANK), BF16),
+            ((PRANK, leaves * RANK), BF16),
             (near_blocks.shape, BF16),
             ((fars * RANK, leaves * RANK), BF16),
             ((tops * PRANK, parents * PRANK), BF16),
@@ -270,27 +332,33 @@
         ],
         [like(a) for a in (roots, near_blocks, far_coupling, top_coupling, near_ids, far_ids, top_ids)]
         + [pltpu.SemaphoreType.DMA((6 + leaves,))],
-    )(product, *pinned(roots, near_blocks, near_ids, far_coupling, far_ids, top_coupling, top_ids))
-    matrices = (*picks, near, leaf_basis, coupling, transfer, top)
+    )(product, leaf_basis, transfer, *pinned(roots, near_blocks, near_ids, far_coupling, far_ids, top_coupling, top_ids))
+    matrices = (*picks, near, leaf_basis, coupling, transfer, top, basis_turned, transfer_turned)
     partial = product
     steps = roots.shape[1] - 1
+    square = ((leaves, PANEL), F32)
     for step in range(steps):
-        product, partial, stack = call(
-            functools.partial(step_kernel, step, step == steps - 1),
-            [VMEM] * 14,
-            [((leaves, PANEL), F32), ((leaves, PANEL), F32), ((leaves, WIDTH), BF16)],
-        )(scales, product, partial, stack, mate, far, *matrices)
+        last = step == steps - 1
+        outs = [square, ((leaves, WIDTH), BF16)] + ([] if last else [square])
+        state = (scales, product, partial, stack, mate)
+        ready = call(functools.partial(step_early, step, last), [VMEM] * 15, outs)(*state, *matrices)
+        partial, stack, *after = call(
+            functools.partial(step_late, step, last), [VMEM] * (16 + len(outs)), outs
+        )(*state, far, *matrices, *ready)
+        product = None if last else after[0]
         far = lax.ppermute(stack, AXES, others)
         mate = lax.ppermute(stack, AXES, mates)
-    image, sums = call(
-        last_kernel, [VMEM] * 13, [((leaves, PANEL), F32), ((devices, 128), F32)]
-    )(partial, stack, mate, far, *matrices, basis)
+    state = (partial, stack, mate)
+    ready = call(last_early, [VMEM] * 14, [square, ((basis.shape[0], 128), F32)])(*state, *matrices, basis)
+    image, sums = call(last_late, [VMEM] * 17, [square, ((devices, 128), F32)])(
+        *state, far, *matrices, basis, *ready
+    )
     sums = lax.all_to_all(sums.reshape(devices, 1, 128), AXES, 0, 0, tiled=True)
     size = float(leaves * PANEL * devices)
     vector, hessen = call(
-        functools.partial(finish_kernel, size), [VMEM] * 3, [((leaves * 2, 128), F32), ((1, 128), F32)]
+        functools.partial(finish_kernel, size), [VMEM] * 3, [((leaves * 2, 128), F32), ((basis.shape[0] + 1,), F32)]
     )(sums.reshape(devices, 128), image, basis)
-    return vector.reshape(leaves * PANEL), hessen[0, : basis.shape[0] + 1]
+    return vector.reshape(leaves * PANEL), hessen
 
 
 def solution(mesh):

time: 81.2 us -> 75.4 us (0.929)
  starting transfers between devices: 38.6 us -> 23.5 us
  waiting for transfers between devices: 3.32 us -> 12.2 us
  blocking collectives: 22.3 us -> 23.3 us
    ppermute x5, starting transfers between devices: 35.5 us -> 23.5 us  [body(): mate = lax.ppermute(stack, AXES, mates)]
    ppermute x5, waiting for transfers between devices: 0.01 us -> 8.87 us  [body(): far = lax.ppermute(stack, AXES, others)]
    ppermute x5, starting transfers between devices: 3.15 us -> 0.01 us  [body(): far = lax.ppermute(stack, AXES, others)]
    all_to_all x1, blocking collectives: 22.3 us -> 23.3 us  [body(): sums = lax.all_to_all(sums.reshape(devices, 1, 128), AXES, 0, 0, tiled=True)]
    pallas_call x6 -> x11, Pallas kernels: 13.5 us -> 13.3 us  [the longest x4 6.85 us: body(): call(functools.partial(step_late, step, last), [VMEM] * (16 + len(outs)),...]
  transfers between devices with their start and end apart: 10 -> 10, of which waited for: 4 -> 8; matrix products, arithmetic and copies ran while one was open for 0% -> 0% of each run, Pallas kernels for 5% -> 7%
where the time goes in v6:
time: 75.4 us; the launch traced here: 75.3 us
  starting transfers between devices  23.5 us (31%)
  blocking collectives  23.3 us (31%)
  Pallas kernels  15.5 us (21%)
  waiting for transfers between devices  12.2 us (16%)
    ppermute x5, starting transfers between devices, body(): mate = lax.ppermute(stack, AXES, mates)  23.5 us
    all_to_all x1, blocking collectives, body(): sums = lax.all_to_all(sums.reshape(devices, 1, 128), AXES, 0, 0, tiled=True)  23.3 us
    ppermute x5, waiting for transfers between devices, body(): far = lax.ppermute(stack, AXES, others)  8.87 us
    pallas_call x4, Pallas kernels, body(): call(functools.partial(step_late, step, last), [VMEM] * (16 + len(outs)),...  6.85 us
    pallas_call x1, Pallas kernels, body(): call(prepare_kernel, [VMEM] * 3 + [HBM] * 7, [((roots.shape[1] * leaves,...  4.77 us
    ppermute x5, waiting for transfers between devices, body(): mate = lax.ppermute(stack, AXES, mates)  3.3 us
    pallas_call x1, Pallas kernels, body(): call(last_late, [VMEM] * 17, [square, ((devices, 128), F32)])  1.57 us
  transfers between devices with their start and end apart: 10, of which 8 were waited for; matrix products, arithmetic and copies ran while one was open for 0% of the time, Pallas kernels for 7%

profile of v6, /device:TPU:1, one launch (start us, length us, event | category | flops | bytes accessed | tf_op | source)
XLA Modules:
  0.0 75.3 jit_solution(4046206946824612441)
XLA Ops:
  0.6 1.4 %shard_map.113 = (f32[8,256]{1,0:T(8,128)S(1)}, bf16[8,512]{1,0:T(8,128)(2,1)S(1)}, f32[8,2048]{1,0:T(8,128)S(1)}, bf16[8,64,256]{2,1,0:T(8,128)(2,1)S(1)}, bf16[8,64,128]{2,1,0:T(8,128)(2,1)S(1)}) custom-call(f32[8,2048]{1,0:T(8,128)} %basis.1, bf16[8,64,256]{2,1,0:T(8,128)(2,1)} %leaf_basis.1, bf16[8,64,128]{2,1,0:T(8,128)(2,1)} %transfer.1), custom_call_target="tpu_custom_call" | custom-call | tf_op jit(solution)/shard_map/pallas_call | solution.py:310
  2.0 3.3 %collective-permute-start = (bf16[8,512]{1,0:T(8,128)(2,1)S(1)}, bf16[8,512]{1,0:T(8,128)(2,1)S(1)}, u32[]{:S(2)}, u32[]{:S(2)}) collective-permute-start(bf16[8,512]{1,0:T(8,128)(2,1)S(1)} %get-tuple-element.48.own), channel_id=1, source_target_pairs={{0,1},{1,0},{2,3},{3,2},{4,5},{5,4},{6,7},{7,6},{8,9},{9,8},{10,11... | collective-permute-start | bytes 24584 | tf_op jit(solution)/shard_map/ppermute | solution.py:317
  5.3 0.0 collective-permute-start.1
  5.3 4.8 %shard_map.114 = (f32[40,256]{1,0:T(8,128)S(1)}, bf16[256,512]{1,0:T(8,128)(2,1)S(1)}, bf16[128,512]{1,0:T(8,128)(2,1)S(1)}, bf16[8,6,256,256]{3,2,1,0:T(8,128)(...) custom-call(f32[8,256]{1,0:T(8,128)S(1)} %get-tuple-element.44._.pro, ...), custom_call_target="tpu_custom_call" | custom-call | tf_op jit(solution)/shard_map/pallas_call | solution.py:319
  10.1 0.0 collective-permute-done.mate
  10.2 0.0 collective-permute-done.1.far
  10.2 1.7 %shard_map.116 = (f32[8,256]{1,0:T(8,128)S(1)}, bf16[8,512]{1,0:T(8,128)(2,1)S(1)}, f32[8,256]{1,0:T(8,128)S(1)}) custom-call(f32[40,256]{1,0:T(8,128)S(1)} %get-tuple-element.47.scales, f32[8,256]{1,0:T(8,128)S(1)} %get-tuple-element.44._.product.partial, f32[8,256]{1,0:T(8,128)S(1)} %get-tuple-element.44._.product.partial, ...), custom_call_target="tpu_custom_call" | custom-call | tf_op jit(solution)/shard_map/pallas_call | solution.py:345
  11.9 8.9 %collective-permute-start.2 = (bf16[8,512]{1,0:T(8,128)(2,1)S(1)}, bf16[8,512]{1,0:T(8,128)(2,1)S(1)}, u32[]{:S(2)}, u32[]{:S(2)}) collective-permute-start(bf16[8,512]{1,0:T(8,128)(2,1)S(1)} %get-tuple-element.62.own), channel_id=1, source_target_pairs={{0,1},{1,0},{2,3},{3,2},{4,5},{5,4},{6,7},{7,6},{8,9},{9,8},{10,11... | collective-permute-start | bytes 24584 | tf_op jit(solution)/shard_map/ppermute | solution.py:350
  20.8 0.0 collective-permute-start.3
  20.8 0.8 %collective-permute-done.2.mate = bf16[8,512]{1,0:T(8,128)(2,1)S(1)} collective-permute-done((bf16[8,512]{1,0:T(8,128)(2,1)S(1)}, bf16[8,512]{1,0:T(8,128)(2,1)S(1)}, u32[]{:S(2)}, u32[]{:S(2)}) %collective-permute-start.2) | collective-permute-done | bytes 8224 | tf_op jit(solution)/shard_map/ppermute | solution.py:350
  21.6 2.2 %collective-permute-done.3.far = bf16[8,512]{1,0:T(8,128)(2,1)S(1)} collective-permute-done((bf16[8,512]{1,0:T(8,128)(2,1)S(1)}, bf16[8,512]{1,0:T(8,128)(2,1)S(1)}, u32[]{:S(2)}, u32[]{:S(2)}) %collective-permute-start.3) | collective-permute-done | bytes 8224 | tf_op jit(solution)/shard_map/ppermute | solution.py:349
  23.9 1.7 %shard_map.118 = (f32[8,256]{1,0:T(8,128)S(1)}, bf16[8,512]{1,0:T(8,128)(2,1)S(1)}, f32[8,256]{1,0:T(8,128)S(1)}) custom-call(f32[40,256]{1,0:T(8,128)S(1)} %get-tuple-element.47.scales, f32[8,256]{1,0:T(8,128)S(1)} %get-tuple-element.60.product, f32[8,256]{1,0:T(8,128)S(1)} %get-tuple-element.61.partial, bf16[8,512]{1,0:T(8,128)(2,1)S(1)} %get-tuple-element.62.own, ...), custom_call_target="tpu_custom_call" | custom-call | tf_op jit(solution)/shard_map/pallas_call | solution.py:345
  25.6 3.8 %collective-permute-start.4 = (bf16[8,512]{1,0:T(8,128)(2,1)S(1)}, bf16[8,512]{1,0:T(8,128)(2,1)S(1)}, u32[]{:S(2)}, u32[]{:S(2)}) collective-permute-start(bf16[8,512]{1,0:T(8,128)(2,1)S(1)} %get-tuple-element.68.own), channel_id=1, source_target_pairs={{0,1},{1,0},{2,3},{3,2},{4,5},{5,4},{6,7},{7,6},{8,9},{9,8},{10,11... | collective-permute-start | bytes 24584 | tf_op jit(solution)/shard_map/ppermute | solution.py:350
  29.4 0.0 collective-permute-start.5
  29.4 0.8 %collective-permute-done.4.mate = bf16[8,512]{1,0:T(8,128)(2,1)S(1)} collective-permute-done((bf16[8,512]{1,0:T(8,128)(2,1)S(1)}, bf16[8,512]{1,0:T(8,128)(2,1)S(1)}, u32[]{:S(2)}, u32[]{:S(2)}) %collective-permute-start.4) | collective-permute-done | bytes 8224 | tf_op jit(solution)/shard_map/ppermute | solution.py:350
  30.3 2.2 %collective-permute-done.5.far = bf16[8,512]{1,0:T(8,128)(2,1)S(1)} collective-permute-done((bf16[8,512]{1,0:T(8,128)(2,1)S(1)}, bf16[8,512]{1,0:T(8,128)(2,1)S(1)}, u32[]{:S(2)}, u32[]{:S(2)}) %collective-permute-start.5) | collective-permute-done | bytes 8224 | tf_op jit(solution)/shard_map/ppermute | solution.py:349
  32.5 1.7 %shard_map.120 = (f32[8,256]{1,0:T(8,128)S(1)}, bf16[8,512]{1,0:T(8,128)(2,1)S(1)}, f32[8,256]{1,0:T(8,128)S(1)}) custom-call(f32[40,256]{1,0:T(8,128)S(1)} %get-tuple-element.47.scales, f32[8,256]{1,0:T(8,128)S(1)} %get-tuple-element.66.product, f32[8,256]{1,0:T(8,128)S(1)} %get-tuple-element.67.partial, bf16[8,512]{1,0:T(8,128)(2,1)S(1)} %get-tuple-element.68.own, ...), custom_call_target="tpu_custom_call" | custom-call | tf_op jit(solution)/shard_map/pallas_call | solution.py:345
  34.2 3.7 %collective-permute-start.6 = (bf16[8,512]{1,0:T(8,128)(2,1)S(1)}, bf16[8,512]{1,0:T(8,128)(2,1)S(1)}, u32[]{:S(2)}, u32[]{:S(2)}) collective-permute-start(bf16[8,512]{1,0:T(8,128)(2,1)S(1)} %get-tuple-element.74.own), channel_id=1, source_target_pairs={{0,1},{1,0},{2,3},{3,2},{4,5},{5,4},{6,7},{7,6},{8,9},{9,8},{10,11... | collective-permute-start | bytes 24584 | tf_op jit(solution)/shard_map/ppermute | solution.py:350
  37.9 0.0 collective-permute-start.7
  37.9 0.8 %collective-permute-done.6.mate = bf16[8,512]{1,0:T(8,128)(2,1)S(1)} collective-permute-done((bf16[8,512]{1,0:T(8,128)(2,1)S(1)}, bf16[8,512]{1,0:T(8,128)(2,1)S(1)}, u32[]{:S(2)}, u32[]{:S(2)}) %collective-permute-start.6) | collective-permute-done | bytes 8224 | tf_op jit(solution)/shard_map/ppermute | solution.py:350
  38.8 2.2 %collective-permute-done.7.far = bf16[8,512]{1,0:T(8,128)(2,1)S(1)} collective-permute-done((bf16[8,512]{1,0:T(8,128)(2,1)S(1)}, bf16[8,512]{1,0:T(8,128)(2,1)S(1)}, u32[]{:S(2)}, u32[]{:S(2)}) %collective-permute-start.7) | collective-permute-done | bytes 8224 | tf_op jit(solution)/shard_map/ppermute | solution.py:349
  41.0 1.7 %shard_map.122 = (f32[8,256]{1,0:T(8,128)S(1)}, bf16[8,512]{1,0:T(8,128)(2,1)S(1)}) custom-call(f32[40,256]{1,0:T(8,128)S(1)} %get-tuple-element.47.scales, f32[8,256]{1,0:T(8,128)S(1)} %get-tuple-element.72.product, f32[8,256]{1,0:T(8,128)S(1)} %get-tuple-element.73.partial, bf16[8,512]{1,0:T(8,128)(2,1)S(1)} %get-tuple-element.74.own, ...), custom_call_target="tpu_custom_call" | custom-call | tf_op jit(solution)/shard_map/pallas_call | solution.py:345
  42.7 3.7 %collective-permute-start.8 = (bf16[8,512]{1,0:T(8,128)(2,1)S(1)}, bf16[8,512]{1,0:T(8,128)(2,1)S(1)}, u32[]{:S(2)}, u32[]{:S(2)}) collective-permute-start(bf16[8,512]{1,0:T(8,128)(2,1)S(1)} %get-tuple-element.78.own), channel_id=1, source_target_pairs={{0,1},{1,0},{2,3},{3,2},{4,5},{5,4},{6,7},{7,6},{8,9},{9,8},{10,11... | collective-permute-start | bytes 24584 | tf_op jit(solution)/shard_map/ppermute | solution.py:350
  46.5 0.0 collective-permute-start.9
  46.5 0.8 %collective-permute-done.8.mate = bf16[8,512]{1,0:T(8,128)(2,1)S(1)} collective-permute-done((bf16[8,512]{1,0:T(8,128)(2,1)S(1)}, bf16[8,512]{1,0:T(8,128)(2,1)S(1)}, u32[]{:S(2)}, u32[]{:S(2)}) %collective-permute-start.8) | collective-permute-done | bytes 8224 | tf_op jit(solution)/shard_map/ppermute | solution.py:350
  47.3 0.1 shard_map.123
  47.4 2.1 %collective-permute-done.9.far = bf16[8,512]{1,0:T(8,128)(2,1)S(1)} collective-permute-done((bf16[8,512]{1,0:T(8,128)(2,1)S(1)}, bf16[8,512]{1,0:T(8,128)(2,1)S(1)}, u32[]{:S(2)}, u32[]{:S(2)}) %collective-permute-start.9) | collective-permute-done | bytes 8224 | tf_op jit(solution)/shard_map/ppermute | solution.py:349
  49.5 1.6 %shard_map.124 = (f32[8,256]{1,0:T(8,128)S(1)}, f32[256,128]{1,0:T(8,128)S(1)}) custom-call(f32[8,256]{1,0:T(8,128)S(1)} %get-tuple-element.77.field, bf16[8,512]{1,0:T(8,128)(2,1)S(1)} %get-tuple-element.78.own, bf16[8,512]{1,0:T(8,128)(2,1)S(1)} %collective-permute-done.8.mate, bf16[8,512]{1,0:T(8,128)(2,1)S(1)} %collective-permute-done.9.far, ...), custom_call_target="tpu_custom_call" | custom-call | tf_op jit(solution)/shard_map/pallas_call | solution.py:353
  51.1 23.3 %all_to_all.5 = f32[256,1,128]{2,1,0:T(1,128)S(1)} all-to-all(f32[256,1,128]{2,1,0:T(1,128)S(1)} %bitcast.7), channel_id=1, replica_groups=mesh['grp'=4,'leaf'=64] {'grp','leaf'}, dimensions={0} | all-to-all | bytes 262144 | tf_op jit(solution)/shard_map/all_to_all | solution.py:356
  74.4 0.8 %shard_map.125 = (f32[16,128]{1,0:T(8,128)}, f32[9]{0:T(128)}) custom-call(f32[256,128]{1,0:T(8,128)S(1)} %bitcast.6, f32[8,256]{1,0:T(8,128)S(1)} %get-tuple-element.83.image, f32[8,2048]{1,0:T(8,128)S(1)} %get-tuple-element.79.rest_10_.basis), custom_call_target="tpu_custom_call" | custom-call | tf_op jit(solution)/shard_map/pallas_call | solution.py:358
  (4 shorter events, 0.0 us)
Async XLA Ops:
  2.0 8.1 %collective-permute-start = (bf16[8,512]{1,0:T(8,128)(2,1)S(1)}, bf16[8,512]{1,0:T(8,128)(2,1)S(1)}, u32[]{:S(2)}, u32[]{:S(2)}) collective-permute-start(bf16[8,512]{1,0:T(8,128)(2,1)S(1)} %get-tuple-element.48.own), channel_id=1, source_target_pairs={{0,1},{1,0},{2,3},{3,2},{4,5},{5,4},{6,7},{7,6},{8,9},{9,8},{10,11... | collective-permute-start | bytes 24584 | tf_op jit(solution)/shard_map/ppermute | solution.py:317
  5.3 4.8 %collective-permute-start.1 = (bf16[8,512]{1,0:T(8,128)(2,1)S(1)}, bf16[8,512]{1,0:T(8,128)(2,1)S(1)}, u32[]{:S(2)}, u32[]{:S(2)}) collective-permute-start(bf16[8,512]{1,0:T(8,128)(2,1)S(1)} %get-tuple-element.48.own), channel_id=1, source_target_pairs={{0,255},{1,2},{2,1},{3,4},{4,3},{5,6},{6,5},{7,8},{8,7},{9,10},{10... | collective-permute-start | bytes 24584 | tf_op jit(solution)/shard_map/ppermute | solution.py:316
  11.9 9.8 %collective-permute-start.2 = (bf16[8,512]{1,0:T(8,128)(2,1)S(1)}, bf16[8,512]{1,0:T(8,128)(2,1)S(1)}, u32[]{:S(2)}, u32[]{:S(2)}) collective-permute-start(bf16[8,512]{1,0:T(8,128)(2,1)S(1)} %get-tuple-element.62.own), channel_id=1, source_target_pairs={{0,1},{1,0},{2,3},{3,2},{4,5},{5,4},{6,7},{7,6},{8,9},{9,8},{10,11... | collective-permute-start | bytes 24584 | tf_op jit(solution)/shard_map/ppermute | solution.py:350
  20.8 3.1 %collective-permute-start.3 = (bf16[8,512]{1,0:T(8,128)(2,1)S(1)}, bf16[8,512]{1,0:T(8,128)(2,1)S(1)}, u32[]{:S(2)}, u32[]{:S(2)}) collective-permute-start(bf16[8,512]{1,0:T(8,128)(2,1)S(1)} %get-tuple-element.62.own), channel_id=1, source_target_pairs={{0,255},{1,2},{2,1},{3,4},{4,3},{5,6},{6,5},{7,8},{8,7},{9,10},{10... | collective-permute-start | bytes 24584 | tf_op jit(solution)/shard_map/ppermute | solution.py:349
  25.6 4.7 %collective-permute-start.4 = (bf16[8,512]{1,0:T(8,128)(2,1)S(1)}, bf16[8,512]{1,0:T(8,128)(2,1)S(1)}, u32[]{:S(2)}, u32[]{:S(2)}) collective-permute-start(bf16[8,512]{1,0:T(8,128)(2,1)S(1)} %get-tuple-element.68.own), channel_id=1, source_target_pairs={{0,1},{1,0},{2,3},{3,2},{4,5},{5,4},{6,7},{7,6},{8,9},{9,8},{10,11... | collective-permute-start | bytes 24584 | tf_op jit(solution)/shard_map/ppermute | solution.py:350
  29.4 3.1 %collective-permute-start.5 = (bf16[8,512]{1,0:T(8,128)(2,1)S(1)}, bf16[8,512]{1,0:T(8,128)(2,1)S(1)}, u32[]{:S(2)}, u32[]{:S(2)}) collective-permute-start(bf16[8,512]{1,0:T(8,128)(2,1)S(1)} %get-tuple-element.68.own), channel_id=1, source_target_pairs={{0,255},{1,2},{2,1},{3,4},{4,3},{5,6},{6,5},{7,8},{8,7},{9,10},{10... | collective-permute-start | bytes 24584 | tf_op jit(solution)/shard_map/ppermute | solution.py:349
  34.2 4.6 %collective-permute-start.6 = (bf16[8,512]{1,0:T(8,128)(2,1)S(1)}, bf16[8,512]{1,0:T(8,128)(2,1)S(1)}, u32[]{:S(2)}, u32[]{:S(2)}) collective-permute-start(bf16[8,512]{1,0:T(8,128)(2,1)S(1)} %get-tuple-element.74.own), channel_id=1, source_target_pairs={{0,1},{1,0},{2,3},{3,2},{4,5},{5,4},{6,7},{7,6},{8,9},{9,8},{10,11... | collective-permute-start | bytes 24584 | tf_op jit(solution)/shard_map/ppermute | solution.py:350
  37.9 3.1 %collective-permute-start.7 = (bf16[8,512]{1,0:T(8,128)(2,1)S(1)}, bf16[8,512]{1,0:T(8,128)(2,1)S(1)}, u32[]{:S(2)}, u32[]{:S(2)}) collective-permute-start(bf16[8,512]{1,0:T(8,128)(2,1)S(1)} %get-tuple-element.74.own), channel_id=1, source_target_pairs={{0,255},{1,2},{2,1},{3,4},{4,3},{5,6},{6,5},{7,8},{8,7},{9,10},{10... | collective-permute-start | bytes 24584 | tf_op jit(solution)/shard_map/ppermute | solution.py:349
  42.7 4.6 %collective-permute-start.8 = (bf16[8,512]{1,0:T(8,128)(2,1)S(1)}, bf16[8,512]{1,0:T(8,128)(2,1)S(1)}, u32[]{:S(2)}, u32[]{:S(2)}) collective-permute-start(bf16[8,512]{1,0:T(8,128)(2,1)S(1)} %get-tuple-element.78.own), channel_id=1, source_target_pairs={{0,1},{1,0},{2,3},{3,2},{4,5},{5,4},{6,7},{7,6},{8,9},{9,8},{10,11... | collective-permute-start | bytes 24584 | tf_op jit(solution)/shard_map/ppermute | solution.py:350
  46.5 3.1 %collective-permute-start.9 = (bf16[8,512]{1,0:T(8,128)(2,1)S(1)}, bf16[8,512]{1,0:T(8,128)(2,1)S(1)}, u32[]{:S(2)}, u32[]{:S(2)}) collective-permute-start(bf16[8,512]{1,0:T(8,128)(2,1)S(1)} %get-tuple-element.78.own), channel_id=1, source_target_pairs={{0,255},{1,2},{2,1},{3,4},{4,3},{5,6},{6,5},{7,8},{8,7},{9,10},{10... | collective-permute-start | bytes 24584 | tf_op jit(solution)/shard_map/ppermute | solution.py:349

commit v7 on v6

--- a/solution.py
+++ b/solution.py
@@ -58,20 +58,30 @@
     window = jnp.concatenate(
         [own[...].astype(F32), mate[...].astype(F32), far[...].astype(F32), rest], axis=0
     ).astype(BF16)
+    panels = dot(pick_near[...], window[:, :PANEL]).astype(BF16)
     parents = tiles(dot(pick_top[...], window[:, T_AT:C_AT]), leaves).astype(BF16)
     coeffs = tiles(dot(pick_far[...], window[:, C_AT : C_AT + RANK]), leaves).astype(BF16)
-    panels = dot(pick_near[...], window[:, :PANEL]).astype(BF16)
+    row = lax.broadcasted_iota(jnp.int32, field.shape, 0)
+
+    def near_rows(total, some):
+        for i in some:
+            image = jnp.zeros(total.shape, F32)
+            for k in range(near.shape[1]):
+                image += dot(panels[k * leaves : (k + 1) * leaves], near[i, k])
+            total += jnp.where(row == i, image, jnp.zeros_like(image))
+        return total
+
+    quarter = leaves // 4
+    total = near_rows(0.5 * field, range(quarter))
     tops = diagonal(dot(parents, top[...]), PRANK)
+    local = diagonal(dot(coeffs, coupling[...]), RANK)
+    total = near_rows(total, range(quarter, 2 * quarter))
     tops = sum(tops[:, at : at + PRANK] for at in range(0, tops.shape[1], PRANK)).astype(BF16)
-    local = diagonal(dot(coeffs, coupling[...]), RANK) + diagonal(dot(tops, transfer_turned[...]), 2 * RANK)
-    total = dot(diagonal(flat(local), RANK).astype(BF16), leaf_basis)
-    row = lax.broadcasted_iota(jnp.int32, total.shape, 0)
-    for i in range(leaves):
-        image = jnp.zeros(total.shape, F32)
-        for k in range(near.shape[1]):
-            image += dot(panels[k * leaves : (k + 1) * leaves], near[i, k])
-        total += jnp.where(row == i, image, jnp.zeros_like(image))
-    return 0.5 * field + total
+    local += diagonal(dot(tops, transfer_turned[...]), 2 * RANK)
+    total = near_rows(total, range(2 * quarter, 3 * quarter))
+    rows = dot(diagonal(flat(local), RANK).astype(BF16), leaf_basis)
+    total = near_rows(total, range(3 * quarter, leaves))
+    return total + rows
 
 
 def stacked(ref):
@@ -122,7 +132,7 @@
         copy.wait()
     for k in range(roots.shape[1]):
         scales[k * leaves : (k + 1) * leaves, :] = jnp.broadcast_to(
-            roots_in[:, k : k + 1], (leaves, scales.shape[1])
+            1.0 / roots_in[:, k : k + 1], (leaves, scales.shape[1])
         )
     place = lax.axis_index(AXES)
     odd = place % 2 == 1
@@ -161,12 +171,12 @@
 def advance(step, last, image, field, scales, partial, matrices, outs):
     leaves = field.shape[0]
     root = scales[step * leaves : (step + 1) * leaves, :]
-    after = field - image / root
-    total = field / root
+    after = field - image * root
+    total = field * root
     if step:
         total += partial[...]
     if last:
-        total += after / scales[(step + 1) * leaves : (step + 2) * leaves, :]
+        total += after * scales[(step + 1) * leaves : (step + 2) * leaves, :]
     else:
         outs[2][...] = after
     outs[0][...] = total
@@ -315,6 +325,7 @@
     )(*pinned(basis, leaf_basis, transfer))
     far = lax.ppermute(stack, AXES, others)
     mate = lax.ppermute(stack, AXES, mates)
+    mate, far = lax.optimization_barrier((mate, far))
     roots = roots.reshape(1, -1)
     scales, basis_turned, transfer_turned, near, coupling, top, *picks = call(
         prepare_kernel,

time: 75.4 us -> 73.7 us (0.977)
  blocking collectives: 23.3 us -> 22.3 us
  Pallas kernels: 15.5 us -> 14.6 us
    ppermute x5, starting transfers between devices: 0.01 us -> 3.2 us  [body(): far = lax.ppermute(stack, AXES, others)]
    ppermute x5, starting transfers between devices: 23.5 us -> 20.6 us  [body(): mate = lax.ppermute(stack, AXES, mates)]
    all_to_all x1, blocking collectives: 23.3 us -> 22.3 us  [body(): sums = lax.all_to_all(sums.reshape(devices, 1, 128), AXES, 0, 0, tiled=True)]
where the time goes in v7:
time: 73.7 us; the launch traced here: 73.6 us
  starting transfers between devices  23.8 us (32%)
  blocking collectives  22.3 us (30%)
  Pallas kernels  14.6 us (20%)
  waiting for transfers between devices  12.2 us (17%)
    all_to_all x1, blocking collectives, body(): sums = lax.all_to_all(sums.reshape(devices, 1, 128), AXES, 0, 0, tiled=True)  22.3 us
    ppermute x5, starting transfers between devices, body(): mate = lax.ppermute(stack, AXES, mates)  20.6 us
    ppermute x5, waiting for transfers between devices, body(): far = lax.ppermute(stack, AXES, others)  8.61 us
    pallas_call x4, Pallas kernels, body(): call(functools.partial(step_late, step, last), [VMEM] * (16 + len(outs)),...  6.14 us
    pallas_call x1, Pallas kernels, body(): call(prepare_kernel, [VMEM] * 3 + [HBM] * 7, [((roots.shape[1] * leaves,...  4.77 us
    ppermute x5, waiting for transfers between devices, body(): mate = lax.ppermute(stack, AXES, mates)  3.56 us
    ppermute x5, starting transfers between devices, body(): far = lax.ppermute(stack, AXES, others)  3.2 us
  transfers between devices with their start and end apart: 10, of which 8 were waited for; matrix products, arithmetic and copies ran while one was open for 0% of the time, Pallas kernels for 7%

profile of v7, /device:TPU:1, one launch (start us, length us, event | category | flops | bytes accessed | tf_op | source)
XLA Modules:
  0.0 73.6 jit_solution(16867834458358519389)
XLA Ops:
  0.6 1.4 %shard_map.113 = (f32[8,256]{1,0:T(8,128)S(1)}, bf16[8,512]{1,0:T(8,128)(2,1)S(1)}, f32[8,2048]{1,0:T(8,128)S(1)}, bf16[8,64,256]{2,1,0:T(8,128)(2,1)S(1)}, bf16[8,64,128]{2,1,0:T(8,128)(2,1)S(1)}) custom-call(f32[8,2048]{1,0:T(8,128)} %basis.1, bf16[8,64,256]{2,1,0:T(8,128)(2,1)} %leaf_basis.1, bf16[8,64,128]{2,1,0:T(8,128)(2,1)} %transfer.1), custom_call_target="tpu_custom_call" | custom-call | tf_op jit(solution)/shard_map/pallas_call | solution.py:320
  2.0 3.1 %collective-permute-start.1 = (bf16[8,512]{1,0:T(8,128)(2,1)S(1)}, bf16[8,512]{1,0:T(8,128)(2,1)S(1)}, u32[]{:S(2)}, u32[]{:S(2)}) collective-permute-start(bf16[8,512]{1,0:T(8,128)(2,1)S(1)} %get-tuple-element.50.own), channel_id=1, source_target_pairs={{0,255},{1,2},{2,1},{3,4},{4,3},{5,6},{6,5},{7,8},{8,7},{9,10},{10... | collective-permute-start | bytes 24584 | tf_op jit(solution)/shard_map/ppermute | solution.py:326
  5.1 8.4 %collective-permute-start = (bf16[8,512]{1,0:T(8,128)(2,1)S(1)}, bf16[8,512]{1,0:T(8,128)(2,1)S(1)}, u32[]{:S(2)}, u32[]{:S(2)}) collective-permute-start(bf16[8,512]{1,0:T(8,128)(2,1)S(1)} %get-tuple-element.50.own), channel_id=1, source_target_pairs={{0,1},{1,0},{2,3},{3,2},{4,5},{5,4},{6,7},{7,6},{8,9},{9,8},{10,11... | collective-permute-start | bytes 24584 | tf_op jit(solution)/shard_map/ppermute | solution.py:327
  13.5 4.8 %shard_map.114 = (f32[40,256]{1,0:T(8,128)S(1)}, bf16[256,512]{1,0:T(8,128)(2,1)S(1)}, bf16[128,512]{1,0:T(8,128)(2,1)S(1)}, bf16[8,6,256,256]{3,2,1,0:T(8,128)(...) custom-call(f32[8,256]{1,0:T(8,128)S(1)} %get-tuple-element.46._.pro, ...), custom_call_target="tpu_custom_call" | custom-call | tf_op jit(solution)/shard_map/pallas_call | solution.py:330
  18.3 0.0 collective-permute-done.1.far
  18.3 0.0 collective-permute-done.mate
  18.4 1.6 %shard_map.116 = (f32[8,256]{1,0:T(8,128)S(1)}, bf16[8,512]{1,0:T(8,128)(2,1)S(1)}, f32[8,256]{1,0:T(8,128)S(1)}) custom-call(f32[40,256]{1,0:T(8,128)S(1)} %get-tuple-element.49.scales, f32[8,256]{1,0:T(8,128)S(1)} %get-tuple-element.46._.product.partial, f32[8,256]{1,0:T(8,128)S(1)} %get-tuple-element.46._.product.partial, ...), custom_call_target="tpu_custom_call" | custom-call | tf_op jit(solution)/shard_map/pallas_call | solution.py:356
  19.9 0.0 collective-permute-start.2
  19.9 0.1 collective-permute-start.3
  20.0 1.1 %collective-permute-done.2.mate = bf16[8,512]{1,0:T(8,128)(2,1)S(1)} collective-permute-done((bf16[8,512]{1,0:T(8,128)(2,1)S(1)}, bf16[8,512]{1,0:T(8,128)(2,1)S(1)}, u32[]{:S(2)}, u32[]{:S(2)}) %collective-permute-start.2) | collective-permute-done | bytes 8224 | tf_op jit(solution)/shard_map/ppermute | solution.py:361
  21.1 2.0 %collective-permute-done.3.far = bf16[8,512]{1,0:T(8,128)(2,1)S(1)} collective-permute-done((bf16[8,512]{1,0:T(8,128)(2,1)S(1)}, bf16[8,512]{1,0:T(8,128)(2,1)S(1)}, u32[]{:S(2)}, u32[]{:S(2)}) %collective-permute-start.3) | collective-permute-done | bytes 8224 | tf_op jit(solution)/shard_map/ppermute | solution.py:360
  23.1 1.5 %shard_map.118 = (f32[8,256]{1,0:T(8,128)S(1)}, bf16[8,512]{1,0:T(8,128)(2,1)S(1)}, f32[8,256]{1,0:T(8,128)S(1)}) custom-call(f32[40,256]{1,0:T(8,128)S(1)} %get-tuple-element.49.scales, f32[8,256]{1,0:T(8,128)S(1)} %get-tuple-element.64.product, f32[8,256]{1,0:T(8,128)S(1)} %get-tuple-element.65.partial, bf16[8,512]{1,0:T(8,128)(2,1)S(1)} %get-tuple-element.66.own, ...), custom_call_target="tpu_custom_call" | custom-call | tf_op jit(solution)/shard_map/pallas_call | solution.py:356
  24.6 4.3 %collective-permute-start.4 = (bf16[8,512]{1,0:T(8,128)(2,1)S(1)}, bf16[8,512]{1,0:T(8,128)(2,1)S(1)}, u32[]{:S(2)}, u32[]{:S(2)}) collective-permute-start(bf16[8,512]{1,0:T(8,128)(2,1)S(1)} %get-tuple-element.72.own), channel_id=1, source_target_pairs={{0,1},{1,0},{2,3},{3,2},{4,5},{5,4},{6,7},{7,6},{8,9},{9,8},{10,11... | collective-permute-start | bytes 24584 | tf_op jit(solution)/shard_map/ppermute | solution.py:361
  28.9 0.0 collective-permute-start.5
  28.9 0.8 %collective-permute-done.4.mate = bf16[8,512]{1,0:T(8,128)(2,1)S(1)} collective-permute-done((bf16[8,512]{1,0:T(8,128)(2,1)S(1)}, bf16[8,512]{1,0:T(8,128)(2,1)S(1)}, u32[]{:S(2)}, u32[]{:S(2)}) %collective-permute-start.4) | collective-permute-done | bytes 8224 | tf_op jit(solution)/shard_map/ppermute | solution.py:361
  29.8 2.2 %collective-permute-done.5.far = bf16[8,512]{1,0:T(8,128)(2,1)S(1)} collective-permute-done((bf16[8,512]{1,0:T(8,128)(2,1)S(1)}, bf16[8,512]{1,0:T(8,128)(2,1)S(1)}, u32[]{:S(2)}, u32[]{:S(2)}) %collective-permute-start.5) | collective-permute-done | bytes 8224 | tf_op jit(solution)/shard_map/ppermute | solution.py:360
  32.0 1.5 %shard_map.120 = (f32[8,256]{1,0:T(8,128)S(1)}, bf16[8,512]{1,0:T(8,128)(2,1)S(1)}, f32[8,256]{1,0:T(8,128)S(1)}) custom-call(f32[40,256]{1,0:T(8,128)S(1)} %get-tuple-element.49.scales, f32[8,256]{1,0:T(8,128)S(1)} %get-tuple-element.70.product, f32[8,256]{1,0:T(8,128)S(1)} %get-tuple-element.71.partial, bf16[8,512]{1,0:T(8,128)(2,1)S(1)} %get-tuple-element.72.own, ...), custom_call_target="tpu_custom_call" | custom-call | tf_op jit(solution)/shard_map/pallas_call | solution.py:356
  33.5 3.9 %collective-permute-start.6 = (bf16[8,512]{1,0:T(8,128)(2,1)S(1)}, bf16[8,512]{1,0:T(8,128)(2,1)S(1)}, u32[]{:S(2)}, u32[]{:S(2)}) collective-permute-start(bf16[8,512]{1,0:T(8,128)(2,1)S(1)} %get-tuple-element.78.own), channel_id=1, source_target_pairs={{0,1},{1,0},{2,3},{3,2},{4,5},{5,4},{6,7},{7,6},{8,9},{9,8},{10,11... | collective-permute-start | bytes 24584 | tf_op jit(solution)/shard_map/ppermute | solution.py:361
  37.4 0.0 collective-permute-start.7
  37.5 0.8 %collective-permute-done.6.mate = bf16[8,512]{1,0:T(8,128)(2,1)S(1)} collective-permute-done((bf16[8,512]{1,0:T(8,128)(2,1)S(1)}, bf16[8,512]{1,0:T(8,128)(2,1)S(1)}, u32[]{:S(2)}, u32[]{:S(2)}) %collective-permute-start.6) | collective-permute-done | bytes 8224 | tf_op jit(solution)/shard_map/ppermute | solution.py:361
  38.3 2.2 %collective-permute-done.7.far = bf16[8,512]{1,0:T(8,128)(2,1)S(1)} collective-permute-done((bf16[8,512]{1,0:T(8,128)(2,1)S(1)}, bf16[8,512]{1,0:T(8,128)(2,1)S(1)}, u32[]{:S(2)}, u32[]{:S(2)}) %collective-permute-start.7) | collective-permute-done | bytes 8224 | tf_op jit(solution)/shard_map/ppermute | solution.py:360
  40.5 1.5 %shard_map.122 = (f32[8,256]{1,0:T(8,128)S(1)}, bf16[8,512]{1,0:T(8,128)(2,1)S(1)}) custom-call(f32[40,256]{1,0:T(8,128)S(1)} %get-tuple-element.49.scales, f32[8,256]{1,0:T(8,128)S(1)} %get-tuple-element.76.product, f32[8,256]{1,0:T(8,128)S(1)} %get-tuple-element.77.partial, bf16[8,512]{1,0:T(8,128)(2,1)S(1)} %get-tuple-element.78.own, ...), custom_call_target="tpu_custom_call" | custom-call | tf_op jit(solution)/shard_map/pallas_call | solution.py:356
  42.1 3.9 %collective-permute-start.8 = (bf16[8,512]{1,0:T(8,128)(2,1)S(1)}, bf16[8,512]{1,0:T(8,128)(2,1)S(1)}, u32[]{:S(2)}, u32[]{:S(2)}) collective-permute-start(bf16[8,512]{1,0:T(8,128)(2,1)S(1)} %get-tuple-element.82.own), channel_id=1, source_target_pairs={{0,1},{1,0},{2,3},{3,2},{4,5},{5,4},{6,7},{7,6},{8,9},{9,8},{10,11... | collective-permute-start | bytes 24584 | tf_op jit(solution)/shard_map/ppermute | solution.py:361
  46.0 0.0 collective-permute-start.9
  46.0 0.8 %collective-permute-done.8.mate = bf16[8,512]{1,0:T(8,128)(2,1)S(1)} collective-permute-done((bf16[8,512]{1,0:T(8,128)(2,1)S(1)}, bf16[8,512]{1,0:T(8,128)(2,1)S(1)}, u32[]{:S(2)}, u32[]{:S(2)}) %collective-permute-start.8) | collective-permute-done | bytes 8224 | tf_op jit(solution)/shard_map/ppermute | solution.py:361
  46.8 0.1 shard_map.123
  46.9 2.1 %collective-permute-done.9.far = bf16[8,512]{1,0:T(8,128)(2,1)S(1)} collective-permute-done((bf16[8,512]{1,0:T(8,128)(2,1)S(1)}, bf16[8,512]{1,0:T(8,128)(2,1)S(1)}, u32[]{:S(2)}, u32[]{:S(2)}) %collective-permute-start.9) | collective-permute-done | bytes 8224 | tf_op jit(solution)/shard_map/ppermute | solution.py:360
  49.0 1.4 %shard_map.124 = (f32[8,256]{1,0:T(8,128)S(1)}, f32[256,128]{1,0:T(8,128)S(1)}) custom-call(f32[8,256]{1,0:T(8,128)S(1)} %get-tuple-element.81.field, bf16[8,512]{1,0:T(8,128)(2,1)S(1)} %get-tuple-element.82.own, bf16[8,512]{1,0:T(8,128)(2,1)S(1)} %collective-permute-done.8.mate, bf16[8,512]{1,0:T(8,128)(2,1)S(1)} %collective-permute-done.9.far, ...), custom_call_target="tpu_custom_call" | custom-call | tf_op jit(solution)/shard_map/pallas_call | solution.py:364
  50.4 22.3 %all_to_all.5 = f32[256,1,128]{2,1,0:T(1,128)S(1)} all-to-all(f32[256,1,128]{2,1,0:T(1,128)S(1)} %bitcast.7), channel_id=1, replica_groups=mesh['grp'=4,'leaf'=64] {'grp','leaf'}, dimensions={0} | all-to-all | bytes 262144 | tf_op jit(solution)/shard_map/all_to_all | solution.py:367
  72.8 0.8 %shard_map.125 = (f32[16,128]{1,0:T(8,128)}, f32[9]{0:T(128)}) custom-call(f32[256,128]{1,0:T(8,128)S(1)} %bitcast.6, f32[8,256]{1,0:T(8,128)S(1)} %get-tuple-element.87.image, f32[8,2048]{1,0:T(8,128)S(1)} %get-tuple-element.83.rest_10_.basis), custom_call_target="tpu_custom_call" | custom-call | tf_op jit(solution)/shard_map/pallas_call | solution.py:369
  (4 shorter events, 0.0 us)
Async XLA Ops:
  2.0 16.3 %collective-permute-start.1 = (bf16[8,512]{1,0:T(8,128)(2,1)S(1)}, bf16[8,512]{1,0:T(8,128)(2,1)S(1)}, u32[]{:S(2)}, u32[]{:S(2)}) collective-permute-start(bf16[8,512]{1,0:T(8,128)(2,1)S(1)} %get-tuple-element.50.own), channel_id=1, source_target_pairs={{0,255},{1,2},{2,1},{3,4},{4,3},{5,6},{6,5},{7,8},{8,7},{9,10},{10... | collective-permute-start | bytes 24584 | tf_op jit(solution)/shard_map/ppermute | solution.py:326
  5.1 13.2 %collective-permute-start = (bf16[8,512]{1,0:T(8,128)(2,1)S(1)}, bf16[8,512]{1,0:T(8,128)(2,1)S(1)}, u32[]{:S(2)}, u32[]{:S(2)}) collective-permute-start(bf16[8,512]{1,0:T(8,128)(2,1)S(1)} %get-tuple-element.50.own), channel_id=1, source_target_pairs={{0,1},{1,0},{2,3},{3,2},{4,5},{5,4},{6,7},{7,6},{8,9},{9,8},{10,11... | collective-permute-start | bytes 24584 | tf_op jit(solution)/shard_map/ppermute | solution.py:327
  19.9 1.2 %collective-permute-start.2 = (bf16[8,512]{1,0:T(8,128)(2,1)S(1)}, bf16[8,512]{1,0:T(8,128)(2,1)S(1)}, u32[]{:S(2)}, u32[]{:S(2)}) collective-permute-start(bf16[8,512]{1,0:T(8,128)(2,1)S(1)} %get-tuple-element.66.own), channel_id=1, source_target_pairs={{0,1},{1,0},{2,3},{3,2},{4,5},{5,4},{6,7},{7,6},{8,9},{9,8},{10,11... | collective-permute-start | bytes 24584 | tf_op jit(solution)/shard_map/ppermute | solution.py:361
  19.9 3.2 %collective-permute-start.3 = (bf16[8,512]{1,0:T(8,128)(2,1)S(1)}, bf16[8,512]{1,0:T(8,128)(2,1)S(1)}, u32[]{:S(2)}, u32[]{:S(2)}) collective-permute-start(bf16[8,512]{1,0:T(8,128)(2,1)S(1)} %get-tuple-element.66.own), channel_id=1, source_target_pairs={{0,255},{1,2},{2,1},{3,4},{4,3},{5,6},{6,5},{7,8},{8,7},{9,10},{10... | collective-permute-start | bytes 24584 | tf_op jit(solution)/shard_map/ppermute | solution.py:360
  24.6 5.2 %collective-permute-start.4 = (bf16[8,512]{1,0:T(8,128)(2,1)S(1)}, bf16[8,512]{1,0:T(8,128)(2,1)S(1)}, u32[]{:S(2)}, u32[]{:S(2)}) collective-permute-start(bf16[8,512]{1,0:T(8,128)(2,1)S(1)} %get-tuple-element.72.own), channel_id=1, source_target_pairs={{0,1},{1,0},{2,3},{3,2},{4,5},{5,4},{6,7},{7,6},{8,9},{9,8},{10,11... | collective-permute-start | bytes 24584 | tf_op jit(solution)/shard_map/ppermute | solution.py:361
  28.9 3.1 %collective-permute-start.5 = (bf16[8,512]{1,0:T(8,128)(2,1)S(1)}, bf16[8,512]{1,0:T(8,128)(2,1)S(1)}, u32[]{:S(2)}, u32[]{:S(2)}) collective-permute-start(bf16[8,512]{1,0:T(8,128)(2,1)S(1)} %get-tuple-element.72.own), channel_id=1, source_target_pairs={{0,255},{1,2},{2,1},{3,4},{4,3},{5,6},{6,5},{7,8},{8,7},{9,10},{10... | collective-permute-start | bytes 24584 | tf_op jit(solution)/shard_map/ppermute | solution.py:360
  33.5 4.7 %collective-permute-start.6 = (bf16[8,512]{1,0:T(8,128)(2,1)S(1)}, bf16[8,512]{1,0:T(8,128)(2,1)S(1)}, u32[]{:S(2)}, u32[]{:S(2)}) collective-permute-start(bf16[8,512]{1,0:T(8,128)(2,1)S(1)} %get-tuple-element.78.own), channel_id=1, source_target_pairs={{0,1},{1,0},{2,3},{3,2},{4,5},{5,4},{6,7},{7,6},{8,9},{9,8},{10,11... | collective-permute-start | bytes 24584 | tf_op jit(solution)/shard_map/ppermute | solution.py:361
  37.4 3.1 %collective-permute-start.7 = (bf16[8,512]{1,0:T(8,128)(2,1)S(1)}, bf16[8,512]{1,0:T(8,128)(2,1)S(1)}, u32[]{:S(2)}, u32[]{:S(2)}) collective-permute-start(bf16[8,512]{1,0:T(8,128)(2,1)S(1)} %get-tuple-element.78.own), channel_id=1, source_target_pairs={{0,255},{1,2},{2,1},{3,4},{4,3},{5,6},{6,5},{7,8},{8,7},{9,10},{10... | collective-permute-start | bytes 24584 | tf_op jit(solution)/shard_map/ppermute | solution.py:360
  42.1 4.7 %collective-permute-start.8 = (bf16[8,512]{1,0:T(8,128)(2,1)S(1)}, bf16[8,512]{1,0:T(8,128)(2,1)S(1)}, u32[]{:S(2)}, u32[]{:S(2)}) collective-permute-start(bf16[8,512]{1,0:T(8,128)(2,1)S(1)} %get-tuple-element.82.own), channel_id=1, source_target_pairs={{0,1},{1,0},{2,3},{3,2},{4,5},{5,4},{6,7},{7,6},{8,9},{9,8},{10,11... | collective-permute-start | bytes 24584 | tf_op jit(solution)/shard_map/ppermute | solution.py:361
  46.0 3.1 %collective-permute-start.9 = (bf16[8,512]{1,0:T(8,128)(2,1)S(1)}, bf16[8,512]{1,0:T(8,128)(2,1)S(1)}, u32[]{:S(2)}, u32[]{:S(2)}) collective-permute-start(bf16[8,512]{1,0:T(8,128)(2,1)S(1)} %get-tuple-element.82.own), channel_id=1, source_target_pairs={{0,255},{1,2},{2,1},{3,4},{4,3},{5,6},{6,5},{7,8},{8,7},{9,10},{10... | collective-permute-start | bytes 24584 | tf_op jit(solution)/shard_map/ppermute | solution.py:360

commit v8 on v7

--- a/solution.py
+++ b/solution.py
@@ -72,15 +72,14 @@
         return total
 
     quarter = leaves // 4
-    total = near_rows(0.5 * field, range(quarter))
+    total = near_rows(0.5 * field, range(2 * quarter))
     tops = diagonal(dot(parents, top[...]), PRANK)
     local = diagonal(dot(coeffs, coupling[...]), RANK)
-    total = near_rows(total, range(quarter, 2 * quarter))
+    total = near_rows(total, range(2 * quarter, 3 * quarter))
     tops = sum(tops[:, at : at + PRANK] for at in range(0, tops.shape[1], PRANK)).astype(BF16)
     local += diagonal(dot(tops, transfer_turned[...]), 2 * RANK)
-    total = near_rows(total, range(2 * quarter, 3 * quarter))
+    total = near_rows(total, range(3 * quarter, leaves))
     rows = dot(diagonal(flat(local), RANK).astype(BF16), leaf_basis)
-    total = near_rows(total, range(3 * quarter, leaves))
     return total + rows
 
 
@@ -128,7 +127,7 @@
     basis_turned[...] = stacked(leaf_basis).T
     transfer_turned[...] = stacked(transfer).T
     unit = identity(PANEL)
-    for copy in copies[:4]:
+    for copy in copies[:6]:
         copy.wait()
     for k in range(roots.shape[1]):
         scales[k * leaves : (k + 1) * leaves, :] = jnp.broadcast_to(
@@ -148,19 +147,18 @@
             if rows < leaves:
                 hot = jnp.concatenate([hot, jnp.zeros((leaves - rows, SOURCES), F32)], axis=0)
             pick[k * leaves : (k + 1) * leaves, :] = hot.astype(BF16)
-    copies[4].wait()
     for k in range(coupling.shape[1]):
         rows = jnp.concatenate([coupling_in[i, k] for i in range(leaves)], axis=0)
         coupling_out[k * RANK : (k + 1) * RANK, :] = rows.T
-    copies[5].wait()
     for p in range(top.shape[0]):
         for k in range(top.shape[1]):
             rows, lanes = slice(k * PRANK, (k + 1) * PRANK), slice(p * PRANK, (p + 1) * PRANK)
             top_out[rows, lanes] = top_in[p, k].T
     for i in range(leaves):
-        copies[6 + i].wait()
+        for copy in copies[6 + i : 8 + i] if i % 2 == 0 else ():
+            copy.wait()
         for k in range(near.shape[1]):
-            near_out[i, k] = dot_nt(unit, near_in[i, k]).astype(BF16) if k % 2 else near_in[i, k].T
+            near_out[i, k] = dot_nt(unit, near_in[i, k]).astype(BF16) if k % 3 == 1 else near_in[i, k].T
 
 
 def at_an_end():

time: 73.7 us -> 73.9 us (level)
  blocking collectives: 22.3 us -> 23.3 us
  Pallas kernels: 14.6 us -> 13.8 us
    all_to_all x1, blocking collectives: 22.3 us -> 23.3 us  [body(): sums = lax.all_to_all(sums.reshape(devices, 1, 128), AXES, 0, 0, tiled=True)]
    pallas_call x1, Pallas kernels: 4.77 us -> 3.93 us  [body(): call(prepare_kernel, [VMEM] * 3 + [HBM] * 7, [((roots.shape[1] * leaves,...]
  transfers between devices with their start and end apart: 10 -> 10, of which waited for: 8 -> 8; matrix products, arithmetic and copies ran while one was open for 0% -> 0% of each run, Pallas kernels for 7% -> 5%
where the time goes in v8:
time: 73.9 us; the launch traced here: 73.8 us
  starting transfers between devices  23.8 us (32%)
  blocking collectives  23.3 us (32%)
  Pallas kernels  13.8 us (19%)
  waiting for transfers between devices  12.2 us (17%)
    all_to_all x1, blocking collectives, body(): sums = lax.all_to_all(sums.reshape(devices, 1, 128), AXES, 0, 0, tiled=True)  23.3 us
    ppermute x5, starting transfers between devices, body(): mate = lax.ppermute(stack, AXES, mates)  20.6 us
    ppermute x5, waiting for transfers between devices, body(): far = lax.ppermute(stack, AXES, others)  8.61 us
    pallas_call x4, Pallas kernels, body(): call(functools.partial(step_late, step, last), [VMEM] * (16 + len(outs)),...  6.14 us
    pallas_call x1, Pallas kernels, body(): call(prepare_kernel, [VMEM] * 3 + [HBM] * 7, [((roots.shape[1] * leaves,...  3.93 us
    ppermute x5, waiting for transfers between devices, body(): mate = lax.ppermute(stack, AXES, mates)  3.56 us
    ppermute x5, starting transfers between devices, body(): far = lax.ppermute(stack, AXES, others)  3.21 us
  transfers between devices with their start and end apart: 10, of which 8 were waited for; matrix products, arithmetic and copies ran while one was open for 0% of the time, Pallas kernels for 5%

profile of v8, /device:TPU:1, one launch (start us, length us, event | category | flops | bytes accessed | tf_op | source)
XLA Modules:
  0.0 73.8 jit_solution(17942082716834618024)
XLA Ops:
  0.6 1.4 %shard_map.113 = (f32[8,256]{1,0:T(8,128)S(1)}, bf16[8,512]{1,0:T(8,128)(2,1)S(1)}, f32[8,2048]{1,0:T(8,128)S(1)}, bf16[8,64,256]{2,1,0:T(8,128)(2,1)S(1)}, bf16[8,64,128]{2,1,0:T(8,128)(2,1)S(1)}) custom-call(f32[8,2048]{1,0:T(8,128)} %basis.1, bf16[8,64,256]{2,1,0:T(8,128)(2,1)} %leaf_basis.1, bf16[8,64,128]{2,1,0:T(8,128)(2,1)} %transfer.1), custom_call_target="tpu_custom_call" | custom-call | tf_op jit(solution)/shard_map/pallas_call | solution.py:318
  2.0 3.1 %collective-permute-start.1 = (bf16[8,512]{1,0:T(8,128)(2,1)S(1)}, bf16[8,512]{1,0:T(8,128)(2,1)S(1)}, u32[]{:S(2)}, u32[]{:S(2)}) collective-permute-start(bf16[8,512]{1,0:T(8,128)(2,1)S(1)} %get-tuple-element.50.own), channel_id=1, source_target_pairs={{0,255},{1,2},{2,1},{3,4},{4,3},{5,6},{6,5},{7,8},{8,7},{9,10},{10... | collective-permute-start | bytes 24584 | tf_op jit(solution)/shard_map/ppermute | solution.py:324
  5.1 8.4 %collective-permute-start = (bf16[8,512]{1,0:T(8,128)(2,1)S(1)}, bf16[8,512]{1,0:T(8,128)(2,1)S(1)}, u32[]{:S(2)}, u32[]{:S(2)}) collective-permute-start(bf16[8,512]{1,0:T(8,128)(2,1)S(1)} %get-tuple-element.50.own), channel_id=1, source_target_pairs={{0,1},{1,0},{2,3},{3,2},{4,5},{5,4},{6,7},{7,6},{8,9},{9,8},{10,11... | collective-permute-start | bytes 24584 | tf_op jit(solution)/shard_map/ppermute | solution.py:325
  13.5 3.9 %shard_map.114 = (f32[40,256]{1,0:T(8,128)S(1)}, bf16[256,512]{1,0:T(8,128)(2,1)S(1)}, bf16[128,512]{1,0:T(8,128)(2,1)S(1)}, bf16[8,6,256,256]{3,2,1,0:T(8,128)(...) custom-call(f32[8,256]{1,0:T(8,128)S(1)} %get-tuple-element.46._.pro, ...), custom_call_target="tpu_custom_call" | custom-call | tf_op jit(solution)/shard_map/pallas_call | solution.py:328
  17.5 0.0 collective-permute-done.1.far
  17.5 0.0 collective-permute-done.mate
  17.5 1.6 %shard_map.116 = (f32[8,256]{1,0:T(8,128)S(1)}, bf16[8,512]{1,0:T(8,128)(2,1)S(1)}, f32[8,256]{1,0:T(8,128)S(1)}) custom-call(f32[40,256]{1,0:T(8,128)S(1)} %get-tuple-element.49.scales, f32[8,256]{1,0:T(8,128)S(1)} %get-tuple-element.46._.product.partial, f32[8,256]{1,0:T(8,128)S(1)} %get-tuple-element.46._.product.partial, ...), custom_call_target="tpu_custom_call" | custom-call | tf_op jit(solution)/shard_map/pallas_call | solution.py:354
  19.1 0.0 collective-permute-start.2
  19.1 0.1 collective-permute-start.3
  19.2 1.1 %collective-permute-done.2.mate = bf16[8,512]{1,0:T(8,128)(2,1)S(1)} collective-permute-done((bf16[8,512]{1,0:T(8,128)(2,1)S(1)}, bf16[8,512]{1,0:T(8,128)(2,1)S(1)}, u32[]{:S(2)}, u32[]{:S(2)}) %collective-permute-start.2) | collective-permute-done | bytes 8224 | tf_op jit(solution)/shard_map/ppermute | solution.py:359
  20.2 2.0 %collective-permute-done.3.far = bf16[8,512]{1,0:T(8,128)(2,1)S(1)} collective-permute-done((bf16[8,512]{1,0:T(8,128)(2,1)S(1)}, bf16[8,512]{1,0:T(8,128)(2,1)S(1)}, u32[]{:S(2)}, u32[]{:S(2)}) %collective-permute-start.3) | collective-permute-done | bytes 8224 | tf_op jit(solution)/shard_map/ppermute | solution.py:358
  22.2 1.5 %shard_map.118 = (f32[8,256]{1,0:T(8,128)S(1)}, bf16[8,512]{1,0:T(8,128)(2,1)S(1)}, f32[8,256]{1,0:T(8,128)S(1)}) custom-call(f32[40,256]{1,0:T(8,128)S(1)} %get-tuple-element.49.scales, f32[8,256]{1,0:T(8,128)S(1)} %get-tuple-element.64.product, f32[8,256]{1,0:T(8,128)S(1)} %get-tuple-element.65.partial, bf16[8,512]{1,0:T(8,128)(2,1)S(1)} %get-tuple-element.66.own, ...), custom_call_target="tpu_custom_call" | custom-call | tf_op jit(solution)/shard_map/pallas_call | solution.py:354
  23.8 4.3 %collective-permute-start.4 = (bf16[8,512]{1,0:T(8,128)(2,1)S(1)}, bf16[8,512]{1,0:T(8,128)(2,1)S(1)}, u32[]{:S(2)}, u32[]{:S(2)}) collective-permute-start(bf16[8,512]{1,0:T(8,128)(2,1)S(1)} %get-tuple-element.72.own), channel_id=1, source_target_pairs={{0,1},{1,0},{2,3},{3,2},{4,5},{5,4},{6,7},{7,6},{8,9},{9,8},{10,11... | collective-permute-start | bytes 24584 | tf_op jit(solution)/shard_map/ppermute | solution.py:359
  28.1 0.0 collective-permute-start.5
  28.1 0.8 %collective-permute-done.4.mate = bf16[8,512]{1,0:T(8,128)(2,1)S(1)} collective-permute-done((bf16[8,512]{1,0:T(8,128)(2,1)S(1)}, bf16[8,512]{1,0:T(8,128)(2,1)S(1)}, u32[]{:S(2)}, u32[]{:S(2)}) %collective-permute-start.4) | collective-permute-done | bytes 8224 | tf_op jit(solution)/shard_map/ppermute | solution.py:359
  28.9 2.2 %collective-permute-done.5.far = bf16[8,512]{1,0:T(8,128)(2,1)S(1)} collective-permute-done((bf16[8,512]{1,0:T(8,128)(2,1)S(1)}, bf16[8,512]{1,0:T(8,128)(2,1)S(1)}, u32[]{:S(2)}, u32[]{:S(2)}) %collective-permute-start.5) | collective-permute-done | bytes 8224 | tf_op jit(solution)/shard_map/ppermute | solution.py:358
  31.2 1.5 %shard_map.120 = (f32[8,256]{1,0:T(8,128)S(1)}, bf16[8,512]{1,0:T(8,128)(2,1)S(1)}, f32[8,256]{1,0:T(8,128)S(1)}) custom-call(f32[40,256]{1,0:T(8,128)S(1)} %get-tuple-element.49.scales, f32[8,256]{1,0:T(8,128)S(1)} %get-tuple-element.70.product, f32[8,256]{1,0:T(8,128)S(1)} %get-tuple-element.71.partial, bf16[8,512]{1,0:T(8,128)(2,1)S(1)} %get-tuple-element.72.own, ...), custom_call_target="tpu_custom_call" | custom-call | tf_op jit(solution)/shard_map/pallas_call | solution.py:354
  32.7 3.9 %collective-permute-start.6 = (bf16[8,512]{1,0:T(8,128)(2,1)S(1)}, bf16[8,512]{1,0:T(8,128)(2,1)S(1)}, u32[]{:S(2)}, u32[]{:S(2)}) collective-permute-start(bf16[8,512]{1,0:T(8,128)(2,1)S(1)} %get-tuple-element.78.own), channel_id=1, source_target_pairs={{0,1},{1,0},{2,3},{3,2},{4,5},{5,4},{6,7},{7,6},{8,9},{9,8},{10,11... | collective-permute-start | bytes 24584 | tf_op jit(solution)/shard_map/ppermute | solution.py:359
  36.6 0.0 collective-permute-start.7
  36.6 0.8 %collective-permute-done.6.mate = bf16[8,512]{1,0:T(8,128)(2,1)S(1)} collective-permute-done((bf16[8,512]{1,0:T(8,128)(2,1)S(1)}, bf16[8,512]{1,0:T(8,128)(2,1)S(1)}, u32[]{:S(2)}, u32[]{:S(2)}) %collective-permute-start.6) | collective-permute-done | bytes 8224 | tf_op jit(solution)/shard_map/ppermute | solution.py:359
  37.4 2.2 %collective-permute-done.7.far = bf16[8,512]{1,0:T(8,128)(2,1)S(1)} collective-permute-done((bf16[8,512]{1,0:T(8,128)(2,1)S(1)}, bf16[8,512]{1,0:T(8,128)(2,1)S(1)}, u32[]{:S(2)}, u32[]{:S(2)}) %collective-permute-start.7) | collective-permute-done | bytes 8224 | tf_op jit(solution)/shard_map/ppermute | solution.py:358
  39.7 1.5 %shard_map.122 = (f32[8,256]{1,0:T(8,128)S(1)}, bf16[8,512]{1,0:T(8,128)(2,1)S(1)}) custom-call(f32[40,256]{1,0:T(8,128)S(1)} %get-tuple-element.49.scales, f32[8,256]{1,0:T(8,128)S(1)} %get-tuple-element.76.product, f32[8,256]{1,0:T(8,128)S(1)} %get-tuple-element.77.partial, bf16[8,512]{1,0:T(8,128)(2,1)S(1)} %get-tuple-element.78.own, ...), custom_call_target="tpu_custom_call" | custom-call | tf_op jit(solution)/shard_map/pallas_call | solution.py:354
  41.2 3.9 %collective-permute-start.8 = (bf16[8,512]{1,0:T(8,128)(2,1)S(1)}, bf16[8,512]{1,0:T(8,128)(2,1)S(1)}, u32[]{:S(2)}, u32[]{:S(2)}) collective-permute-start(bf16[8,512]{1,0:T(8,128)(2,1)S(1)} %get-tuple-element.82.own), channel_id=1, source_target_pairs={{0,1},{1,0},{2,3},{3,2},{4,5},{5,4},{6,7},{7,6},{8,9},{9,8},{10,11... | collective-permute-start | bytes 24584 | tf_op jit(solution)/shard_map/ppermute | solution.py:359
  45.1 0.0 collective-permute-start.9
  45.1 0.8 %collective-permute-done.8.mate = bf16[8,512]{1,0:T(8,128)(2,1)S(1)} collective-permute-done((bf16[8,512]{1,0:T(8,128)(2,1)S(1)}, bf16[8,512]{1,0:T(8,128)(2,1)S(1)}, u32[]{:S(2)}, u32[]{:S(2)}) %collective-permute-start.8) | collective-permute-done | bytes 8224 | tf_op jit(solution)/shard_map/ppermute | solution.py:359
  46.0 0.1 shard_map.123
  46.1 2.1 %collective-permute-done.9.far = bf16[8,512]{1,0:T(8,128)(2,1)S(1)} collective-permute-done((bf16[8,512]{1,0:T(8,128)(2,1)S(1)}, bf16[8,512]{1,0:T(8,128)(2,1)S(1)}, u32[]{:S(2)}, u32[]{:S(2)}) %collective-permute-start.9) | collective-permute-done | bytes 8224 | tf_op jit(solution)/shard_map/ppermute | solution.py:358
  48.2 1.4 %shard_map.124 = (f32[8,256]{1,0:T(8,128)S(1)}, f32[256,128]{1,0:T(8,128)S(1)}) custom-call(f32[8,256]{1,0:T(8,128)S(1)} %get-tuple-element.81.field, bf16[8,512]{1,0:T(8,128)(2,1)S(1)} %get-tuple-element.82.own, bf16[8,512]{1,0:T(8,128)(2,1)S(1)} %collective-permute-done.8.mate, bf16[8,512]{1,0:T(8,128)(2,1)S(1)} %collective-permute-done.9.far, ...), custom_call_target="tpu_custom_call" | custom-call | tf_op jit(solution)/shard_map/pallas_call | solution.py:362
  49.6 23.3 %all_to_all.5 = f32[256,1,128]{2,1,0:T(1,128)S(1)} all-to-all(f32[256,1,128]{2,1,0:T(1,128)S(1)} %bitcast.7), channel_id=1, replica_groups=mesh['grp'=4,'leaf'=64] {'grp','leaf'}, dimensions={0} | all-to-all | bytes 262144 | tf_op jit(solution)/shard_map/all_to_all | solution.py:365
  72.9 0.8 %shard_map.125 = (f32[16,128]{1,0:T(8,128)}, f32[9]{0:T(128)}) custom-call(f32[256,128]{1,0:T(8,128)S(1)} %bitcast.6, f32[8,256]{1,0:T(8,128)S(1)} %get-tuple-element.87.image, f32[8,2048]{1,0:T(8,128)S(1)} %get-tuple-element.83.rest_10_.basis), custom_call_target="tpu_custom_call" | custom-call | tf_op jit(solution)/shard_map/pallas_call | solution.py:367
  (4 shorter events, 0.0 us)
Async XLA Ops:
  2.0 15.5 %collective-permute-start.1 = (bf16[8,512]{1,0:T(8,128)(2,1)S(1)}, bf16[8,512]{1,0:T(8,128)(2,1)S(1)}, u32[]{:S(2)}, u32[]{:S(2)}) collective-permute-start(bf16[8,512]{1,0:T(8,128)(2,1)S(1)} %get-tuple-element.50.own), channel_id=1, source_target_pairs={{0,255},{1,2},{2,1},{3,4},{4,3},{5,6},{6,5},{7,8},{8,7},{9,10},{10... | collective-permute-start | bytes 24584 | tf_op jit(solution)/shard_map/ppermute | solution.py:324
  5.1 12.4 %collective-permute-start = (bf16[8,512]{1,0:T(8,128)(2,1)S(1)}, bf16[8,512]{1,0:T(8,128)(2,1)S(1)}, u32[]{:S(2)}, u32[]{:S(2)}) collective-permute-start(bf16[8,512]{1,0:T(8,128)(2,1)S(1)} %get-tuple-element.50.own), channel_id=1, source_target_pairs={{0,1},{1,0},{2,3},{3,2},{4,5},{5,4},{6,7},{7,6},{8,9},{9,8},{10,11... | collective-permute-start | bytes 24584 | tf_op jit(solution)/shard_map/ppermute | solution.py:325
  19.1 1.2 %collective-permute-start.2 = (bf16[8,512]{1,0:T(8,128)(2,1)S(1)}, bf16[8,512]{1,0:T(8,128)(2,1)S(1)}, u32[]{:S(2)}, u32[]{:S(2)}) collective-permute-start(bf16[8,512]{1,0:T(8,128)(2,1)S(1)} %get-tuple-element.66.own), channel_id=1, source_target_pairs={{0,1},{1,0},{2,3},{3,2},{4,5},{5,4},{6,7},{7,6},{8,9},{9,8},{10,11... | collective-permute-start | bytes 24584 | tf_op jit(solution)/shard_map/ppermute | solution.py:359
  19.1 3.2 %collective-permute-start.3 = (bf16[8,512]{1,0:T(8,128)(2,1)S(1)}, bf16[8,512]{1,0:T(8,128)(2,1)S(1)}, u32[]{:S(2)}, u32[]{:S(2)}) collective-permute-start(bf16[8,512]{1,0:T(8,128)(2,1)S(1)} %get-tuple-element.66.own), channel_id=1, source_target_pairs={{0,255},{1,2},{2,1},{3,4},{4,3},{5,6},{6,5},{7,8},{8,7},{9,10},{10... | collective-permute-start | bytes 24584 | tf_op jit(solution)/shard_map/ppermute | solution.py:358
  23.8 5.2 %collective-permute-start.4 = (bf16[8,512]{1,0:T(8,128)(2,1)S(1)}, bf16[8,512]{1,0:T(8,128)(2,1)S(1)}, u32[]{:S(2)}, u32[]{:S(2)}) collective-permute-start(bf16[8,512]{1,0:T(8,128)(2,1)S(1)} %get-tuple-element.72.own), channel_id=1, source_target_pairs={{0,1},{1,0},{2,3},{3,2},{4,5},{5,4},{6,7},{7,6},{8,9},{9,8},{10,11... | collective-permute-start | bytes 24584 | tf_op jit(solution)/shard_map/ppermute | solution.py:359
  28.1 3.1 %collective-permute-start.5 = (bf16[8,512]{1,0:T(8,128)(2,1)S(1)}, bf16[8,512]{1,0:T(8,128)(2,1)S(1)}, u32[]{:S(2)}, u32[]{:S(2)}) collective-permute-start(bf16[8,512]{1,0:T(8,128)(2,1)S(1)} %get-tuple-element.72.own), channel_id=1, source_target_pairs={{0,255},{1,2},{2,1},{3,4},{4,3},{5,6},{6,5},{7,8},{8,7},{9,10},{10... | collective-permute-start | bytes 24584 | tf_op jit(solution)/shard_map/ppermute | solution.py:358
  32.7 4.7 %collective-permute-start.6 = (bf16[8,512]{1,0:T(8,128)(2,1)S(1)}, bf16[8,512]{1,0:T(8,128)(2,1)S(1)}, u32[]{:S(2)}, u32[]{:S(2)}) collective-permute-start(bf16[8,512]{1,0:T(8,128)(2,1)S(1)} %get-tuple-element.78.own), channel_id=1, source_target_pairs={{0,1},{1,0},{2,3},{3,2},{4,5},{5,4},{6,7},{7,6},{8,9},{9,8},{10,11... | collective-permute-start | bytes 24584 | tf_op jit(solution)/shard_map/ppermute | solution.py:359
  36.6 3.1 %collective-permute-start.7 = (bf16[8,512]{1,0:T(8,128)(2,1)S(1)}, bf16[8,512]{1,0:T(8,128)(2,1)S(1)}, u32[]{:S(2)}, u32[]{:S(2)}) collective-permute-start(bf16[8,512]{1,0:T(8,128)(2,1)S(1)} %get-tuple-element.78.own), channel_id=1, source_target_pairs={{0,255},{1,2},{2,1},{3,4},{4,3},{5,6},{6,5},{7,8},{8,7},{9,10},{10... | collective-permute-start | bytes 24584 | tf_op jit(solution)/shard_map/ppermute | solution.py:358
  41.2 4.7 %collective-permute-start.8 = (bf16[8,512]{1,0:T(8,128)(2,1)S(1)}, bf16[8,512]{1,0:T(8,128)(2,1)S(1)}, u32[]{:S(2)}, u32[]{:S(2)}) collective-permute-start(bf16[8,512]{1,0:T(8,128)(2,1)S(1)} %get-tuple-element.82.own), channel_id=1, source_target_pairs={{0,1},{1,0},{2,3},{3,2},{4,5},{5,4},{6,7},{7,6},{8,9},{9,8},{10,11... | collective-permute-start | bytes 24584 | tf_op jit(solution)/shard_map/ppermute | solution.py:359
  45.1 3.1 %collective-permute-start.9 = (bf16[8,512]{1,0:T(8,128)(2,1)S(1)}, bf16[8,512]{1,0:T(8,128)(2,1)S(1)}, u32[]{:S(2)}, u32[]{:S(2)}) collective-permute-start(bf16[8,512]{1,0:T(8,128)(2,1)S(1)} %get-tuple-element.82.own), channel_id=1, source_target_pairs={{0,255},{1,2},{2,1},{3,4},{4,3},{5,6},{6,5},{7,8},{8,7},{9,10},{10... | collective-permute-start | bytes 24584 | tf_op jit(solution)/shard_map/ppermute | solution.py:358

commit v9 on v8

--- a/solution.py
+++ b/solution.py
@@ -72,14 +72,15 @@
         return total
 
     quarter = leaves // 4
-    total = near_rows(0.5 * field, range(2 * quarter))
+    total = near_rows(0.5 * field, range(quarter))
     tops = diagonal(dot(parents, top[...]), PRANK)
     local = diagonal(dot(coeffs, coupling[...]), RANK)
-    total = near_rows(total, range(2 * quarter, 3 * quarter))
+    total = near_rows(total, range(quarter, 2 * quarter))
     tops = sum(tops[:, at : at + PRANK] for at in range(0, tops.shape[1], PRANK)).astype(BF16)
     local += diagonal(dot(tops, transfer_turned[...]), 2 * RANK)
+    total = near_rows(total, range(2 * quarter, 3 * quarter))
+    rows = dot(diagonal(flat(local), RANK).astype(BF16), leaf_basis)
     total = near_rows(total, range(3 * quarter, leaves))
-    rows = dot(diagonal(flat(local), RANK).astype(BF16), leaf_basis)
     return total + rows
 
 
@@ -96,11 +97,12 @@
     ]
     for copy in copies:
         copy.start()
-    for copy in copies:
-        copy.wait()
+    copies[0].wait()
     count = basis.shape[0]
     for i in range(product.shape[0]):
         product[i : i + 1, :] = basis_in[count - 1 : count, i * PANEL : (i + 1) * PANEL]
+    for copy in copies[1:]:
+        copy.wait()
     write_stack(product[...], stacked(leaf_basis_in), stacked(transfer_in), stack)
 
 

time: 73.9 us -> 73.9 us (level)
  no operation moved by 1% of the time
where the time goes in v9:
time: 73.9 us; the launch traced here: 73.8 us
  starting transfers between devices  23.8 us (32%)
  blocking collectives  23.3 us (32%)
  Pallas kernels  13.8 us (19%)
  waiting for transfers between devices  12.2 us (17%)
    all_to_all x1, blocking collectives, body(): sums = lax.all_to_all(sums.reshape(devices, 1, 128), AXES, 0, 0, tiled=True)  23.3 us
    ppermute x5, starting transfers between devices, body(): mate = lax.ppermute(stack, AXES, mates)  20.6 us
    ppermute x5, waiting for transfers between devices, body(): far = lax.ppermute(stack, AXES, others)  8.61 us
    pallas_call x4, Pallas kernels, body(): call(functools.partial(step_late, step, last), [VMEM] * (16 + len(outs)),...  6.14 us
    pallas_call x1, Pallas kernels, body(): call(prepare_kernel, [VMEM] * 3 + [HBM] * 7, [((roots.shape[1] * leaves,...  3.94 us
    ppermute x5, waiting for transfers between devices, body(): mate = lax.ppermute(stack, AXES, mates)  3.56 us
    ppermute x5, starting transfers between devices, body(): far = lax.ppermute(stack, AXES, others)  3.21 us
  transfers between devices with their start and end apart: 10, of which 8 were waited for; matrix products, arithmetic and copies ran while one was open for 0% of the time, Pallas kernels for 5%

profile of v9, /device:TPU:1, one launch (start us, length us, event | category | flops | bytes accessed | tf_op | source)
XLA Modules:
  0.0 73.8 jit_solution(125161996486059160)
XLA Ops:
  0.6 1.4 %shard_map.113 = (f32[8,256]{1,0:T(8,128)S(1)}, bf16[8,512]{1,0:T(8,128)(2,1)S(1)}, f32[8,2048]{1,0:T(8,128)S(1)}, bf16[8,64,256]{2,1,0:T(8,128)(2,1)S(1)}, bf16[8,64,128]{2,1,0:T(8,128)(2,1)S(1)}) custom-call(f32[8,2048]{1,0:T(8,128)} %basis.1, bf16[8,64,256]{2,1,0:T(8,128)(2,1)} %leaf_basis.1, bf16[8,64,128]{2,1,0:T(8,128)(2,1)} %transfer.1), custom_call_target="tpu_custom_call" | custom-call | tf_op jit(solution)/shard_map/pallas_call | solution.py:320
  2.0 3.1 %collective-permute-start.1 = (bf16[8,512]{1,0:T(8,128)(2,1)S(1)}, bf16[8,512]{1,0:T(8,128)(2,1)S(1)}, u32[]{:S(2)}, u32[]{:S(2)}) collective-permute-start(bf16[8,512]{1,0:T(8,128)(2,1)S(1)} %get-tuple-element.50.own), channel_id=1, source_target_pairs={{0,255},{1,2},{2,1},{3,4},{4,3},{5,6},{6,5},{7,8},{8,7},{9,10},{10... | collective-permute-start | bytes 24584 | tf_op jit(solution)/shard_map/ppermute | solution.py:326
  5.1 8.4 %collective-permute-start = (bf16[8,512]{1,0:T(8,128)(2,1)S(1)}, bf16[8,512]{1,0:T(8,128)(2,1)S(1)}, u32[]{:S(2)}, u32[]{:S(2)}) collective-permute-start(bf16[8,512]{1,0:T(8,128)(2,1)S(1)} %get-tuple-element.50.own), channel_id=1, source_target_pairs={{0,1},{1,0},{2,3},{3,2},{4,5},{5,4},{6,7},{7,6},{8,9},{9,8},{10,11... | collective-permute-start | bytes 24584 | tf_op jit(solution)/shard_map/ppermute | solution.py:327
  13.5 3.9 %shard_map.114 = (f32[40,256]{1,0:T(8,128)S(1)}, bf16[256,512]{1,0:T(8,128)(2,1)S(1)}, bf16[128,512]{1,0:T(8,128)(2,1)S(1)}, bf16[8,6,256,256]{3,2,1,0:T(8,128)(...) custom-call(f32[8,256]{1,0:T(8,128)S(1)} %get-tuple-element.46._.pro, ...), custom_call_target="tpu_custom_call" | custom-call | tf_op jit(solution)/shard_map/pallas_call | solution.py:330
  17.5 0.0 collective-permute-done.1.far
  17.5 0.0 collective-permute-done.mate
  17.5 1.6 %shard_map.116 = (f32[8,256]{1,0:T(8,128)S(1)}, bf16[8,512]{1,0:T(8,128)(2,1)S(1)}, f32[8,256]{1,0:T(8,128)S(1)}) custom-call(f32[40,256]{1,0:T(8,128)S(1)} %get-tuple-element.49.scales, f32[8,256]{1,0:T(8,128)S(1)} %get-tuple-element.46._.product.partial, f32[8,256]{1,0:T(8,128)S(1)} %get-tuple-element.46._.product.partial, ...), custom_call_target="tpu_custom_call" | custom-call | tf_op jit(solution)/shard_map/pallas_call | solution.py:356
  19.1 0.0 collective-permute-start.2
  19.1 0.1 collective-permute-start.3
  19.2 1.1 %collective-permute-done.2.mate = bf16[8,512]{1,0:T(8,128)(2,1)S(1)} collective-permute-done((bf16[8,512]{1,0:T(8,128)(2,1)S(1)}, bf16[8,512]{1,0:T(8,128)(2,1)S(1)}, u32[]{:S(2)}, u32[]{:S(2)}) %collective-permute-start.2) | collective-permute-done | bytes 8224 | tf_op jit(solution)/shard_map/ppermute | solution.py:361
  20.3 2.0 %collective-permute-done.3.far = bf16[8,512]{1,0:T(8,128)(2,1)S(1)} collective-permute-done((bf16[8,512]{1,0:T(8,128)(2,1)S(1)}, bf16[8,512]{1,0:T(8,128)(2,1)S(1)}, u32[]{:S(2)}, u32[]{:S(2)}) %collective-permute-start.3) | collective-permute-done | bytes 8224 | tf_op jit(solution)/shard_map/ppermute | solution.py:360
  22.2 1.5 %shard_map.118 = (f32[8,256]{1,0:T(8,128)S(1)}, bf16[8,512]{1,0:T(8,128)(2,1)S(1)}, f32[8,256]{1,0:T(8,128)S(1)}) custom-call(f32[40,256]{1,0:T(8,128)S(1)} %get-tuple-element.49.scales, f32[8,256]{1,0:T(8,128)S(1)} %get-tuple-element.64.product, f32[8,256]{1,0:T(8,128)S(1)} %get-tuple-element.65.partial, bf16[8,512]{1,0:T(8,128)(2,1)S(1)} %get-tuple-element.66.own, ...), custom_call_target="tpu_custom_call" | custom-call | tf_op jit(solution)/shard_map/pallas_call | solution.py:356
  23.8 4.3 %collective-permute-start.4 = (bf16[8,512]{1,0:T(8,128)(2,1)S(1)}, bf16[8,512]{1,0:T(8,128)(2,1)S(1)}, u32[]{:S(2)}, u32[]{:S(2)}) collective-permute-start(bf16[8,512]{1,0:T(8,128)(2,1)S(1)} %get-tuple-element.72.own), channel_id=1, source_target_pairs={{0,1},{1,0},{2,3},{3,2},{4,5},{5,4},{6,7},{7,6},{8,9},{9,8},{10,11... | collective-permute-start | bytes 24584 | tf_op jit(solution)/shard_map/ppermute | solution.py:361
  28.1 0.0 collective-permute-start.5
  28.1 0.8 %collective-permute-done.4.mate = bf16[8,512]{1,0:T(8,128)(2,1)S(1)} collective-permute-done((bf16[8,512]{1,0:T(8,128)(2,1)S(1)}, bf16[8,512]{1,0:T(8,128)(2,1)S(1)}, u32[]{:S(2)}, u32[]{:S(2)}) %collective-permute-start.4) | collective-permute-done | bytes 8224 | tf_op jit(solution)/shard_map/ppermute | solution.py:361
  28.9 2.2 %collective-permute-done.5.far = bf16[8,512]{1,0:T(8,128)(2,1)S(1)} collective-permute-done((bf16[8,512]{1,0:T(8,128)(2,1)S(1)}, bf16[8,512]{1,0:T(8,128)(2,1)S(1)}, u32[]{:S(2)}, u32[]{:S(2)}) %collective-permute-start.5) | collective-permute-done | bytes 8224 | tf_op jit(solution)/shard_map/ppermute | solution.py:360
  31.2 1.5 %shard_map.120 = (f32[8,256]{1,0:T(8,128)S(1)}, bf16[8,512]{1,0:T(8,128)(2,1)S(1)}, f32[8,256]{1,0:T(8,128)S(1)}) custom-call(f32[40,256]{1,0:T(8,128)S(1)} %get-tuple-element.49.scales, f32[8,256]{1,0:T(8,128)S(1)} %get-tuple-element.70.product, f32[8,256]{1,0:T(8,128)S(1)} %get-tuple-element.71.partial, bf16[8,512]{1,0:T(8,128)(2,1)S(1)} %get-tuple-element.72.own, ...), custom_call_target="tpu_custom_call" | custom-call | tf_op jit(solution)/shard_map/pallas_call | solution.py:356
  32.7 3.9 %collective-permute-start.6 = (bf16[8,512]{1,0:T(8,128)(2,1)S(1)}, bf16[8,512]{1,0:T(8,128)(2,1)S(1)}, u32[]{:S(2)}, u32[]{:S(2)}) collective-permute-start(bf16[8,512]{1,0:T(8,128)(2,1)S(1)} %get-tuple-element.78.own), channel_id=1, source_target_pairs={{0,1},{1,0},{2,3},{3,2},{4,5},{5,4},{6,7},{7,6},{8,9},{9,8},{10,11... | collective-permute-start | bytes 24584 | tf_op jit(solution)/shard_map/ppermute | solution.py:361
  36.6 0.0 collective-permute-start.7
  36.6 0.8 %collective-permute-done.6.mate = bf16[8,512]{1,0:T(8,128)(2,1)S(1)} collective-permute-done((bf16[8,512]{1,0:T(8,128)(2,1)S(1)}, bf16[8,512]{1,0:T(8,128)(2,1)S(1)}, u32[]{:S(2)}, u32[]{:S(2)}) %collective-permute-start.6) | collective-permute-done | bytes 8224 | tf_op jit(solution)/shard_map/ppermute | solution.py:361
  37.4 2.2 %collective-permute-done.7.far = bf16[8,512]{1,0:T(8,128)(2,1)S(1)} collective-permute-done((bf16[8,512]{1,0:T(8,128)(2,1)S(1)}, bf16[8,512]{1,0:T(8,128)(2,1)S(1)}, u32[]{:S(2)}, u32[]{:S(2)}) %collective-permute-start.7) | collective-permute-done | bytes 8224 | tf_op jit(solution)/shard_map/ppermute | solution.py:360
  39.7 1.5 %shard_map.122 = (f32[8,256]{1,0:T(8,128)S(1)}, bf16[8,512]{1,0:T(8,128)(2,1)S(1)}) custom-call(f32[40,256]{1,0:T(8,128)S(1)} %get-tuple-element.49.scales, f32[8,256]{1,0:T(8,128)S(1)} %get-tuple-element.76.product, f32[8,256]{1,0:T(8,128)S(1)} %get-tuple-element.77.partial, bf16[8,512]{1,0:T(8,128)(2,1)S(1)} %get-tuple-element.78.own, ...), custom_call_target="tpu_custom_call" | custom-call | tf_op jit(solution)/shard_map/pallas_call | solution.py:356
  41.2 3.9 %collective-permute-start.8 = (bf16[8,512]{1,0:T(8,128)(2,1)S(1)}, bf16[8,512]{1,0:T(8,128)(2,1)S(1)}, u32[]{:S(2)}, u32[]{:S(2)}) collective-permute-start(bf16[8,512]{1,0:T(8,128)(2,1)S(1)} %get-tuple-element.82.own), channel_id=1, source_target_pairs={{0,1},{1,0},{2,3},{3,2},{4,5},{5,4},{6,7},{7,6},{8,9},{9,8},{10,11... | collective-permute-start | bytes 24584 | tf_op jit(solution)/shard_map/ppermute | solution.py:361
  45.1 0.0 collective-permute-start.9
  45.1 0.8 %collective-permute-done.8.mate = bf16[8,512]{1,0:T(8,128)(2,1)S(1)} collective-permute-done((bf16[8,512]{1,0:T(8,128)(2,1)S(1)}, bf16[8,512]{1,0:T(8,128)(2,1)S(1)}, u32[]{:S(2)}, u32[]{:S(2)}) %collective-permute-start.8) | collective-permute-done | bytes 8224 | tf_op jit(solution)/shard_map/ppermute | solution.py:361
  46.0 0.1 shard_map.123
  46.1 2.1 %collective-permute-done.9.far = bf16[8,512]{1,0:T(8,128)(2,1)S(1)} collective-permute-done((bf16[8,512]{1,0:T(8,128)(2,1)S(1)}, bf16[8,512]{1,0:T(8,128)(2,1)S(1)}, u32[]{:S(2)}, u32[]{:S(2)}) %collective-permute-start.9) | collective-permute-done | bytes 8224 | tf_op jit(solution)/shard_map/ppermute | solution.py:360
  48.2 1.4 %shard_map.124 = (f32[8,256]{1,0:T(8,128)S(1)}, f32[256,128]{1,0:T(8,128)S(1)}) custom-call(f32[8,256]{1,0:T(8,128)S(1)} %get-tuple-element.81.field, bf16[8,512]{1,0:T(8,128)(2,1)S(1)} %get-tuple-element.82.own, bf16[8,512]{1,0:T(8,128)(2,1)S(1)} %collective-permute-done.8.mate, bf16[8,512]{1,0:T(8,128)(2,1)S(1)} %collective-permute-done.9.far, ...), custom_call_target="tpu_custom_call" | custom-call | tf_op jit(solution)/shard_map/pallas_call | solution.py:364
  49.6 23.3 %all_to_all.5 = f32[256,1,128]{2,1,0:T(1,128)S(1)} all-to-all(f32[256,1,128]{2,1,0:T(1,128)S(1)} %bitcast.7), channel_id=1, replica_groups=mesh['grp'=4,'leaf'=64] {'grp','leaf'}, dimensions={0} | all-to-all | bytes 262144 | tf_op jit(solution)/shard_map/all_to_all | solution.py:367
  72.9 0.8 %shard_map.125 = (f32[16,128]{1,0:T(8,128)}, f32[9]{0:T(128)}) custom-call(f32[256,128]{1,0:T(8,128)S(1)} %bitcast.6, f32[8,256]{1,0:T(8,128)S(1)} %get-tuple-element.87.image, f32[8,2048]{1,0:T(8,128)S(1)} %get-tuple-element.83.rest_10_.basis), custom_call_target="tpu_custom_call" | custom-call | tf_op jit(solution)/shard_map/pallas_call | solution.py:369
  (4 shorter events, 0.0 us)
Async XLA Ops:
  2.0 15.5 %collective-permute-start.1 = (bf16[8,512]{1,0:T(8,128)(2,1)S(1)}, bf16[8,512]{1,0:T(8,128)(2,1)S(1)}, u32[]{:S(2)}, u32[]{:S(2)}) collective-permute-start(bf16[8,512]{1,0:T(8,128)(2,1)S(1)} %get-tuple-element.50.own), channel_id=1, source_target_pairs={{0,255},{1,2},{2,1},{3,4},{4,3},{5,6},{6,5},{7,8},{8,7},{9,10},{10... | collective-permute-start | bytes 24584 | tf_op jit(solution)/shard_map/ppermute | solution.py:326
  5.1 12.4 %collective-permute-start = (bf16[8,512]{1,0:T(8,128)(2,1)S(1)}, bf16[8,512]{1,0:T(8,128)(2,1)S(1)}, u32[]{:S(2)}, u32[]{:S(2)}) collective-permute-start(bf16[8,512]{1,0:T(8,128)(2,1)S(1)} %get-tuple-element.50.own), channel_id=1, source_target_pairs={{0,1},{1,0},{2,3},{3,2},{4,5},{5,4},{6,7},{7,6},{8,9},{9,8},{10,11... | collective-permute-start | bytes 24584 | tf_op jit(solution)/shard_map/ppermute | solution.py:327
  19.1 1.2 %collective-permute-start.2 = (bf16[8,512]{1,0:T(8,128)(2,1)S(1)}, bf16[8,512]{1,0:T(8,128)(2,1)S(1)}, u32[]{:S(2)}, u32[]{:S(2)}) collective-permute-start(bf16[8,512]{1,0:T(8,128)(2,1)S(1)} %get-tuple-element.66.own), channel_id=1, source_target_pairs={{0,1},{1,0},{2,3},{3,2},{4,5},{5,4},{6,7},{7,6},{8,9},{9,8},{10,11... | collective-permute-start | bytes 24584 | tf_op jit(solution)/shard_map/ppermute | solution.py:361
  19.1 3.2 %collective-permute-start.3 = (bf16[8,512]{1,0:T(8,128)(2,1)S(1)}, bf16[8,512]{1,0:T(8,128)(2,1)S(1)}, u32[]{:S(2)}, u32[]{:S(2)}) collective-permute-start(bf16[8,512]{1,0:T(8,128)(2,1)S(1)} %get-tuple-element.66.own), channel_id=1, source_target_pairs={{0,255},{1,2},{2,1},{3,4},{4,3},{5,6},{6,5},{7,8},{8,7},{9,10},{10... | collective-permute-start | bytes 24584 | tf_op jit(solution)/shard_map/ppermute | solution.py:360
  23.8 5.2 %collective-permute-start.4 = (bf16[8,512]{1,0:T(8,128)(2,1)S(1)}, bf16[8,512]{1,0:T(8,128)(2,1)S(1)}, u32[]{:S(2)}, u32[]{:S(2)}) collective-permute-start(bf16[8,512]{1,0:T(8,128)(2,1)S(1)} %get-tuple-element.72.own), channel_id=1, source_target_pairs={{0,1},{1,0},{2,3},{3,2},{4,5},{5,4},{6,7},{7,6},{8,9},{9,8},{10,11... | collective-permute-start | bytes 24584 | tf_op jit(solution)/shard_map/ppermute | solution.py:361
  28.1 3.1 %collective-permute-start.5 = (bf16[8,512]{1,0:T(8,128)(2,1)S(1)}, bf16[8,512]{1,0:T(8,128)(2,1)S(1)}, u32[]{:S(2)}, u32[]{:S(2)}) collective-permute-start(bf16[8,512]{1,0:T(8,128)(2,1)S(1)} %get-tuple-element.72.own), channel_id=1, source_target_pairs={{0,255},{1,2},{2,1},{3,4},{4,3},{5,6},{6,5},{7,8},{8,7},{9,10},{10... | collective-permute-start | bytes 24584 | tf_op jit(solution)/shard_map/ppermute | solution.py:360
  32.7 4.7 %collective-permute-start.6 = (bf16[8,512]{1,0:T(8,128)(2,1)S(1)}, bf16[8,512]{1,0:T(8,128)(2,1)S(1)}, u32[]{:S(2)}, u32[]{:S(2)}) collective-permute-start(bf16[8,512]{1,0:T(8,128)(2,1)S(1)} %get-tuple-element.78.own), channel_id=1, source_target_pairs={{0,1},{1,0},{2,3},{3,2},{4,5},{5,4},{6,7},{7,6},{8,9},{9,8},{10,11... | collective-permute-start | bytes 24584 | tf_op jit(solution)/shard_map/ppermute | solution.py:361
  36.6 3.1 %collective-permute-start.7 = (bf16[8,512]{1,0:T(8,128)(2,1)S(1)}, bf16[8,512]{1,0:T(8,128)(2,1)S(1)}, u32[]{:S(2)}, u32[]{:S(2)}) collective-permute-start(bf16[8,512]{1,0:T(8,128)(2,1)S(1)} %get-tuple-element.78.own), channel_id=1, source_target_pairs={{0,255},{1,2},{2,1},{3,4},{4,3},{5,6},{6,5},{7,8},{8,7},{9,10},{10... | collective-permute-start | bytes 24584 | tf_op jit(solution)/shard_map/ppermute | solution.py:360
  41.2 4.7 %collective-permute-start.8 = (bf16[8,512]{1,0:T(8,128)(2,1)S(1)}, bf16[8,512]{1,0:T(8,128)(2,1)S(1)}, u32[]{:S(2)}, u32[]{:S(2)}) collective-permute-start(bf16[8,512]{1,0:T(8,128)(2,1)S(1)} %get-tuple-element.82.own), channel_id=1, source_target_pairs={{0,1},{1,0},{2,3},{3,2},{4,5},{5,4},{6,7},{7,6},{8,9},{9,8},{10,11... | collective-permute-start | bytes 24584 | tf_op jit(solution)/shard_map/ppermute | solution.py:361
  45.1 3.1 %collective-permute-start.9 = (bf16[8,512]{1,0:T(8,128)(2,1)S(1)}, bf16[8,512]{1,0:T(8,128)(2,1)S(1)}, u32[]{:S(2)}, u32[]{:S(2)}) collective-permute-start(bf16[8,512]{1,0:T(8,128)(2,1)S(1)} %get-tuple-element.82.own), channel_id=1, source_target_pairs={{0,255},{1,2},{2,1},{3,4},{4,3},{5,6},{6,5},{7,8},{8,7},{9,10},{10... | collective-permute-start | bytes 24584 | tf_op jit(solution)/shard_map/ppermute | solution.py:360
